TPU v7x, 256 devices: a whole 4x4x8 slice. The times are simulated.
256 devices in a mesh: tm: 64 (over z, y, core), space: 4 (over x).
Axes of the slice: x: 4, y: 4, z: 8, core: 2. Of those that a mesh axis runs over, the one named last changes fastest.
Arguments:
- coarse_points: float32 [128, 2, 128, 1024], P('tm', None, 'space'), may hold values from -4 to 4
- coarse_decay: float32 [128, 2, 128, 1024], P('tm', None, 'space'), may hold values from 0 to 1, as said below
- diffusion: float32 [128, 1024], P('space'), may hold values from 0.2 to 0.22
- forcing: float32 [2, 128, 1024], P(None, 'space'), may hold values from -5 to 5
Outputs:
- updated: float32 [128, 2, 128, 1024], P('tm', None, 'space')
Inputs may be any that keep to these rules, and one draw needn't show every extreme that they name: `coarse_decay`: 0 to 1 for every interval, cell and component.
All inputs are finite; a program needn't handle non-finite values.
Results may differ from a plain program's by a relative error of at most 0.00002.
Values sent between devices are 32-bit elements; how exact they have to be, the bound alone decides.
A program may use at most 128 MiB of HBM per device.

v0:
```python
import jax
import jax.numpy as jnp
from jax import lax
from jax.sharding import PartitionSpec as P

M = 16


def with_halo(block, sides, width):
    for axis, dim in sides:
        count = lax.axis_size(axis)
        forward = [(i, i + 1) for i in range(count - 1)]
        backward = [(target, source) for source, target in forward]
        low = lax.ppermute(
            lax.slice_in_dim(block, block.shape[dim] - width, None, axis=dim), axis, forward
        )
        high = lax.ppermute(lax.slice_in_dim(block, 0, width, axis=dim), axis, backward)
        block = jnp.concatenate([low, block, high], axis=dim)
    return block


def in_one_piece(arrays, axis, split_dim, concat_dim, along):
    both = jnp.concatenate(arrays, axis=along)
    filled, at, finished = (
        lax.all_to_all(both, axis, split_axis=split_dim, concat_axis=concat_dim, tiled=True),
        0,
        [],
    )
    for a in arrays:
        finished.append(lax.slice_in_dim(filled, at, at + a.shape[along], axis=along))
        at += a.shape[along]
    return tuple(finished)


def compose(earlier, later_pair):
    return (later_pair[0] * earlier[0], later_pair[0] * earlier[1] + later_pair[1])


def per_device(coarse_points, coarse_decay, diffusion, forcing):
    row_count = coarse_points.shape[2]
    slot_count = coarse_points.shape[0]
    row_number = lax.broadcasted_iota(jnp.int32, (1, 1, row_count, 1), 2)
    at_top = row_number == 0
    at_bottom = row_number == row_count - 1

    def one_step(counter, field_state):
        edges = jnp.concatenate([field_state[:, :, :1], field_state[:, :, -1:]], axis=2)
        rims = with_halo(edges, (("space", 2),), 1)
        next_row = jnp.where(at_bottom, rims[:, :, 3:4], jnp.roll(field_state, -1, axis=2))
        prev_row = jnp.where(at_top, rims[:, :, 0:1], jnp.roll(field_state, 1, axis=2))
        next_col = jnp.roll(field_state, -1, axis=3)
        prev_col = jnp.roll(field_state, 1, axis=3)
        speed_x = field_state[:, 0:1]
        speed_y = field_state[:, 1:2]
        return (
            field_state
            + diffusion * (next_row + prev_row + next_col + prev_col - 4.0 * field_state)
            - 0.05 * (speed_x * (next_row - prev_row) + speed_y * (next_col - prev_col))
            + 0.05 * forcing
        )

    fine_end = lax.fori_loop(0, M, one_step, coarse_points)
    shift_terms = fine_end - coarse_decay * coarse_points
    scale_terms = coarse_decay
    at_anchor = lax.axis_index("tm") == 0
    scale_terms = scale_terms.at[0].set(jnp.where(at_anchor, 0.0, scale_terms[0]))
    shift_terms = shift_terms.at[0].set(jnp.where(at_anchor, fine_end[0], shift_terms[0]))
    local_scale = scale_terms[0]
    local_shift = shift_terms[0]
    slot_index = 1
    local_shift = scale_terms[slot_index] * local_shift + shift_terms[slot_index]
    local_scale = scale_terms[slot_index] * local_scale
    every_scale, every_shift = in_one_piece((local_scale[None], local_shift[None]), "tm", 3, 0, 1)
    inclusive_scale, inclusive_shift = lax.associative_scan(
        compose, (every_scale, every_shift), axis=0
    )
    exclusive_scale = jnp.concatenate(
        [jnp.ones_like(inclusive_scale[:1]), inclusive_scale[:-1]], axis=0
    )
    exclusive_shift = jnp.concatenate(
        [jnp.zeros_like(inclusive_shift[:1]), inclusive_shift[:-1]], axis=0
    )
    back_scale, back_shift = (
        lax.all_to_all(exclusive_scale, "tm", split_axis=0, concat_axis=3, tiled=True),
        lax.all_to_all(exclusive_shift, "tm", split_axis=0, concat_axis=3, tiled=True),
    )
    prefix_shift = back_shift[0]
    current = prefix_shift
    results = []
    for slot_index in range(slot_count):
        current = scale_terms[slot_index] * current + shift_terms[slot_index]
        results.append(current)
    return jnp.stack(results, axis=0)


def solution(mesh):
    placed = (
        P("tm", None, "space", None),
        P("tm", None, "space", None),
        P("space", None),
        P(None, "space", None),
    )
    return jax.shard_map(
        per_device,
        mesh=mesh,
        in_specs=placed,
        out_specs=P("tm", None, "space", None),
        check_vma=False,
    )
```

profile of v0, /device:TPU:1, one launch (start us, length us, event | category | flops | bytes accessed | tf_op | source)
XLA Modules:
  0.0 342.3 jit_solution(7102397711355047756)
XLA Ops:
  1.0 179.7 %while.13 = (s32[]{:T(128)}, f32[2,2,32,1024]{3,2,1,0:T(8,128)S(1)}, f32[32,1024]{1,0:T(8,128)}, f32[2,32,1024]{2,1,0:T(8,128)}, s32[]{:T(128)}) while((s32[]{:T(128)}, f32[2,2,32,1024]{3,2,1,0:T(8,128)S(1)}, f32[32,1024]{1,0:T(8,128)}, f32[2,32,1024]{2,1,0:T(8,128)}, s32[]{:T(128)}) %tuple.58), condition=%wide.region_1.2_spmd.clone, body=%wide.region_0.1_spmd.clone.sunk | while | flops 2818114 | bytes 11108649 | solution.py:62
  1.7 4.5 %collective-permute-start = (f32[2,2,1,1024]{3,2,1,0:T(1,128)}, f32[2,2,1,1024]{3,2,1,0:T(1,128)}, u32[]{:S(2)}, u32[]{:S(2)}) collective-permute-start(f32[2,2,1,1024]{3,2,1,0:T(1,128)} %get-tuple-element.156), channel_id=1, source_target_pairs={{0,1},{1,2},{2,3},{4,5},{5,6},{6,7},{8,9},{9,10},{10,11},{12,13},{... | collective-permute-start | bytes 49160 | tf_op jit(solution)/shard_map/while/body/eval_jaxpr/ppermute | solution.py:14
  13.7 3.7 %collective-permute-start = (f32[2,2,1,1024]{3,2,1,0:T(1,128)}, f32[2,2,1,1024]{3,2,1,0:T(1,128)}, u32[]{:S(2)}, u32[]{:S(2)}) collective-permute-start(f32[2,2,1,1024]{3,2,1,0:T(1,128)} %get-tuple-element.156), channel_id=1, source_target_pairs={{0,1},{1,2},{2,3},{4,5},{5,6},{6,7},{8,9},{9,10},{10,11},{12,13},{... | collective-permute-start | bytes 49160 | tf_op jit(solution)/shard_map/while/body/eval_jaxpr/ppermute | solution.py:14
  24.8 3.7 %collective-permute-start = (f32[2,2,1,1024]{3,2,1,0:T(1,128)}, f32[2,2,1,1024]{3,2,1,0:T(1,128)}, u32[]{:S(2)}, u32[]{:S(2)}) collective-permute-start(f32[2,2,1,1024]{3,2,1,0:T(1,128)} %get-tuple-element.156), channel_id=1, source_target_pairs={{0,1},{1,2},{2,3},{4,5},{5,6},{6,7},{8,9},{9,10},{10,11},{12,13},{... | collective-permute-start | bytes 49160 | tf_op jit(solution)/shard_map/while/body/eval_jaxpr/ppermute | solution.py:14
  36.0 3.7 %collective-permute-start = (f32[2,2,1,1024]{3,2,1,0:T(1,128)}, f32[2,2,1,1024]{3,2,1,0:T(1,128)}, u32[]{:S(2)}, u32[]{:S(2)}) collective-permute-start(f32[2,2,1,1024]{3,2,1,0:T(1,128)} %get-tuple-element.156), channel_id=1, source_target_pairs={{0,1},{1,2},{2,3},{4,5},{5,6},{6,7},{8,9},{9,10},{10,11},{12,13},{... | collective-permute-start | bytes 49160 | tf_op jit(solution)/shard_map/while/body/eval_jaxpr/ppermute | solution.py:14
  47.2 3.7 %collective-permute-start = (f32[2,2,1,1024]{3,2,1,0:T(1,128)}, f32[2,2,1,1024]{3,2,1,0:T(1,128)}, u32[]{:S(2)}, u32[]{:S(2)}) collective-permute-start(f32[2,2,1,1024]{3,2,1,0:T(1,128)} %get-tuple-element.156), channel_id=1, source_target_pairs={{0,1},{1,2},{2,3},{4,5},{5,6},{6,7},{8,9},{9,10},{10,11},{12,13},{... | collective-permute-start | bytes 49160 | tf_op jit(solution)/shard_map/while/body/eval_jaxpr/ppermute | solution.py:14
  58.4 3.7 %collective-permute-start = (f32[2,2,1,1024]{3,2,1,0:T(1,128)}, f32[2,2,1,1024]{3,2,1,0:T(1,128)}, u32[]{:S(2)}, u32[]{:S(2)}) collective-permute-start(f32[2,2,1,1024]{3,2,1,0:T(1,128)} %get-tuple-element.156), channel_id=1, source_target_pairs={{0,1},{1,2},{2,3},{4,5},{5,6},{6,7},{8,9},{9,10},{10,11},{12,13},{... | collective-permute-start | bytes 49160 | tf_op jit(solution)/shard_map/while/body/eval_jaxpr/ppermute | solution.py:14
  69.6 3.7 %collective-permute-start = (f32[2,2,1,1024]{3,2,1,0:T(1,128)}, f32[2,2,1,1024]{3,2,1,0:T(1,128)}, u32[]{:S(2)}, u32[]{:S(2)}) collective-permute-start(f32[2,2,1,1024]{3,2,1,0:T(1,128)} %get-tuple-element.156), channel_id=1, source_target_pairs={{0,1},{1,2},{2,3},{4,5},{5,6},{6,7},{8,9},{9,10},{10,11},{12,13},{... | collective-permute-start | bytes 49160 | tf_op jit(solution)/shard_map/while/body/eval_jaxpr/ppermute | solution.py:14
  80.8 3.7 %collective-permute-start = (f32[2,2,1,1024]{3,2,1,0:T(1,128)}, f32[2,2,1,1024]{3,2,1,0:T(1,128)}, u32[]{:S(2)}, u32[]{:S(2)}) collective-permute-start(f32[2,2,1,1024]{3,2,1,0:T(1,128)} %get-tuple-element.156), channel_id=1, source_target_pairs={{0,1},{1,2},{2,3},{4,5},{5,6},{6,7},{8,9},{9,10},{10,11},{12,13},{... | collective-permute-start | bytes 49160 | tf_op jit(solution)/shard_map/while/body/eval_jaxpr/ppermute | solution.py:14
  92.0 3.7 %collective-permute-start = (f32[2,2,1,1024]{3,2,1,0:T(1,128)}, f32[2,2,1,1024]{3,2,1,0:T(1,128)}, u32[]{:S(2)}, u32[]{:S(2)}) collective-permute-start(f32[2,2,1,1024]{3,2,1,0:T(1,128)} %get-tuple-element.156), channel_id=1, source_target_pairs={{0,1},{1,2},{2,3},{4,5},{5,6},{6,7},{8,9},{9,10},{10,11},{12,13},{... | collective-permute-start | bytes 49160 | tf_op jit(solution)/shard_map/while/body/eval_jaxpr/ppermute | solution.py:14
  103.1 3.7 %collective-permute-start = (f32[2,2,1,1024]{3,2,1,0:T(1,128)}, f32[2,2,1,1024]{3,2,1,0:T(1,128)}, u32[]{:S(2)}, u32[]{:S(2)}) collective-permute-start(f32[2,2,1,1024]{3,2,1,0:T(1,128)} %get-tuple-element.156), channel_id=1, source_target_pairs={{0,1},{1,2},{2,3},{4,5},{5,6},{6,7},{8,9},{9,10},{10,11},{12,13},{... | collective-permute-start | bytes 49160 | tf_op jit(solution)/shard_map/while/body/eval_jaxpr/ppermute | solution.py:14
  114.3 3.7 %collective-permute-start = (f32[2,2,1,1024]{3,2,1,0:T(1,128)}, f32[2,2,1,1024]{3,2,1,0:T(1,128)}, u32[]{:S(2)}, u32[]{:S(2)}) collective-permute-start(f32[2,2,1,1024]{3,2,1,0:T(1,128)} %get-tuple-element.156), channel_id=1, source_target_pairs={{0,1},{1,2},{2,3},{4,5},{5,6},{6,7},{8,9},{9,10},{10,11},{12,13},{... | collective-permute-start | bytes 49160 | tf_op jit(solution)/shard_map/while/body/eval_jaxpr/ppermute | solution.py:14
  125.5 3.7 %collective-permute-start = (f32[2,2,1,1024]{3,2,1,0:T(1,128)}, f32[2,2,1,1024]{3,2,1,0:T(1,128)}, u32[]{:S(2)}, u32[]{:S(2)}) collective-permute-start(f32[2,2,1,1024]{3,2,1,0:T(1,128)} %get-tuple-element.156), channel_id=1, source_target_pairs={{0,1},{1,2},{2,3},{4,5},{5,6},{6,7},{8,9},{9,10},{10,11},{12,13},{... | collective-permute-start | bytes 49160 | tf_op jit(solution)/shard_map/while/body/eval_jaxpr/ppermute | solution.py:14
  136.7 3.7 %collective-permute-start = (f32[2,2,1,1024]{3,2,1,0:T(1,128)}, f32[2,2,1,1024]{3,2,1,0:T(1,128)}, u32[]{:S(2)}, u32[]{:S(2)}) collective-permute-start(f32[2,2,1,1024]{3,2,1,0:T(1,128)} %get-tuple-element.156), channel_id=1, source_target_pairs={{0,1},{1,2},{2,3},{4,5},{5,6},{6,7},{8,9},{9,10},{10,11},{12,13},{... | collective-permute-start | bytes 49160 | tf_op jit(solution)/shard_map/while/body/eval_jaxpr/ppermute | solution.py:14
  147.9 3.7 %collective-permute-start = (f32[2,2,1,1024]{3,2,1,0:T(1,128)}, f32[2,2,1,1024]{3,2,1,0:T(1,128)}, u32[]{:S(2)}, u32[]{:S(2)}) collective-permute-start(f32[2,2,1,1024]{3,2,1,0:T(1,128)} %get-tuple-element.156), channel_id=1, source_target_pairs={{0,1},{1,2},{2,3},{4,5},{5,6},{6,7},{8,9},{9,10},{10,11},{12,13},{... | collective-permute-start | bytes 49160 | tf_op jit(solution)/shard_map/while/body/eval_jaxpr/ppermute | solution.py:14
  159.1 3.7 %collective-permute-start = (f32[2,2,1,1024]{3,2,1,0:T(1,128)}, f32[2,2,1,1024]{3,2,1,0:T(1,128)}, u32[]{:S(2)}, u32[]{:S(2)}) collective-permute-start(f32[2,2,1,1024]{3,2,1,0:T(1,128)} %get-tuple-element.156), channel_id=1, source_target_pairs={{0,1},{1,2},{2,3},{4,5},{5,6},{6,7},{8,9},{9,10},{10,11},{12,13},{... | collective-permute-start | bytes 49160 | tf_op jit(solution)/shard_map/while/body/eval_jaxpr/ppermute | solution.py:14
  170.3 3.7 %collective-permute-start = (f32[2,2,1,1024]{3,2,1,0:T(1,128)}, f32[2,2,1,1024]{3,2,1,0:T(1,128)}, u32[]{:S(2)}, u32[]{:S(2)}) collective-permute-start(f32[2,2,1,1024]{3,2,1,0:T(1,128)} %get-tuple-element.156), channel_id=1, source_target_pairs={{0,1},{1,2},{2,3},{4,5},{5,6},{6,7},{8,9},{9,10},{10,11},{12,13},{... | collective-permute-start | bytes 49160 | tf_op jit(solution)/shard_map/while/body/eval_jaxpr/ppermute | solution.py:14
  187.8 40.3 %all_to_all.33 = f32[64,1,2048]{2,1,0:T(1,128)S(1)} all-to-all(f32[64,1,2048]{2,1,0:T(1,128)} %reshape.95), channel_id=1, replica_groups=mesh['tm'=64,'space'=4] {'tm'}, dimensions={0} | all-to-all | bytes 1048576 | tf_op jit(solution)/shard_map/all_to_all | solution.py:25
  250.8 4.7 %pad.47 = f32[8,2,32,16]{2,3,0,1:T(8,128)} pad(f32[4,2,32,16]{2,3,0,1:T(8,128)} %add.131, f32[]{:T(128)} %constant.67.clone.1), padding=1_0_1x0_0_0x0_0_0x0_0_0 | pad | bytes 49156 | tf_op jit(solution)/shard_map/pad | solution.py:74
  259.0 8.4 %pad.49 = f32[16,2,32,16]{2,3,0,1:T(8,128)} pad(f32[8,2,32,16]{2,3,0,1:T(8,128)} %add.133, f32[]{:T(128)} %constant.67.clone.1), padding=1_0_1x0_0_0x0_0_0x0_0_0 | pad | bytes 98308 | tf_op jit(solution)/shard_map/pad | solution.py:74
  270.4 10.3 %pad.50 = f32[32,2,32,16]{2,3,0,1:T(8,128)} pad(f32[16,2,32,16]{2,3,0,1:T(8,128)S(1)} %pad_maximum_fusion.5, f32[]{:T(128)} %constant.67.clone.1), padding=0_1_1x0_0_0x0_0_0x0_0_0 | pad | bytes 196612 | tf_op jit(solution)/shard_map/pad | solution.py:74
  280.7 15.1 %pad.51 = f32[32,2,32,16]{2,3,0,1:T(8,128)} pad(f32[16,2,32,16]{2,3,0,1:T(8,128)} %add.135, f32[]{:T(128)} %constant.67.clone.1), padding=1_0_1x0_0_0x0_0_0x0_0_0 | pad | bytes 196612 | tf_op jit(solution)/shard_map/pad | solution.py:74
  297.5 20.0 %pad.77 = f32[63,2,32,16]{2,3,0,1:T(8,128)} pad(f32[32,2,32,16]{2,3,0,1:T(8,128)S(1)} %pad_maximum_fusion.3, f32[]{:T(128)} %constant.67.clone.1), padding=0_0_1x0_0_0x0_0_0x0_0_0 | pad | bytes 389124 | tf_op jit(solution)/shard_map/slice | solution.py:81
  320.0 18.6 %all_to_all.34 = f32[64,1,1024]{2,1,0:T(1,128)S(1)} all-to-all(f32[64,1,1024]{2,1,0:T(1,128)S(1)} %reshape.97), channel_id=1, replica_groups=mesh['tm'=64,'space'=4] {'tm'}, dimensions={0} | all-to-all | bytes 524288 | tf_op jit(solution)/shard_map/all_to_all | solution.py:85
  (310 shorter events, 163.2 us)
Async XLA Ops:
  1.7 7.5 %collective-permute-start = (f32[2,2,1,1024]{3,2,1,0:T(1,128)}, f32[2,2,1,1024]{3,2,1,0:T(1,128)}, u32[]{:S(2)}, u32[]{:S(2)}) collective-permute-start(f32[2,2,1,1024]{3,2,1,0:T(1,128)} %get-tuple-element.156), channel_id=1, source_target_pairs={{0,1},{1,2},{2,3},{4,5},{5,6},{6,7},{8,9},{9,10},{10,11},{12,13},{... | collective-permute-start | bytes 49160 | tf_op jit(solution)/shard_map/while/body/eval_jaxpr/ppermute | solution.py:14
  6.2 4.6 %collective-permute-start.1 = (f32[2,2,1,1024]{3,2,1,0:T(1,128)S(1)}, f32[2,2,1,1024]{3,2,1,0:T(1,128)}, u32[]{:S(2)}, u32[]{:S(2)}) collective-permute-start(f32[2,2,1,1024]{3,2,1,0:T(1,128)S(1)} %get-tuple-element.157), channel_id=1, source_target_pairs={{1,0},{2,1},{3,2},{5,4},{6,5},{7,6},{9,8},{10,9},{11,10},{13,12},{... | collective-permute-start | bytes 49160 | tf_op jit(solution)/shard_map/while/body/eval_jaxpr/ppermute | solution.py:17
  13.7 6.7 %collective-permute-start = (f32[2,2,1,1024]{3,2,1,0:T(1,128)}, f32[2,2,1,1024]{3,2,1,0:T(1,128)}, u32[]{:S(2)}, u32[]{:S(2)}) collective-permute-start(f32[2,2,1,1024]{3,2,1,0:T(1,128)} %get-tuple-element.156), channel_id=1, source_target_pairs={{0,1},{1,2},{2,3},{4,5},{5,6},{6,7},{8,9},{9,10},{10,11},{12,13},{... | collective-permute-start | bytes 49160 | tf_op jit(solution)/shard_map/while/body/eval_jaxpr/ppermute | solution.py:14
  17.4 4.6 %collective-permute-start.1 = (f32[2,2,1,1024]{3,2,1,0:T(1,128)S(1)}, f32[2,2,1,1024]{3,2,1,0:T(1,128)}, u32[]{:S(2)}, u32[]{:S(2)}) collective-permute-start(f32[2,2,1,1024]{3,2,1,0:T(1,128)S(1)} %get-tuple-element.157), channel_id=1, source_target_pairs={{1,0},{2,1},{3,2},{5,4},{6,5},{7,6},{9,8},{10,9},{11,10},{13,12},{... | collective-permute-start | bytes 49160 | tf_op jit(solution)/shard_map/while/body/eval_jaxpr/ppermute | solution.py:17
  24.8 6.7 %collective-permute-start = (f32[2,2,1,1024]{3,2,1,0:T(1,128)}, f32[2,2,1,1024]{3,2,1,0:T(1,128)}, u32[]{:S(2)}, u32[]{:S(2)}) collective-permute-start(f32[2,2,1,1024]{3,2,1,0:T(1,128)} %get-tuple-element.156), channel_id=1, source_target_pairs={{0,1},{1,2},{2,3},{4,5},{5,6},{6,7},{8,9},{9,10},{10,11},{12,13},{... | collective-permute-start | bytes 49160 | tf_op jit(solution)/shard_map/while/body/eval_jaxpr/ppermute | solution.py:14
  36.0 6.7 %collective-permute-start = (f32[2,2,1,1024]{3,2,1,0:T(1,128)}, f32[2,2,1,1024]{3,2,1,0:T(1,128)}, u32[]{:S(2)}, u32[]{:S(2)}) collective-permute-start(f32[2,2,1,1024]{3,2,1,0:T(1,128)} %get-tuple-element.156), channel_id=1, source_target_pairs={{0,1},{1,2},{2,3},{4,5},{5,6},{6,7},{8,9},{9,10},{10,11},{12,13},{... | collective-permute-start | bytes 49160 | tf_op jit(solution)/shard_map/while/body/eval_jaxpr/ppermute | solution.py:14
  47.2 6.7 %collective-permute-start = (f32[2,2,1,1024]{3,2,1,0:T(1,128)}, f32[2,2,1,1024]{3,2,1,0:T(1,128)}, u32[]{:S(2)}, u32[]{:S(2)}) collective-permute-start(f32[2,2,1,1024]{3,2,1,0:T(1,128)} %get-tuple-element.156), channel_id=1, source_target_pairs={{0,1},{1,2},{2,3},{4,5},{5,6},{6,7},{8,9},{9,10},{10,11},{12,13},{... | collective-permute-start | bytes 49160 | tf_op jit(solution)/shard_map/while/body/eval_jaxpr/ppermute | solution.py:14
  58.4 6.7 %collective-permute-start = (f32[2,2,1,1024]{3,2,1,0:T(1,128)}, f32[2,2,1,1024]{3,2,1,0:T(1,128)}, u32[]{:S(2)}, u32[]{:S(2)}) collective-permute-start(f32[2,2,1,1024]{3,2,1,0:T(1,128)} %get-tuple-element.156), channel_id=1, source_target_pairs={{0,1},{1,2},{2,3},{4,5},{5,6},{6,7},{8,9},{9,10},{10,11},{12,13},{... | collective-permute-start | bytes 49160 | tf_op jit(solution)/shard_map/while/body/eval_jaxpr/ppermute | solution.py:14
  62.1 4.6 %collective-permute-start.1 = (f32[2,2,1,1024]{3,2,1,0:T(1,128)S(1)}, f32[2,2,1,1024]{3,2,1,0:T(1,128)}, u32[]{:S(2)}, u32[]{:S(2)}) collective-permute-start(f32[2,2,1,1024]{3,2,1,0:T(1,128)S(1)} %get-tuple-element.157), channel_id=1, source_target_pairs={{1,0},{2,1},{3,2},{5,4},{6,5},{7,6},{9,8},{10,9},{11,10},{13,12},{... | collective-permute-start | bytes 49160 | tf_op jit(solution)/shard_map/while/body/eval_jaxpr/ppermute | solution.py:17
  69.6 6.7 %collective-permute-start = (f32[2,2,1,1024]{3,2,1,0:T(1,128)}, f32[2,2,1,1024]{3,2,1,0:T(1,128)}, u32[]{:S(2)}, u32[]{:S(2)}) collective-permute-start(f32[2,2,1,1024]{3,2,1,0:T(1,128)} %get-tuple-element.156), channel_id=1, source_target_pairs={{0,1},{1,2},{2,3},{4,5},{5,6},{6,7},{8,9},{9,10},{10,11},{12,13},{... | collective-permute-start | bytes 49160 | tf_op jit(solution)/shard_map/while/body/eval_jaxpr/ppermute | solution.py:14
  73.3 4.6 %collective-permute-start.1 = (f32[2,2,1,1024]{3,2,1,0:T(1,128)S(1)}, f32[2,2,1,1024]{3,2,1,0:T(1,128)}, u32[]{:S(2)}, u32[]{:S(2)}) collective-permute-start(f32[2,2,1,1024]{3,2,1,0:T(1,128)S(1)} %get-tuple-element.157), channel_id=1, source_target_pairs={{1,0},{2,1},{3,2},{5,4},{6,5},{7,6},{9,8},{10,9},{11,10},{13,12},{... | collective-permute-start | bytes 49160 | tf_op jit(solution)/shard_map/while/body/eval_jaxpr/ppermute | solution.py:17
  80.8 6.7 %collective-permute-start = (f32[2,2,1,1024]{3,2,1,0:T(1,128)}, f32[2,2,1,1024]{3,2,1,0:T(1,128)}, u32[]{:S(2)}, u32[]{:S(2)}) collective-permute-start(f32[2,2,1,1024]{3,2,1,0:T(1,128)} %get-tuple-element.156), channel_id=1, source_target_pairs={{0,1},{1,2},{2,3},{4,5},{5,6},{6,7},{8,9},{9,10},{10,11},{12,13},{... | collective-permute-start | bytes 49160 | tf_op jit(solution)/shard_map/while/body/eval_jaxpr/ppermute | solution.py:14
  84.5 4.6 %collective-permute-start.1 = (f32[2,2,1,1024]{3,2,1,0:T(1,128)S(1)}, f32[2,2,1,1024]{3,2,1,0:T(1,128)}, u32[]{:S(2)}, u32[]{:S(2)}) collective-permute-start(f32[2,2,1,1024]{3,2,1,0:T(1,128)S(1)} %get-tuple-element.157), channel_id=1, source_target_pairs={{1,0},{2,1},{3,2},{5,4},{6,5},{7,6},{9,8},{10,9},{11,10},{13,12},{... | collective-permute-start | bytes 49160 | tf_op jit(solution)/shard_map/while/body/eval_jaxpr/ppermute | solution.py:17
  92.0 6.7 %collective-permute-start = (f32[2,2,1,1024]{3,2,1,0:T(1,128)}, f32[2,2,1,1024]{3,2,1,0:T(1,128)}, u32[]{:S(2)}, u32[]{:S(2)}) collective-permute-start(f32[2,2,1,1024]{3,2,1,0:T(1,128)} %get-tuple-element.156), channel_id=1, source_target_pairs={{0,1},{1,2},{2,3},{4,5},{5,6},{6,7},{8,9},{9,10},{10,11},{12,13},{... | collective-permute-start | bytes 49160 | tf_op jit(solution)/shard_map/while/body/eval_jaxpr/ppermute | solution.py:14
  103.1 6.7 %collective-permute-start = (f32[2,2,1,1024]{3,2,1,0:T(1,128)}, f32[2,2,1,1024]{3,2,1,0:T(1,128)}, u32[]{:S(2)}, u32[]{:S(2)}) collective-permute-start(f32[2,2,1,1024]{3,2,1,0:T(1,128)} %get-tuple-element.156), channel_id=1, source_target_pairs={{0,1},{1,2},{2,3},{4,5},{5,6},{6,7},{8,9},{9,10},{10,11},{12,13},{... | collective-permute-start | bytes 49160 | tf_op jit(solution)/shard_map/while/body/eval_jaxpr/ppermute | solution.py:14
  114.3 6.7 %collective-permute-start = (f32[2,2,1,1024]{3,2,1,0:T(1,128)}, f32[2,2,1,1024]{3,2,1,0:T(1,128)}, u32[]{:S(2)}, u32[]{:S(2)}) collective-permute-start(f32[2,2,1,1024]{3,2,1,0:T(1,128)} %get-tuple-element.156), channel_id=1, source_target_pairs={{0,1},{1,2},{2,3},{4,5},{5,6},{6,7},{8,9},{9,10},{10,11},{12,13},{... | collective-permute-start | bytes 49160 | tf_op jit(solution)/shard_map/while/body/eval_jaxpr/ppermute | solution.py:14
  125.5 6.7 %collective-permute-start = (f32[2,2,1,1024]{3,2,1,0:T(1,128)}, f32[2,2,1,1024]{3,2,1,0:T(1,128)}, u32[]{:S(2)}, u32[]{:S(2)}) collective-permute-start(f32[2,2,1,1024]{3,2,1,0:T(1,128)} %get-tuple-element.156), channel_id=1, source_target_pairs={{0,1},{1,2},{2,3},{4,5},{5,6},{6,7},{8,9},{9,10},{10,11},{12,13},{... | collective-permute-start | bytes 49160 | tf_op jit(solution)/shard_map/while/body/eval_jaxpr/ppermute | solution.py:14
  129.2 4.6 %collective-permute-start.1 = (f32[2,2,1,1024]{3,2,1,0:T(1,128)S(1)}, f32[2,2,1,1024]{3,2,1,0:T(1,128)}, u32[]{:S(2)}, u32[]{:S(2)}) collective-permute-start(f32[2,2,1,1024]{3,2,1,0:T(1,128)S(1)} %get-tuple-element.157), channel_id=1, source_target_pairs={{1,0},{2,1},{3,2},{5,4},{6,5},{7,6},{9,8},{10,9},{11,10},{13,12},{... | collective-permute-start | bytes 49160 | tf_op jit(solution)/shard_map/while/body/eval_jaxpr/ppermute | solution.py:17
  136.7 6.7 %collective-permute-start = (f32[2,2,1,1024]{3,2,1,0:T(1,128)}, f32[2,2,1,1024]{3,2,1,0:T(1,128)}, u32[]{:S(2)}, u32[]{:S(2)}) collective-permute-start(f32[2,2,1,1024]{3,2,1,0:T(1,128)} %get-tuple-element.156), channel_id=1, source_target_pairs={{0,1},{1,2},{2,3},{4,5},{5,6},{6,7},{8,9},{9,10},{10,11},{12,13},{... | collective-permute-start | bytes 49160 | tf_op jit(solution)/shard_map/while/body/eval_jaxpr/ppermute | solution.py:14
  140.4 4.6 %collective-permute-start.1 = (f32[2,2,1,1024]{3,2,1,0:T(1,128)S(1)}, f32[2,2,1,1024]{3,2,1,0:T(1,128)}, u32[]{:S(2)}, u32[]{:S(2)}) collective-permute-start(f32[2,2,1,1024]{3,2,1,0:T(1,128)S(1)} %get-tuple-element.157), channel_id=1, source_target_pairs={{1,0},{2,1},{3,2},{5,4},{6,5},{7,6},{9,8},{10,9},{11,10},{13,12},{... | collective-permute-start | bytes 49160 | tf_op jit(solution)/shard_map/while/body/eval_jaxpr/ppermute | solution.py:17
  147.9 6.7 %collective-permute-start = (f32[2,2,1,1024]{3,2,1,0:T(1,128)}, f32[2,2,1,1024]{3,2,1,0:T(1,128)}, u32[]{:S(2)}, u32[]{:S(2)}) collective-permute-start(f32[2,2,1,1024]{3,2,1,0:T(1,128)} %get-tuple-element.156), channel_id=1, source_target_pairs={{0,1},{1,2},{2,3},{4,5},{5,6},{6,7},{8,9},{9,10},{10,11},{12,13},{... | collective-permute-start | bytes 49160 | tf_op jit(solution)/shard_map/while/body/eval_jaxpr/ppermute | solution.py:14
  151.6 4.6 %collective-permute-start.1 = (f32[2,2,1,1024]{3,2,1,0:T(1,128)S(1)}, f32[2,2,1,1024]{3,2,1,0:T(1,128)}, u32[]{:S(2)}, u32[]{:S(2)}) collective-permute-start(f32[2,2,1,1024]{3,2,1,0:T(1,128)S(1)} %get-tuple-element.157), channel_id=1, source_target_pairs={{1,0},{2,1},{3,2},{5,4},{6,5},{7,6},{9,8},{10,9},{11,10},{13,12},{... | collective-permute-start | bytes 49160 | tf_op jit(solution)/shard_map/while/body/eval_jaxpr/ppermute | solution.py:17
  159.1 6.7 %collective-permute-start = (f32[2,2,1,1024]{3,2,1,0:T(1,128)}, f32[2,2,1,1024]{3,2,1,0:T(1,128)}, u32[]{:S(2)}, u32[]{:S(2)}) collective-permute-start(f32[2,2,1,1024]{3,2,1,0:T(1,128)} %get-tuple-element.156), channel_id=1, source_target_pairs={{0,1},{1,2},{2,3},{4,5},{5,6},{6,7},{8,9},{9,10},{10,11},{12,13},{... | collective-permute-start | bytes 49160 | tf_op jit(solution)/shard_map/while/body/eval_jaxpr/ppermute | solution.py:14
  170.3 6.7 %collective-permute-start = (f32[2,2,1,1024]{3,2,1,0:T(1,128)}, f32[2,2,1,1024]{3,2,1,0:T(1,128)}, u32[]{:S(2)}, u32[]{:S(2)}) collective-permute-start(f32[2,2,1,1024]{3,2,1,0:T(1,128)} %get-tuple-element.156), channel_id=1, source_target_pairs={{0,1},{1,2},{2,3},{4,5},{5,6},{6,7},{8,9},{9,10},{10,11},{12,13},{... | collective-permute-start | bytes 49160 | tf_op jit(solution)/shard_map/while/body/eval_jaxpr/ppermute | solution.py:14
  (34 other events, 72.6 us)
where the time goes:
time: 349 us; the launch traced here: 342 us
  local copies, waits for them, and re-layouts  132 us (38%)
  starting transfers between devices  80.8 us (23%)
  blocking collectives  58.9 us (17%)
  other arithmetic  55.7 us (16%)
  waiting for transfers between devices  13.9 us (4%)
    ppermute x16, starting transfers between devices, with_halo(): lax.ppermute(lax.slice_in_dim(block, block.shape[dim] - width, None, axis...  60.3 us
    pad x8, local copies, waits for them, and re-layouts, per_device(): lax.associative_scan(compose, (every_scale, every_shift), axis=0)  48 us
    all_to_all x1, blocking collectives, in_one_piece(): lax.all_to_all(both, axis, split_axis=split_dim, concat_axis=concat_dim,...  40.3 us
    while x64, local copies, waits for them, and re-layouts  33.7 us
    add x16, other arithmetic, one_step(): field_state + diffusion * (next_row + prev_row + next_col + prev_col - 4....  24.1 us
    ppermute x16, starting transfers between devices, with_halo(): lax.ppermute(lax.slice_in_dim(block, 0, width, axis=dim), axis, backward)  20.5 us
    slice x1, local copies, waits for them, and re-layouts, per_device(): inclusive_shift[:-1]  20 us
    all_to_all x1, blocking collectives, per_device(): lax.all_to_all(exclusive_shift, 'tm', split_axis=0, concat_axis=3, tiled=...  18.6 us
  transfers between devices with their start and end apart: 32, of which 16 were waited for; matrix products, arithmetic and copies ran while one was open for 8% of the time, Pallas kernels for 0%

commit v1 on v0

v1 whole, which is shorter than its diff:
```python
import jax
import jax.numpy as jnp
from jax import lax
from jax.experimental import pallas as pl
from jax.experimental.pallas import tpu as pltpu
from jax.sharding import PartitionSpec as P

M = 16
HALO = M


def fine_kernel(st_ref, dif_ref, frc_ref, keep_ref, out_ref, buf):
    rows = st_ref.shape[1]
    cols = st_ref.shape[2]
    buf[...] = st_ref[...]
    dif = dif_ref[...]
    keep = keep_ref[...] > 0.5

    def one_step(counter, carry):
        for slot in range(2):
            u = buf[2 * slot]
            v = buf[2 * slot + 1]
            new = []
            for comp, c in enumerate((u, v)):
                next_row = pltpu.roll(c, rows - 1, 0)
                prev_row = pltpu.roll(c, 1, 0)
                next_col = pltpu.roll(c, cols - 1, 1)
                prev_col = pltpu.roll(c, 1, 1)
                value = (
                    c
                    + dif * (next_row + prev_row + next_col + prev_col - 4.0 * c)
                    - 0.05 * (u * (next_row - prev_row) + v * (next_col - prev_col))
                    + 0.05 * frc_ref[comp]
                )
                new.append(jnp.where(keep, value, 0.0))
            buf[2 * slot] = new[0]
            buf[2 * slot + 1] = new[1]
        return carry

    lax.fori_loop(0, M, one_step, 0)
    out_ref[...] = buf[:, HALO:rows - HALO, :]


def scan_kernel(a_ref, b_ref, x_ref):
    x = jnp.zeros(a_ref.shape[1:], jnp.float32)
    for s in range(a_ref.shape[0]):
        x_ref[s] = x
        x = a_ref[s] * x + b_ref[s]


def to_tiles(block):
    rows, cols = block.shape[-2] * block.shape[-3], block.shape[-1]
    flat = block.reshape(rows // 8, 8, cols // 128, 128)
    return flat.transpose(0, 2, 1, 3).reshape(-1, 8, 128)


def from_tiles(tiles, shape):
    rows, cols = shape[0] * shape[1], shape[2]
    grid = tiles.reshape(rows // 8, cols // 128, 8, 128)
    return grid.transpose(0, 2, 1, 3).reshape(shape)


def per_device(coarse_points, coarse_decay, diffusion, forcing):
    slots, comps, row_count, col_count = coarse_points.shape
    space_count = lax.axis_size("space")
    tm_count = lax.axis_size("tm")
    me = lax.axis_index("space")

    state = coarse_points.reshape(slots * comps, row_count, col_count)
    pack = jnp.concatenate([state, diffusion[None], forcing], axis=0)
    forward = [(i, i + 1) for i in range(space_count - 1)]
    backward = [(i + 1, i) for i in range(space_count - 1)]
    above = lax.ppermute(pack[:, row_count - HALO:], "space", forward)
    below = lax.ppermute(pack[:, :HALO], "space", backward)
    ext = jnp.concatenate([above, pack, below], axis=1)
    ext_rows = row_count + 2 * HALO
    global_row = me * row_count - HALO + lax.broadcasted_iota(jnp.int32, (ext_rows, 1), 0)
    keep = ((global_row >= 0) & (global_row < space_count * row_count)).astype(jnp.float32)

    fine_end = pl.pallas_call(
        fine_kernel,
        out_shape=jax.ShapeDtypeStruct((slots * comps, row_count, col_count), jnp.float32),
        scratch_shapes=[pltpu.VMEM((slots * comps, ext_rows, col_count), jnp.float32)],
    )(ext[: slots * comps], ext[slots * comps], ext[slots * comps + 1:], keep)
    fine_end = fine_end.reshape(coarse_points.shape)

    shift = fine_end - coarse_decay * coarse_points
    scale = coarse_decay
    at_anchor = lax.axis_index("tm") == 0
    shift0 = jnp.where(at_anchor, coarse_decay[0] * coarse_points[0] + shift[0], shift[0])
    scale0 = jnp.where(at_anchor, 0.0, scale[0])
    comp_scale = scale[1] * scale0
    comp_shift = scale[1] * shift0 + shift[1]

    both = jnp.stack([to_tiles(comp_scale), to_tiles(comp_shift)])
    got = lax.all_to_all(both, "tm", split_axis=1, concat_axis=1, tiled=True)
    per_src = got.shape[1] // tm_count
    got = got.reshape(2, tm_count, per_src, 8, 128)
    prefix = pl.pallas_call(
        scan_kernel,
        out_shape=jax.ShapeDtypeStruct((tm_count, per_src, 8, 128), jnp.float32),
    )(got[0], got[1])
    back = lax.all_to_all(
        prefix.reshape(tm_count * per_src, 8, 128), "tm", split_axis=0, concat_axis=0, tiled=True
    )
    entering = from_tiles(back, (comps, row_count, col_count))

    first = scale0 * entering + shift0
    second = scale[1] * first + shift[1]
    return jnp.stack([first, second], axis=0)


def solution(mesh):
    placed = (
        P("tm", None, "space", None),
        P("tm", None, "space", None),
        P("space", None),
        P(None, "space", None),
    )
    return jax.shard_map(
        per_device,
        mesh=mesh,
        in_specs=placed,
        out_specs=P("tm", None, "space", None),
        check_vma=False,
    )
```

time: 349 us -> 95.9 us (0.27); the launches traced: 342 us -> 95.6 us
  local copies, waits for them, and re-layouts: 132 us -> 2.92 us
  starting transfers between devices: 80.8 us -> 5.24 us
  other arithmetic: 55.7 us -> 5.95 us
  Pallas kernels: 0 us -> 20.4 us
  blocking collectives: 58.9 us -> 49.7 us
    ppermute x32 -> x2, starting transfers between devices: 80.8 us -> 5.24 us  [the longest x1 3.95 us: per_device(): above = lax.ppermute(pack[:, row_count - HALO:], 'space', forward)]
    pad x8 -> x0, local copies, waits for them, and re-layouts: 48 us -> none  [per_device(): lax.associative_scan(compose, (every_scale, every_shift), axis=0)]
    slice x70 -> x3, local copies, waits for them, and re-layouts: 38.1 us -> 2.07 us  [the longest x1 1.05 us: per_device(): ext[:slots * comps]]
    add x26 -> x1, other arithmetic: 34.3 us -> 0.11 us  [per_device(): second = scale[1] * first + shift[1]]
    while x64 -> x0, local copies, waits for them, and re-layouts: 33.7 us -> none
    pallas_call x0 -> x2, Pallas kernels: none -> 20.4 us  [the longest x1 18.6 us: per_device(): pl.pallas_call(fine_kernel, out_shape=jax.ShapeDtypeStruct((slots * comps...]
    broadcast_in_dim x16 -> x0, other arithmetic: 9.34 us -> none  [one_step(): jnp.where(at_top, rims[:, :, 0:1], jnp.roll(field_state, 1, axis=2))]
    all_to_all x2, blocking collectives: 58.9 us -> 49.7 us  [the longest x1 31 us: per_device(): got = lax.all_to_all(both, 'tm', split_axis=1, concat_axis=1, tiled=True)]
  transfers between devices with their start and end apart: 32 -> 2, of which waited for: 16 -> 2; matrix products, arithmetic and copies ran while one was open for 8% -> 1% of each run, Pallas kernels for 0% -> 0%
where the time goes in v1:
time: 95.9 us; the launch traced here: 95.6 us
  blocking collectives  49.7 us (52%)
  Pallas kernels  20.4 us (21%)
  waiting for transfers between devices  11.2 us (12%)
  other arithmetic  5.95 us (6%)
  starting transfers between devices  5.24 us (5%)
  local copies, waits for them, and re-layouts  2.92 us (3%)
    all_to_all x1, blocking collectives, per_device(): got = lax.all_to_all(both, 'tm', split_axis=1, concat_axis=1, tiled=True)  31 us
    all_to_all x1, blocking collectives, per_device(): lax.all_to_all(prefix.reshape(tm_count * per_src, 8, 128), 'tm', split_ax...  18.8 us
    pallas_call x1, Pallas kernels, per_device(): pl.pallas_call(fine_kernel, out_shape=jax.ShapeDtypeStruct((slots * comps...  18.6 us
    ppermute x1, waiting for transfers between devices, per_device(): above = lax.ppermute(pack[:, row_count - HALO:], 'space', forward)  7.47 us
    ppermute x1, starting transfers between devices, per_device(): above = lax.ppermute(pack[:, row_count - HALO:], 'space', forward)  3.95 us
    ppermute x1, waiting for transfers between devices, per_device(): below = lax.ppermute(pack[:, :HALO], 'space', backward)  3.75 us
  transfers between devices with their start and end apart: 2, of which 2 were waited for; matrix products, arithmetic and copies ran while one was open for 1% of the time, Pallas kernels for 0%

profile of v1, /device:TPU:1, one launch (start us, length us, event | category | flops | bytes accessed | tf_op | source)
XLA Modules:
  0.0 95.6 jit_solution(280286858478030102)
XLA Ops:
  0.0 1.3 %pad_maximum_fusion.1 = f32[7,32,1024]{2,1,0:T(8,128)S(1)} fusion(f32[2,32,1024]{2,1,0:T(8,128)} %param.7, f32[1,32,1024]{2,1,0:T(8,128)} %bitcast.35, f32[4,32,1024]{2,1,0:T(8,128)} %bitcast.30), kind=kLoop, calls=%fused_computation.1 | loop fusion | flops 458752 | bytes 1835008 | tf_op jit(solution)/shard_map/concatenate | solution.py:70
  1.3 0.0 copy-start.2
  1.4 0.0 copy-start.3
  1.4 1.0 %fusion.8 = (f32[7,16,1024]{2,1,0:T(8,128)}, f32[7,16,1024]{2,1,0:T(8,128)}) fusion(f32[7,32,1024]{2,1,0:T(8,128)S(1)} %pad_maximum_fusion.1), kind=kLoop, calls=%fused_computation.22 | loop fusion | bytes 1835008 | tf_op jit(solution)/shard_map/slice | solution.py:73
  2.4 3.9 %collective-permute-start = (f32[7,16,1024]{2,1,0:T(8,128)}, f32[7,16,1024]{2,1,0:T(8,128)S(1)}, u32[]{:S(2)}, u32[]{:S(2)}) collective-permute-start(f32[7,16,1024]{2,1,0:T(8,128)} %get-tuple-element.7), channel_id=1, source_target_pairs={{0,1},{1,2},{2,3},{4,5},{5,6},{6,7},{8,9},{9,10},{10,11},{12,13},{... | collective-permute-start | bytes 1376264 | tf_op jit(solution)/shard_map/ppermute | solution.py:73
  6.3 1.3 %collective-permute-start.1 = (f32[7,16,1024]{2,1,0:T(8,128)}, f32[7,16,1024]{2,1,0:T(8,128)S(1)}, u32[]{:S(2)}, u32[]{:S(2)}) collective-permute-start(f32[7,16,1024]{2,1,0:T(8,128)} %get-tuple-element.8), channel_id=1, source_target_pairs={{1,0},{2,1},{3,2},{5,4},{6,5},{7,6},{9,8},{10,9},{11,10},{13,12},{... | collective-permute-start | bytes 1376264 | tf_op jit(solution)/shard_map/ppermute | solution.py:74
  7.6 0.6 fusion.6.keep_ref
  8.2 0.0 copy-done
  8.2 0.1 slice_select_fusion
  8.3 7.5 %collective-permute-done = f32[7,16,1024]{2,1,0:T(8,128)S(1)} collective-permute-done((f32[7,16,1024]{2,1,0:T(8,128)}, f32[7,16,1024]{2,1,0:T(8,128)S(1)}, u32[]{:S(2)}, u32[]{:S(2)}) %collective-permute-start) | collective-permute-done | bytes 458784 | tf_op jit(solution)/shard_map/ppermute | solution.py:73
  15.8 3.8 %collective-permute-done.1 = f32[7,16,1024]{2,1,0:T(8,128)S(1)} collective-permute-done((f32[7,16,1024]{2,1,0:T(8,128)}, f32[7,16,1024]{2,1,0:T(8,128)S(1)}, u32[]{:S(2)}, u32[]{:S(2)}) %collective-permute-start.1) | collective-permute-done | bytes 458784 | tf_op jit(solution)/shard_map/ppermute | solution.py:74
  19.5 0.2 pad_maximum_fusion
  19.8 1.0 %slice.57.st_ref = f32[4,64,1024]{2,1,0:T(8,128)} slice(f32[7,64,1024]{2,1,0:T(8,128)S(1)} %pad_maximum_fusion), slice={[0:4], [0:64], [0:1024]} | slice | bytes 2097152 | tf_op jit(solution)/shard_map/slice | solution.py:84
  20.8 0.8 pad_maximum_fusion.2.frc_ref
  21.6 0.7 maximum_bitcast_fusion.dif_ref
  22.4 18.6 %shard_map.46 = f32[4,32,1024]{2,1,0:T(8,128)} custom-call(f32[4,64,1024]{2,1,0:T(8,128)} %slice.57.st_ref, f32[64,1024]{1,0:T(8,128)} %maximum_bitcast_fusion.dif_ref, f32[2,64,1024]{2,1,0:T(8,128)} %pad_maximum_fusion.2.frc_ref, f32[64,1]{1,0:T(8,128)} %fusion.6.keep_ref), custom_call_target="tpu_custom_call" | custom-call | tf_op jit(solution)/shard_map/pallas_call | solution.py:80
  40.9 1.1 %multiply_subtract_fusion = f32[2,2,32,1024]{3,2,1,0:T(8,128)S(1)} fusion(f32[2,2,32,1024]{3,2,1,0:T(8,128)} %bitcast.39, f32[2,2,32,1024]{3,2,1,0:T(8,128)S(1)} %copy-done.1, f32[2,2,32,1024]{3,2,1,0:T(8,128)S(1)} %copy-done), kind=kLoop, calls=%fused_computation.5 | loop fusion | flops 262144 | bytes 2097152 | tf_op jit(solution)/shard_map/sub | solution.py:87
  42.1 0.1 fusion.10
  42.2 31.0 %all_to_all.10 = f32[2,64,8,128]{3,2,0,1:T(8,128)S(1)} all-to-all(f32[2,64,8,128]{3,2,0,1:T(8,128)S(1)} %pad_maximum_fusion.3), channel_id=1, replica_groups=mesh['tm'=64,'space'=4] {'tm'}, dimensions={1} | all-to-all | bytes 1048576 | tf_op jit(solution)/shard_map/all_to_all | solution.py:96
  73.2 0.8 slice_bitcast_fusion
  74.0 1.9 %shard_map.47 = f32[64,1,8,128]{3,2,1,0:T(8,128)} custom-call(f32[64,1,8,128]{3,2,1,0:T(8,128)} %get-tuple-element.10.a_ref, f32[64,1,8,128]{3,2,1,0:T(8,128)} %get-tuple-element.9.b_ref), custom_call_target="tpu_custom_call" | custom-call | tf_op jit(solution)/shard_map/pallas_call | solution.py:99
  75.9 18.8 %all_to_all.11 = f32[64,8,128]{2,1,0:T(8,128)S(1)} all-to-all(f32[64,8,128]{2,1,0:T(8,128)} %bitcast.41), channel_id=1, replica_groups=mesh['tm'=64,'space'=4] {'tm'}, dimensions={0} | all-to-all | bytes 524288 | tf_op jit(solution)/shard_map/all_to_all | solution.py:103
  94.6 0.1 multiply_add_fusion
  94.7 0.8 pad_maximum_fusion.4
  (7 shorter events, 0.1 us)
Async XLA Ops:
  0.0 8.2 %copy-start = (f32[2,2,32,1024]{3,2,1,0:T(8,128)S(1)}, f32[2,2,32,1024]{3,2,1,0:T(8,128)}, u32[]{:S(2)}) copy-start(f32[2,2,32,1024]{3,2,1,0:T(8,128)} %param.4) | copy-start | bytes 1572868
  0.0 8.2 %copy-start.1 = (f32[2,2,32,1024]{3,2,1,0:T(8,128)S(1)}, f32[2,2,32,1024]{3,2,1,0:T(8,128)}, u32[]{:S(2)}) copy-start(f32[2,2,32,1024]{3,2,1,0:T(8,128)} %param.5) | copy-start | bytes 1572868
  1.3 18.2 %copy-start.2 = (f32[2,32,1024]{2,1,0:T(8,128)S(1)}, f32[2,32,1024]{2,1,0:T(8,128)}, u32[]{:S(2)}) copy-start(f32[2,32,1024]{2,1,0:T(8,128)} %param.7) | copy-start | bytes 786436
  1.4 18.2 %copy-start.3 = (f32[32,1024]{1,0:T(8,128)S(1)}, f32[32,1024]{1,0:T(8,128)}, u32[]{:S(2)}) copy-start(f32[32,1024]{1,0:T(8,128)} %param.6) | copy-start | bytes 393220
  2.4 13.4 %collective-permute-start = (f32[7,16,1024]{2,1,0:T(8,128)}, f32[7,16,1024]{2,1,0:T(8,128)S(1)}, u32[]{:S(2)}, u32[]{:S(2)}) collective-permute-start(f32[7,16,1024]{2,1,0:T(8,128)} %get-tuple-element.7), channel_id=1, source_target_pairs={{0,1},{1,2},{2,3},{4,5},{5,6},{6,7},{8,9},{9,10},{10,11},{12,13},{... | collective-permute-start | bytes 1376264 | tf_op jit(solution)/shard_map/ppermute | solution.py:73
  6.3 13.2 %collective-permute-start.1 = (f32[7,16,1024]{2,1,0:T(8,128)}, f32[7,16,1024]{2,1,0:T(8,128)S(1)}, u32[]{:S(2)}, u32[]{:S(2)}) collective-permute-start(f32[7,16,1024]{2,1,0:T(8,128)} %get-tuple-element.8), channel_id=1, source_target_pairs={{1,0},{2,1},{3,2},{5,4},{6,5},{7,6},{9,8},{10,9},{11,10},{13,12},{... | collective-permute-start | bytes 1376264 | tf_op jit(solution)/shard_map/ppermute | solution.py:74

commit v2 on v1

v2 whole, which is shorter than its diff:
```python
import jax
import jax.numpy as jnp
from jax import lax
from jax.experimental import pallas as pl
from jax.experimental.pallas import tpu as pltpu
from jax.sharding import PartitionSpec as P

M = 16
HALO = M


def fine_kernel(st_ref, dif_ref, frc_ref, up_ref, dn_ref, keep_ref, order_ref, out_ref, buf, dbuf, fbuf):
    n_state = st_ref.shape[0]
    own = st_ref.shape[1]
    cols = st_ref.shape[2]
    rows = own + 2 * HALO
    buf[:, :HALO] = up_ref[:n_state]
    buf[:, HALO:HALO + own] = st_ref[...]
    buf[:, HALO + own:] = dn_ref[:n_state]
    dbuf[:HALO] = up_ref[n_state]
    dbuf[HALO:HALO + own] = dif_ref[...]
    dbuf[HALO + own:] = dn_ref[n_state]
    fbuf[:, :HALO] = up_ref[n_state + 1:]
    fbuf[:, HALO:HALO + own] = frc_ref[...]
    fbuf[:, HALO + own:] = dn_ref[n_state + 1:]

    def make_step(lo, hi):
        span = hi - lo

        def one_step(counter, carry):
            dif = dbuf[lo:hi]
            keep = keep_ref[lo:hi] > 0.5
            for slot in range(2):
                u = buf[2 * slot, lo:hi]
                v = buf[2 * slot + 1, lo:hi]
                new = []
                for comp, c in enumerate((u, v)):
                    next_row = pltpu.roll(c, span - 1, 0)
                    prev_row = pltpu.roll(c, 1, 0)
                    next_col = pltpu.roll(c, cols - 1, 1)
                    prev_col = pltpu.roll(c, 1, 1)
                    value = (
                        c
                        + dif * (next_row + prev_row + next_col + prev_col - 4.0 * c)
                        - 0.05 * (u * (next_row - prev_row) + v * (next_col - prev_col))
                        + 0.05 * fbuf[comp, lo:hi]
                    )
                    new.append(jnp.where(keep, value, 0.0))
                buf[2 * slot, lo:hi] = new[0]
                buf[2 * slot + 1, lo:hi] = new[1]
            return carry

        return one_step

    half = M // 2
    lax.fori_loop(0, half, make_step(0, rows), 0)
    lax.fori_loop(0, M - half, make_step(half, rows - half), 0)
    out_ref[...] = buf[:, HALO:HALO + own, :]


def scan_kernel(a_ref, b_ref, x_ref):
    x = jnp.zeros(a_ref.shape[1:], jnp.float32)
    for s in range(a_ref.shape[0]):
        x_ref[s] = x
        x = a_ref[s] * x + b_ref[s]


def to_tiles(block):
    rows, cols = block.shape[-2] * block.shape[-3], block.shape[-1]
    flat = block.reshape(rows // 8, 8, cols // 128, 128)
    return flat.transpose(0, 2, 1, 3).reshape(-1, 8, 128)


def from_tiles(tiles, shape):
    rows, cols = shape[0] * shape[1], shape[2]
    grid = tiles.reshape(rows // 8, cols // 128, 8, 128)
    return grid.transpose(0, 2, 1, 3).reshape(shape)


def per_device_body(coarse_points, coarse_decay, diffusion, forcing):
    slots, comps, row_count, col_count = coarse_points.shape
    space_count = lax.axis_size("space")
    tm_count = lax.axis_size("tm")
    me = lax.axis_index("space")

    at_anchor = lax.axis_index("tm") == 0
    scale0 = jnp.where(at_anchor, 0.0, coarse_decay[0])
    comp_scale = coarse_decay[1] * scale0
    scale_tiles = to_tiles(comp_scale)
    got_scale = lax.all_to_all(scale_tiles, "tm", split_axis=0, concat_axis=0, tiled=True)

    state = coarse_points.reshape(slots * comps, row_count, col_count)
    forward = [(i, i + 1) for i in range(space_count - 1)]
    backward = [(i + 1, i) for i in range(space_count - 1)]

    def rim(lo, hi):
        return jnp.concatenate([state[:, lo:hi], diffusion[None, lo:hi], forcing[:, lo:hi]], axis=0)

    up_rim = rim(row_count - HALO, row_count)
    dn_rim = rim(0, HALO)
    above = lax.ppermute(up_rim, "space", forward)
    below = lax.ppermute(dn_rim, "space", backward)
    ext_rows = row_count + 2 * HALO
    global_row = me * row_count - HALO + lax.broadcasted_iota(jnp.int32, (ext_rows, 1), 0)
    keep = ((global_row >= 0) & (global_row < space_count * row_count)).astype(jnp.float32)

    vmem = pl.BlockSpec(memory_space=pltpu.VMEM)
    fine_end = pl.pallas_call(
        fine_kernel,
        out_shape=jax.ShapeDtypeStruct((slots * comps, row_count, col_count), jnp.float32),
        in_specs=[vmem] * 6 + [pl.BlockSpec(memory_space=pl.ANY)],
        out_specs=vmem,
        scratch_shapes=[
            pltpu.VMEM((slots * comps, ext_rows, col_count), jnp.float32),
            pltpu.VMEM((ext_rows, col_count), jnp.float32),
            pltpu.VMEM((comps, ext_rows, col_count), jnp.float32),
        ],
    )(state, diffusion, forcing, above, below, keep, got_scale)
    fine_end = fine_end.reshape(coarse_points.shape)

    shift = fine_end - coarse_decay * coarse_points
    scale = coarse_decay
    shift0 = jnp.where(at_anchor, coarse_decay[0] * coarse_points[0] + shift[0], shift[0])
    comp_shift = scale[1] * shift0 + shift[1]

    got_shift = lax.all_to_all(to_tiles(comp_shift), "tm", split_axis=0, concat_axis=0, tiled=True)
    per_src = got_shift.shape[0] // tm_count
    tile_shape = (tm_count, per_src, 8, 128)
    prefix = pl.pallas_call(
        scan_kernel,
        out_shape=jax.ShapeDtypeStruct(tile_shape, jnp.float32),
    )(got_scale.reshape(tile_shape), got_shift.reshape(tile_shape))
    back = lax.all_to_all(
        prefix.reshape(tm_count * per_src, 8, 128), "tm", split_axis=0, concat_axis=0, tiled=True
    )
    entering = from_tiles(back, (comps, row_count, col_count))

    first = scale0 * entering + shift0
    second = scale[1] * first + shift[1]
    return jnp.stack([first, second], axis=0)


def solution(mesh):
    placed = (
        P("tm", None, "space", None),
        P("tm", None, "space", None),
        P("space", None),
        P(None, "space", None),
    )
    return jax.shard_map(
        per_device_body,
        mesh=mesh,
        in_specs=placed,
        out_specs=P("tm", None, "space", None),
        check_vma=False,
    )
```

time: 95.9 us -> 98.5 us (1.027)
  starting transfers between devices: 5.24 us -> 18.7 us
  blocking collectives: 49.7 us -> 42 us
  Pallas kernels: 20.4 us -> 18.3 us
  other arithmetic: 5.95 us -> 4.41 us
    all_to_all x0 -> x1, starting transfers between devices: none -> 12.6 us  [per_device_body(): lax.all_to_all(scale_tiles, 'tm', split_axis=0, concat_axis=0, tiled=True)]
    all_to_all x2, blocking collectives: 49.7 us -> 42 us  [the longest x1 24.2 us: per_device_body(): lax.all_to_all(to_tiles(comp_shift), 'tm', split_axis=0, concat_axis=0, t...]
    pallas_call x2, Pallas kernels: 20.4 us -> 18.3 us  [the longest x1 16.4 us: per_device_body(): pl.pallas_call(fine_kernel, out_shape=jax.ShapeDtypeStruct((slots * comps...]
    slice x3, local copies, waits for them, and re-layouts: 2.07 us -> 0.1 us  [the longest x1 0.04 us: per_device_body(): shift[0]]
    unnamed x8 -> x12, local copies, waits for them, and re-layouts: 0.02 us -> 1.68 us
  transfers between devices with their start and end apart: 2 -> 3, of which waited for: 2 -> 1; matrix products, arithmetic and copies ran while one was open for 1% -> 2% of each run, Pallas kernels for 0% -> 0%
where the time goes in v2:
time: 98.5 us; the launch traced here: 98.1 us
  blocking collectives  42 us (43%)
  starting transfers between devices  18.7 us (19%)
  Pallas kernels  18.3 us (19%)
  waiting for transfers between devices  11.8 us (12%)
  other arithmetic  4.41 us (4%)
  local copies, waits for them, and re-layouts  2.73 us (3%)
    all_to_all x1, blocking collectives, per_device_body(): lax.all_to_all(to_tiles(comp_shift), 'tm', split_axis=0, concat_axis=0, t...  24.2 us
    all_to_all x1, blocking collectives, per_device_body(): lax.all_to_all(prefix.reshape(tm_count * per_src, 8, 128), 'tm', split_ax...  17.8 us
    pallas_call x1, Pallas kernels, per_device_body(): pl.pallas_call(fine_kernel, out_shape=jax.ShapeDtypeStruct((slots * comps...  16.4 us
    all_to_all x1, starting transfers between devices, per_device_body(): lax.all_to_all(scale_tiles, 'tm', split_axis=0, concat_axis=0, tiled=True)  12.6 us
    ppermute x1, waiting for transfers between devices, per_device_body(): below = lax.ppermute(dn_rim, 'space', backward)  11.8 us
    ppermute x1, starting transfers between devices, per_device_body(): above = lax.ppermute(up_rim, 'space', forward)  4.84 us
  transfers between devices with their start and end apart: 3, of which 1 were waited for; matrix products, arithmetic and copies ran while one was open for 2% of the time, Pallas kernels for 0%

profile of v2, /device:TPU:1, one launch (start us, length us, event | category | flops | bytes accessed | tf_op | source)
XLA Modules:
  0.0 98.1 jit_solution(2423219459137370761)
XLA Ops:
  0.0 1.0 slice_bitcast_fusion
  1.0 0.1 copy-done.4
  1.0 0.2 copy-done
  1.2 0.0 copy-start.2
  1.3 4.8 %collective-permute-start = (f32[7,16,1024]{2,1,0:T(8,128)S(1)}, f32[7,16,1024]{2,1,0:T(8,128)}, u32[]{:S(2)}, u32[]{:S(2)}) collective-permute-start(f32[7,16,1024]{2,1,0:T(8,128)S(1)} %pad_maximum_fusion.1), channel_id=1, source_target_pairs={{0,1},{1,2},{2,3},{4,5},{5,6},{6,7},{8,9},{9,10},{10,11},{12,13},{... | collective-permute-start | bytes 1376264 | tf_op jit(solution)/shard_map/ppermute | solution.py:101
  6.1 0.1 slice_multiply_fusion
  6.2 0.7 mul.32
  6.9 12.6 %all-to-all-start = ((f32[64,8,128]{2,1,0:T(8,128)}), f32[64,8,128]{2,1,0:T(8,128)S(1)}, u32[]{:S(2)}, u32[]{:S(2)}) async-start(f32[64,8,128]{2,1,0:T(8,128)} %bitcast.3), calls=%async_computation | async-start | bytes 524288 | tf_op jit(solution)/shard_map/all_to_all | solution.py:90
  19.6 0.8 pad_maximum_fusion.2
  20.4 1.3 %collective-permute-start.1 = (f32[7,16,1024]{2,1,0:T(8,128)}, f32[7,16,1024]{2,1,0:T(8,128)S(1)}, u32[]{:S(2)}, u32[]{:S(2)}) collective-permute-start(f32[7,16,1024]{2,1,0:T(8,128)} %pad_maximum_fusion.2), channel_id=1, source_target_pairs={{1,0},{2,1},{3,2},{5,4},{6,5},{7,6},{9,8},{10,9},{11,10},{13,12},{... | collective-permute-start | bytes 1376264 | tf_op jit(solution)/shard_map/ppermute | solution.py:102
  21.6 0.6 fusion.6.keep_ref
  22.3 0.0 collective-permute-done.up_ref
  22.3 11.8 %collective-permute-done.1.dn_ref = f32[7,16,1024]{2,1,0:T(8,128)S(1)} collective-permute-done((f32[7,16,1024]{2,1,0:T(8,128)}, f32[7,16,1024]{2,1,0:T(8,128)S(1)}, u32[]{:S(2)}, u32[]{:S(2)}) %collective-permute-start.1) | collective-permute-done | bytes 458784 | tf_op jit(solution)/shard_map/ppermute | solution.py:102
  34.1 0.0 all-to-all-done.order_ref
  34.1 0.8 copy-done.5
  34.8 0.7 copy-done.3
  35.5 16.4 %shard_map.46 = f32[4,32,1024]{2,1,0:T(8,128)} custom-call(f32[4,32,1024]{2,1,0:T(8,128)} %bitcast.25, f32[32,1024]{1,0:T(8,128)} %dif_ref.1, f32[2,32,1024]{2,1,0:T(8,128)} %frc_ref.1, f32[7,16,1024]{2,1,0:T(8,128)} %collective-permute-done.up_ref, f32[7,16,1024]{2,1,0:T(8,128)} %copy-done.5, f32[64,1]{1,0:T(8,128)} %fusion.6.keep_ref, f32[64,8,128]{2,1,0:T(8,128)} %copy-done.3), custom_call_target="tpu_custom_call" | custom-call | tf_op jit(solution)/shard_map/pallas_call | solution.py:108
  52.0 1.1 %multiply_subtract_fusion = f32[2,2,32,1024]{3,2,1,0:T(8,128)S(1)} fusion(f32[2,2,32,1024]{3,2,1,0:T(8,128)} %bitcast.31, f32[2,2,32,1024]{3,2,1,0:T(8,128)S(1)} %copy-done.2, f32[2,2,32,1024]{3,2,1,0:T(8,128)S(1)} %copy-done.1), kind=kLoop, calls=%fused_computation.1 | loop fusion | flops 262144 | bytes 2097152 | tf_op jit(solution)/shard_map/sub | solution.py:121
  53.2 0.1 fusion.1
  53.2 24.2 %all_to_all.15 = f32[64,8,128]{2,1,0:T(8,128)} all-to-all(f32[64,8,128]{2,1,0:T(8,128)S(1)} %bitcast.33), channel_id=1, replica_groups=mesh['tm'=64,'space'=4] {'tm'}, dimensions={0} | all-to-all | bytes 524288 | tf_op jit(solution)/shard_map/all_to_all | solution.py:126
  77.4 1.9 %shard_map.47 = f32[64,1,8,128]{3,2,1,0:T(8,128)} custom-call(f32[64,1,8,128]{3,2,1,0:T(8,128)} %bitcast.30, f32[64,1,8,128]{3,2,1,0:T(8,128)} %bitcast.34), custom_call_target="tpu_custom_call" | custom-call | tf_op jit(solution)/shard_map/pallas_call | solution.py:129
  79.3 17.8 %all_to_all.16 = f32[64,8,128]{2,1,0:T(8,128)S(1)} all-to-all(f32[64,8,128]{2,1,0:T(8,128)} %bitcast.35), channel_id=1, replica_groups=mesh['tm'=64,'space'=4] {'tm'}, dimensions={0} | all-to-all | bytes 524288 | tf_op jit(solution)/shard_map/all_to_all | solution.py:133
  97.2 0.1 multiply_add_fusion
  97.3 0.8 pad_maximum_fusion
  (11 shorter events, 0.1 us)
Async XLA Ops:
  0.0 1.0 %copy-start.4 = (f32[2,32,1024]{2,1,0:T(8,128)S(1)}, f32[2,32,1024]{2,1,0:T(8,128)}, u32[]{:S(2)}) copy-start(f32[2,32,1024]{2,1,0:T(8,128)} %frc_ref.1) | copy-start | bytes 786436
  0.0 1.2 %copy-start = (f32[2,2,32,1024]{3,2,1,0:T(8,128)S(1)}, f32[2,2,32,1024]{3,2,1,0:T(8,128)}, u32[]{:S(2)}) copy-start(f32[2,2,32,1024]{3,2,1,0:T(8,128)} %param.4) | copy-start | bytes 1572868
  1.2 4.9 %copy-start.2 = (f32[2,2,32,1024]{3,2,1,0:T(8,128)S(1)}, f32[2,2,32,1024]{3,2,1,0:T(8,128)}, u32[]{:S(2)}) copy-start(f32[2,2,32,1024]{3,2,1,0:T(8,128)} %param.5) | copy-start | bytes 1572868
  1.3 21.0 %collective-permute-start = (f32[7,16,1024]{2,1,0:T(8,128)S(1)}, f32[7,16,1024]{2,1,0:T(8,128)}, u32[]{:S(2)}, u32[]{:S(2)}) collective-permute-start(f32[7,16,1024]{2,1,0:T(8,128)S(1)} %pad_maximum_fusion.1), channel_id=1, source_target_pairs={{0,1},{1,2},{2,3},{4,5},{5,6},{6,7},{8,9},{9,10},{10,11},{12,13},{... | collective-permute-start | bytes 1376264 | tf_op jit(solution)/shard_map/ppermute | solution.py:101
  6.9 27.1 %all-to-all-start = ((f32[64,8,128]{2,1,0:T(8,128)}), f32[64,8,128]{2,1,0:T(8,128)S(1)}, u32[]{:S(2)}, u32[]{:S(2)}) async-start(f32[64,8,128]{2,1,0:T(8,128)} %bitcast.3), calls=%async_computation | async-start | bytes 524288 | tf_op jit(solution)/shard_map/all_to_all | solution.py:90
  20.4 13.7 %collective-permute-start.1 = (f32[7,16,1024]{2,1,0:T(8,128)}, f32[7,16,1024]{2,1,0:T(8,128)S(1)}, u32[]{:S(2)}, u32[]{:S(2)}) collective-permute-start(f32[7,16,1024]{2,1,0:T(8,128)} %pad_maximum_fusion.2), channel_id=1, source_target_pairs={{1,0},{2,1},{3,2},{5,4},{6,5},{7,6},{9,8},{10,9},{11,10},{13,12},{... | collective-permute-start | bytes 1376264 | tf_op jit(solution)/shard_map/ppermute | solution.py:102
  22.3 29.7 %copy-start.1 = (f32[2,2,32,1024]{3,2,1,0:T(8,128)S(1)}, f32[2,2,32,1024]{3,2,1,0:T(8,128)}, u32[]{:S(2)}) copy-start(f32[2,2,32,1024]{3,2,1,0:T(8,128)} %param.4) | copy-start | bytes 1572868
  34.1 0.8 copy-start.5
  34.8 0.7 copy-start.3

commit v3 on v2

--- a/solution.py
+++ b/solution.py
@@ -9,7 +9,7 @@
 HALO = M
 
 
-def fine_kernel(st_ref, dif_ref, frc_ref, up_ref, dn_ref, keep_ref, order_ref, out_ref, buf, dbuf, fbuf):
+def fine_kernel(st_ref, dif_ref, frc_ref, up_ref, dn_ref, keep_ref, out_ref, buf, dbuf, fbuf):
     n_state = st_ref.shape[0]
     own = st_ref.shape[1]
     cols = st_ref.shape[2]
@@ -86,8 +86,6 @@
     at_anchor = lax.axis_index("tm") == 0
     scale0 = jnp.where(at_anchor, 0.0, coarse_decay[0])
     comp_scale = coarse_decay[1] * scale0
-    scale_tiles = to_tiles(comp_scale)
-    got_scale = lax.all_to_all(scale_tiles, "tm", split_axis=0, concat_axis=0, tiled=True)
 
     state = coarse_points.reshape(slots * comps, row_count, col_count)
     forward = [(i, i + 1) for i in range(space_count - 1)]
@@ -108,14 +106,14 @@
     fine_end = pl.pallas_call(
         fine_kernel,
         out_shape=jax.ShapeDtypeStruct((slots * comps, row_count, col_count), jnp.float32),
-        in_specs=[vmem] * 6 + [pl.BlockSpec(memory_space=pl.ANY)],
+        in_specs=[vmem] * 6,
         out_specs=vmem,
         scratch_shapes=[
             pltpu.VMEM((slots * comps, ext_rows, col_count), jnp.float32),
             pltpu.VMEM((ext_rows, col_count), jnp.float32),
             pltpu.VMEM((comps, ext_rows, col_count), jnp.float32),
         ],
-    )(state, diffusion, forcing, above, below, keep, got_scale)
+    )(state, diffusion, forcing, above, below, keep)
     fine_end = fine_end.reshape(coarse_points.shape)
 
     shift = fine_end - coarse_decay * coarse_points
@@ -123,7 +121,9 @@
     shift0 = jnp.where(at_anchor, coarse_decay[0] * coarse_points[0] + shift[0], shift[0])
     comp_shift = scale[1] * shift0 + shift[1]
 
-    got_shift = lax.all_to_all(to_tiles(comp_shift), "tm", split_axis=0, concat_axis=0, tiled=True)
+    both = jnp.stack([to_tiles(comp_scale), to_tiles(comp_shift)])
+    got = lax.all_to_all(both, "tm", split_axis=1, concat_axis=1, tiled=True)
+    got_scale, got_shift = got[0], got[1]
     per_src = got_shift.shape[0] // tm_count
     tile_shape = (tm_count, per_src, 8, 128)
     prefix = pl.pallas_call(

time: 98.5 us -> 91.6 us (0.930)
  starting transfers between devices: 18.7 us -> 5.37 us
  blocking collectives: 42 us -> 49.7 us
    all_to_all x1 -> x0, starting transfers between devices: 12.6 us -> none  [per_device_body(): lax.all_to_all(scale_tiles, 'tm', split_axis=0, concat_axis=0, tiled=True)]
    ppermute x1, waiting for transfers between devices: 11.8 us -> 4.86 us  [per_device_body(): below = lax.ppermute(dn_rim, 'space', backward)]
    all_to_all x1, blocking collectives: 24.2 us -> 31 us  [per_device_body(): got = lax.all_to_all(both, 'tm', split_axis=1, concat_axis=1, tiled=True)]
    ppermute x1, waiting for transfers between devices: 0.01 us -> 6.36 us  [per_device_body(): above = lax.ppermute(up_rim, 'space', forward)]
  transfers between devices with their start and end apart: 3 -> 2, of which waited for: 1 -> 2; matrix products, arithmetic and copies ran while one was open for 2% -> 2% of each run, Pallas kernels for 0% -> 0%
where the time goes in v3:
time: 91.6 us; the launch traced here: 91.3 us
  blocking collectives  49.7 us (54%)
  Pallas kernels  18.3 us (20%)
  waiting for transfers between devices  11.2 us (12%)
  starting transfers between devices  5.37 us (6%)
  other arithmetic  3.72 us (4%)
  local copies, waits for them, and re-layouts  2.86 us (3%)
    all_to_all x1, blocking collectives, per_device_body(): got = lax.all_to_all(both, 'tm', split_axis=1, concat_axis=1, tiled=True)  31 us
    all_to_all x1, blocking collectives, per_device_body(): lax.all_to_all(prefix.reshape(tm_count * per_src, 8, 128), 'tm', split_ax...  18.8 us
    pallas_call x1, Pallas kernels, per_device_body(): pl.pallas_call(fine_kernel, out_shape=jax.ShapeDtypeStruct((slots * comps...  16.4 us
    ppermute x1, waiting for transfers between devices, per_device_body(): above = lax.ppermute(up_rim, 'space', forward)  6.36 us
    ppermute x1, waiting for transfers between devices, per_device_body(): below = lax.ppermute(dn_rim, 'space', backward)  4.86 us
    ppermute x1, starting transfers between devices, per_device_body(): above = lax.ppermute(up_rim, 'space', forward)  4.09 us
    pallas_call x1, Pallas kernels, per_device_body(): pl.pallas_call(scan_kernel, out_shape=jax.ShapeDtypeStruct(tile_shape, jn...  1.86 us
  transfers between devices with their start and end apart: 2, of which 2 were waited for; matrix products, arithmetic and copies ran while one was open for 2% of the time, Pallas kernels for 0%

profile of v3, /device:TPU:1, one launch (start us, length us, event | category | flops | bytes accessed | tf_op | source)
XLA Modules:
  0.0 91.3 jit_solution(13610147827810659862)
XLA Ops:
  0.0 1.0 %slice_bitcast_fusion.2 = (f32[1,16,1024]{2,1,0:T(8,128)S(1)}, f32[1,16,1024]{2,1,0:T(8,128)S(1)}) fusion(f32[32,1024]{1,0:T(8,128)} %dif_ref.1), kind=kLoop, calls=%fused_computation.15 | loop fusion | bytes 262144 | tf_op jit(solution)/shard_map/broadcast_in_dim | solution.py:95
  1.0 0.1 copy-done.3
  1.0 0.2 copy-done
  1.3 0.0 copy-start.2
  1.3 4.1 %collective-permute-start = (f32[7,16,1024]{2,1,0:T(8,128)S(1)}, f32[7,16,1024]{2,1,0:T(8,128)S(1)}, u32[]{:S(2)}, u32[]{:S(2)}) collective-permute-start(f32[7,16,1024]{2,1,0:T(8,128)S(1)} %pad_maximum_fusion.2), channel_id=1, source_target_pairs={{0,1},{1,2},{2,3},{4,5},{5,6},{6,7},{8,9},{9,10},{10,11},{12,13},{... | collective-permute-start | bytes 1376264 | tf_op jit(solution)/shard_map/ppermute | solution.py:99
  5.4 0.8 pad_maximum_fusion.3
  6.2 1.3 %collective-permute-start.1 = (f32[7,16,1024]{2,1,0:T(8,128)}, f32[7,16,1024]{2,1,0:T(8,128)S(1)}, u32[]{:S(2)}, u32[]{:S(2)}) collective-permute-start(f32[7,16,1024]{2,1,0:T(8,128)} %pad_maximum_fusion.3), channel_id=1, source_target_pairs={{1,0},{2,1},{3,2},{5,4},{6,5},{7,6},{9,8},{10,9},{11,10},{13,12},{... | collective-permute-start | bytes 1376264 | tf_op jit(solution)/shard_map/ppermute | solution.py:100
  7.5 0.6 fusion.6.keep_ref
  8.1 0.0 copy-done.2
  8.1 0.1 slice_select_fusion
  8.2 0.0 copy-start.1
  8.2 6.4 %collective-permute-done.up_ref = f32[7,16,1024]{2,1,0:T(8,128)S(1)} collective-permute-done((f32[7,16,1024]{2,1,0:T(8,128)S(1)}, f32[7,16,1024]{2,1,0:T(8,128)S(1)}, u32[]{:S(2)}, u32[]{:S(2)}) %collective-permute-start) | collective-permute-done | bytes 458784 | tf_op jit(solution)/shard_map/ppermute | solution.py:99
  14.5 4.9 %collective-permute-done.1.dn_ref = f32[7,16,1024]{2,1,0:T(8,128)S(1)} collective-permute-done((f32[7,16,1024]{2,1,0:T(8,128)}, f32[7,16,1024]{2,1,0:T(8,128)S(1)}, u32[]{:S(2)}, u32[]{:S(2)}) %collective-permute-start.1) | collective-permute-done | bytes 458784 | tf_op jit(solution)/shard_map/ppermute | solution.py:100
  19.4 0.0 copy-done.4
  19.4 0.8 copy-done.5
  20.2 16.4 %shard_map.46 = f32[4,32,1024]{2,1,0:T(8,128)} custom-call(f32[4,32,1024]{2,1,0:T(8,128)} %bitcast.31, f32[32,1024]{1,0:T(8,128)} %dif_ref.1, f32[2,32,1024]{2,1,0:T(8,128)} %frc_ref.1, f32[7,16,1024]{2,1,0:T(8,128)} %copy-done.4, f32[7,16,1024]{2,1,0:T(8,128)} %copy-done.5, f32[64,1]{1,0:T(8,128)} %fusion.6.keep_ref), custom_call_target="tpu_custom_call" | custom-call | tf_op jit(solution)/shard_map/pallas_call | solution.py:106
  36.6 1.1 %multiply_subtract_fusion = f32[2,2,32,1024]{3,2,1,0:T(8,128)S(1)} fusion(f32[2,2,32,1024]{3,2,1,0:T(8,128)} %bitcast.34, f32[2,2,32,1024]{3,2,1,0:T(8,128)S(1)} %copy-done.2, f32[2,2,32,1024]{3,2,1,0:T(8,128)S(1)} %copy-done.1), kind=kLoop, calls=%fused_computation.2 | loop fusion | flops 262144 | bytes 2097152 | tf_op jit(solution)/shard_map/sub | solution.py:119
  37.8 0.1 fusion.10
  37.9 31.0 %all_to_all.10 = f32[2,64,8,128]{3,2,0,1:T(8,128)S(1)} all-to-all(f32[2,64,8,128]{3,2,0,1:T(8,128)S(1)} %pad_maximum_fusion), channel_id=1, replica_groups=mesh['tm'=64,'space'=4] {'tm'}, dimensions={1} | all-to-all | bytes 1048576 | tf_op jit(solution)/shard_map/all_to_all | solution.py:125
  68.9 0.8 slice_bitcast_fusion
  69.7 1.9 %shard_map.47 = f32[64,1,8,128]{3,2,1,0:T(8,128)} custom-call(f32[64,1,8,128]{3,2,1,0:T(8,128)} %get-tuple-element.8.a_ref, f32[64,1,8,128]{3,2,1,0:T(8,128)} %get-tuple-element.7.b_ref), custom_call_target="tpu_custom_call" | custom-call | tf_op jit(solution)/shard_map/pallas_call | solution.py:129
  71.6 18.8 %all_to_all.11 = f32[64,8,128]{2,1,0:T(8,128)S(1)} all-to-all(f32[64,8,128]{2,1,0:T(8,128)} %bitcast.36), channel_id=1, replica_groups=mesh['tm'=64,'space'=4] {'tm'}, dimensions={0} | all-to-all | bytes 524288 | tf_op jit(solution)/shard_map/all_to_all | solution.py:133
  90.3 0.1 multiply_add_fusion
  90.4 0.8 pad_maximum_fusion.1
  (10 shorter events, 0.2 us)
Async XLA Ops:
  0.0 1.0 %copy-start.3 = (f32[2,32,1024]{2,1,0:T(8,128)S(1)}, f32[2,32,1024]{2,1,0:T(8,128)}, u32[]{:S(2)}) copy-start(f32[2,32,1024]{2,1,0:T(8,128)} %frc_ref.1) | copy-start | bytes 786436
  0.0 1.2 %copy-start = (f32[2,2,32,1024]{3,2,1,0:T(8,128)S(1)}, f32[2,2,32,1024]{3,2,1,0:T(8,128)}, u32[]{:S(2)}) copy-start(f32[2,2,32,1024]{3,2,1,0:T(8,128)} %param.4) | copy-start | bytes 1572868
  1.3 6.8 %copy-start.2 = (f32[2,2,32,1024]{3,2,1,0:T(8,128)S(1)}, f32[2,2,32,1024]{3,2,1,0:T(8,128)}, u32[]{:S(2)}) copy-start(f32[2,2,32,1024]{3,2,1,0:T(8,128)} %param.5) | copy-start | bytes 1572868
  1.3 13.3 %collective-permute-start = (f32[7,16,1024]{2,1,0:T(8,128)S(1)}, f32[7,16,1024]{2,1,0:T(8,128)S(1)}, u32[]{:S(2)}, u32[]{:S(2)}) collective-permute-start(f32[7,16,1024]{2,1,0:T(8,128)S(1)} %pad_maximum_fusion.2), channel_id=1, source_target_pairs={{0,1},{1,2},{2,3},{4,5},{5,6},{6,7},{8,9},{9,10},{10,11},{12,13},{... | collective-permute-start | bytes 1376264 | tf_op jit(solution)/shard_map/ppermute | solution.py:99
  6.2 13.2 %collective-permute-start.1 = (f32[7,16,1024]{2,1,0:T(8,128)}, f32[7,16,1024]{2,1,0:T(8,128)S(1)}, u32[]{:S(2)}, u32[]{:S(2)}) collective-permute-start(f32[7,16,1024]{2,1,0:T(8,128)} %pad_maximum_fusion.3), channel_id=1, source_target_pairs={{1,0},{2,1},{3,2},{5,4},{6,5},{7,6},{9,8},{10,9},{11,10},{13,12},{... | collective-permute-start | bytes 1376264 | tf_op jit(solution)/shard_map/ppermute | solution.py:100
  8.2 28.4 %copy-start.1 = (f32[2,2,32,1024]{3,2,1,0:T(8,128)S(1)}, f32[2,2,32,1024]{3,2,1,0:T(8,128)}, u32[]{:S(2)}) copy-start(f32[2,2,32,1024]{3,2,1,0:T(8,128)} %param.4) | copy-start | bytes 1572868
  14.5 4.9 %copy-start.4 = (f32[7,16,1024]{2,1,0:T(8,128)}, f32[7,16,1024]{2,1,0:T(8,128)S(1)}, u32[]{:S(2)}) copy-start(f32[7,16,1024]{2,1,0:T(8,128)S(1)} %collective-permute-done.up_ref) | copy-start | bytes 1376260
  19.4 0.8 copy-start.5

commit v4 on v3

--- a/solution.py
+++ b/solution.py
@@ -65,6 +65,19 @@
         x = a_ref[s] * x + b_ref[s]
 
 
+def group_kernel(a_ref, b_ref, pa_ref, pb_ref, ga_ref, gb_ref):
+    pa = jnp.ones(a_ref.shape[1:], jnp.float32)
+    pb = jnp.zeros(a_ref.shape[1:], jnp.float32)
+    for s in range(a_ref.shape[0]):
+        pa_ref[s] = pa
+        pb_ref[s] = pb
+        a = a_ref[s]
+        pa = a * pa
+        pb = a * pb + b_ref[s]
+    ga_ref[...] = pa
+    gb_ref[...] = pb
+
+
 def to_tiles(block):
     rows, cols = block.shape[-2] * block.shape[-3], block.shape[-1]
     flat = block.reshape(rows // 8, 8, cols // 128, 128)
@@ -80,10 +93,9 @@
 def per_device_body(coarse_points, coarse_decay, diffusion, forcing):
     slots, comps, row_count, col_count = coarse_points.shape
     space_count = lax.axis_size("space")
-    tm_count = lax.axis_size("tm")
     me = lax.axis_index("space")
 
-    at_anchor = lax.axis_index("tm") == 0
+    at_anchor = (lax.axis_index("tz") == 0) & (lax.axis_index("tq") == 0)
     scale0 = jnp.where(at_anchor, 0.0, coarse_decay[0])
     comp_scale = coarse_decay[1] * scale0
 
@@ -121,17 +133,31 @@
     shift0 = jnp.where(at_anchor, coarse_decay[0] * coarse_points[0] + shift[0], shift[0])
     comp_shift = scale[1] * shift0 + shift[1]
 
+    q_count = lax.axis_size("tq")
+    z_count = lax.axis_size("tz")
     both = jnp.stack([to_tiles(comp_scale), to_tiles(comp_shift)])
-    got = lax.all_to_all(both, "tm", split_axis=1, concat_axis=1, tiled=True)
-    got_scale, got_shift = got[0], got[1]
-    per_src = got_shift.shape[0] // tm_count
-    tile_shape = (tm_count, per_src, 8, 128)
-    prefix = pl.pallas_call(
+    tiles = both.shape[1]
+    c1 = tiles // q_count
+    c2 = c1 // z_count
+    got = lax.all_to_all(both, "tq", split_axis=1, concat_axis=1, tiled=True)
+    got = got.reshape(2, q_count, c1, 8, 128)
+    shape1 = jax.ShapeDtypeStruct((q_count, c1, 8, 128), jnp.float32)
+    shape_g = jax.ShapeDtypeStruct((c1, 8, 128), jnp.float32)
+    pa, pb, ga, gb = pl.pallas_call(group_kernel, out_shape=(shape1, shape1, shape_g, shape_g))(
+        got[0], got[1]
+    )
+    groups = lax.all_to_all(jnp.stack([ga, gb]), "tz", split_axis=1, concat_axis=1, tiled=True)
+    groups = groups.reshape(2, z_count, c2, 8, 128)
+    group_in = pl.pallas_call(
         scan_kernel,
-        out_shape=jax.ShapeDtypeStruct(tile_shape, jnp.float32),
-    )(got_scale.reshape(tile_shape), got_shift.reshape(tile_shape))
+        out_shape=jax.ShapeDtypeStruct((z_count, c2, 8, 128), jnp.float32),
+    )(groups[0], groups[1])
+    group_in = lax.all_to_all(
+        group_in.reshape(c1, 8, 128), "tz", split_axis=0, concat_axis=0, tiled=True
+    )
+    prefix = pa * group_in[None] + pb
     back = lax.all_to_all(
-        prefix.reshape(tm_count * per_src, 8, 128), "tm", split_axis=0, concat_axis=0, tiled=True
+        prefix.reshape(tiles, 8, 128), "tq", split_axis=0, concat_axis=0, tiled=True
     )
     entering = from_tiles(back, (comps, row_count, col_count))
 
@@ -141,9 +167,14 @@
 
 
 def solution(mesh):
+    tm_count = mesh.shape["tm"]
+    q_count = 8 if tm_count >= 16 and tm_count % 8 == 0 else 2
+    grid = mesh.devices.reshape(tm_count // q_count, q_count, mesh.shape["space"])
+    mesh = jax.sharding.Mesh(grid, ("tz", "tq", "space"))
+    time_axes = ("tz", "tq")
     placed = (
-        P("tm", None, "space", None),
-        P("tm", None, "space", None),
+        P(time_axes, None, "space", None),
+        P(time_axes, None, "space", None),
         P("space", None),
         P(None, "space", None),
     )
@@ -151,6 +182,6 @@
         per_device_body,
         mesh=mesh,
         in_specs=placed,
-        out_specs=P("tm", None, "space", None),
+        out_specs=P(time_axes, None, "space", None),
         check_vma=False,
     )

time: 91.6 us -> 98.3 us (1.073)
  blocking collectives: 49.7 us -> 53.3 us
  Pallas kernels: 18.3 us -> 19.7 us
    all_to_all x2 -> x4, blocking collectives: 49.7 us -> 53.3 us  [the longest x1 15.4 us: per_device_body(): got = lax.all_to_all(both, 'tq', split_axis=1, concat_axis=1, tiled=True)]
    pallas_call x1 -> x2, Pallas kernels: 1.86 us -> 3.26 us  [the longest x1 1.87 us: per_device_body(): pl.pallas_call(group_kernel, out_shape=(shape1, shape1, shape_g, shape_g))]
where the time goes in v4:
time: 98.3 us; the launch traced here: 97.8 us
  blocking collectives  53.3 us (54%)
  Pallas kernels  19.7 us (20%)
  waiting for transfers between devices  11.2 us (11%)
  starting transfers between devices  5.37 us (5%)
  other arithmetic  4.53 us (5%)
  local copies, waits for them, and re-layouts  3.48 us (4%)
    pallas_call x1, Pallas kernels, per_device_body(): pl.pallas_call(fine_kernel, out_shape=jax.ShapeDtypeStruct((slots * comps...  16.4 us
    all_to_all x1, blocking collectives, per_device_body(): got = lax.all_to_all(both, 'tq', split_axis=1, concat_axis=1, tiled=True)  15.4 us
    all_to_all x1, blocking collectives, per_device_body(): lax.all_to_all(jnp.stack([ga, gb]), 'tz', split_axis=1, concat_axis=1, ti...  15.3 us
    all_to_all x1, blocking collectives, per_device_body(): lax.all_to_all(prefix.reshape(tiles, 8, 128), 'tq', split_axis=0, concat_...  12.4 us
    all_to_all x1, blocking collectives, per_device_body(): lax.all_to_all(group_in.reshape(c1, 8, 128), 'tz', split_axis=0, concat_a...  10.2 us
    ppermute x1, waiting for transfers between devices, per_device_body(): above = lax.ppermute(up_rim, 'space', forward)  6.35 us
    ppermute x1, waiting for transfers between devices, per_device_body(): below = lax.ppermute(dn_rim, 'space', backward)  4.86 us
    ppermute x1, starting transfers between devices, per_device_body(): above = lax.ppermute(up_rim, 'space', forward)  4.09 us
  transfers between devices with their start and end apart: 2, of which 2 were waited for; matrix products, arithmetic and copies ran while one was open for 2% of the time, Pallas kernels for 0%

profile of v4, /device:TPU:1, one launch (start us, length us, event | category | flops | bytes accessed | tf_op | source)
XLA Modules:
  0.0 97.8 jit_solution(9910229822058177485)
XLA Ops:
  0.0 1.0 slice_bitcast_fusion
  1.0 0.2 copy-done
  1.3 4.1 %collective-permute-start = (f32[7,16,1024]{2,1,0:T(8,128)S(1)}, f32[7,16,1024]{2,1,0:T(8,128)S(1)}, u32[]{:S(2)}, u32[]{:S(2)}) collective-permute-start(f32[7,16,1024]{2,1,0:T(8,128)S(1)} %pad_maximum_fusion.2), channel_id=1, source_target_pairs={{0,1},{1,2},{2,3},{4,5},{5,6},{6,7},{8,9},{9,10},{10,11},{12,13},{... | collective-permute-start | bytes 1376264 | tf_op jit(solution)/shard_map/ppermute | solution.py:111
  5.4 0.8 pad_maximum_fusion.3
  6.2 1.3 %collective-permute-start.1 = (f32[7,16,1024]{2,1,0:T(8,128)}, f32[7,16,1024]{2,1,0:T(8,128)S(1)}, u32[]{:S(2)}, u32[]{:S(2)}) collective-permute-start(f32[7,16,1024]{2,1,0:T(8,128)} %pad_maximum_fusion.3), channel_id=1, source_target_pairs={{1,0},{2,1},{3,2},{5,4},{6,5},{7,6},{9,8},{10,9},{11,10},{13,12},{... | collective-permute-start | bytes 1376264 | tf_op jit(solution)/shard_map/ppermute | solution.py:112
  7.5 0.6 fusion.6.keep_ref
  8.1 0.1 slice_select_fusion
  8.2 6.4 %collective-permute-done.up_ref = f32[7,16,1024]{2,1,0:T(8,128)S(1)} collective-permute-done((f32[7,16,1024]{2,1,0:T(8,128)S(1)}, f32[7,16,1024]{2,1,0:T(8,128)S(1)}, u32[]{:S(2)}, u32[]{:S(2)}) %collective-permute-start) | collective-permute-done | bytes 458784 | tf_op jit(solution)/shard_map/ppermute | solution.py:111
  14.5 4.9 %collective-permute-done.1.dn_ref = f32[7,16,1024]{2,1,0:T(8,128)S(1)} collective-permute-done((f32[7,16,1024]{2,1,0:T(8,128)}, f32[7,16,1024]{2,1,0:T(8,128)S(1)}, u32[]{:S(2)}, u32[]{:S(2)}) %collective-permute-start.1) | collective-permute-done | bytes 458784 | tf_op jit(solution)/shard_map/ppermute | solution.py:112
  19.4 0.8 copy-done.5
  20.2 16.4 %shard_map.46 = f32[4,32,1024]{2,1,0:T(8,128)} custom-call(f32[4,32,1024]{2,1,0:T(8,128)} %bitcast.36, f32[32,1024]{1,0:T(8,128)} %dif_ref.1, f32[2,32,1024]{2,1,0:T(8,128)} %frc_ref.1, f32[7,16,1024]{2,1,0:T(8,128)} %copy-done.4, f32[7,16,1024]{2,1,0:T(8,128)} %copy-done.5, f32[64,1]{1,0:T(8,128)} %fusion.6.keep_ref), custom_call_target="tpu_custom_call" | custom-call | tf_op jit(solution)/shard_map/pallas_call | solution.py:118
  36.6 1.1 %multiply_subtract_fusion = f32[2,2,32,1024]{3,2,1,0:T(8,128)S(1)} fusion(f32[2,2,32,1024]{3,2,1,0:T(8,128)} %bitcast.39, f32[2,2,32,1024]{3,2,1,0:T(8,128)S(1)} %copy-done.2, f32[2,2,32,1024]{3,2,1,0:T(8,128)S(1)} %copy-done.1), kind=kLoop, calls=%fused_computation.2 | loop fusion | flops 262144 | bytes 2097152 | tf_op jit(solution)/shard_map/sub | solution.py:131
  37.8 0.1 fusion.11
  37.9 15.4 %all_to_all.20 = f32[2,64,8,128]{3,2,0,1:T(8,128)S(1)} all-to-all(f32[2,64,8,128]{3,2,0,1:T(8,128)S(1)} %pad_maximum_fusion), channel_id=1, replica_groups=mesh['tz'=8,'tq'=8,'space'=4] {'tq'}, dimensions={1} | all-to-all | bytes 1048576 | tf_op jit(solution)/shard_map/all_to_all | solution.py:142
  53.3 0.8 fusion.8
  54.1 1.9 %shard_map.47 = (f32[8,8,8,128]{3,2,1,0:T(8,128)}, f32[8,8,8,128]{3,2,1,0:T(8,128)}, f32[8,8,128]{2,1,0:T(8,128)}, f32[8,8,128]{2,1,0:T(8,128)}) custom-call(f32[8,8,8,128]{3,2,1,0:T(8,128)} %bitcast.43, f32[8,8,8,128]{3,2,1,0:T(8,128)} %bitcast.42), custom_call_target="tpu_custom_call" | custom-call | tf_op jit(solution)/shard_map/pallas_call | solution.py:146
  56.0 0.8 pad_maximum_fusion.4
  56.8 15.3 %all_to_all.21 = f32[2,8,8,128]{3,2,0,1:T(8,128)S(1)} all-to-all(f32[2,8,8,128]{3,2,0,1:T(8,128)S(1)} %copy.10), channel_id=1, replica_groups=mesh['tz'=8,'tq'=8,'space'=4] {'tz'}, dimensions={1} | all-to-all | bytes 131072 | tf_op jit(solution)/shard_map/all_to_all | solution.py:149
  72.2 0.6 slice_bitcast_fusion.2
  72.8 1.4 %shard_map.48 = f32[8,1,8,128]{3,2,1,0:T(8,128)} custom-call(f32[8,1,8,128]{3,2,1,0:T(8,128)} %get-tuple-element.31.a_ref, f32[8,1,8,128]{3,2,1,0:T(8,128)} %get-tuple-element.30.b_ref), custom_call_target="tpu_custom_call" | custom-call | tf_op jit(solution)/shard_map/pallas_call | solution.py:151
  74.2 10.2 %all_to_all.22 = f32[8,8,128]{2,1,0:T(8,128)S(1)} all-to-all(f32[8,8,128]{2,1,0:T(8,128)} %bitcast.50), channel_id=1, replica_groups=mesh['tz'=8,'tq'=8,'space'=4] {'tz'}, dimensions={0} | all-to-all | bytes 65536 | tf_op jit(solution)/shard_map/all_to_all | solution.py:155
  84.4 12.4 %all_to_all.23 = f32[64,8,128]{2,1,0:T(8,128)S(1)} all-to-all(f32[64,8,128]{2,1,0:T(8,128)S(1)} %bitcast.41), channel_id=1, replica_groups=mesh['tz'=8,'tq'=8,'space'=4] {'tq'}, dimensions={0} | all-to-all | bytes 524288 | tf_op jit(solution)/shard_map/all_to_all | solution.py:159
  96.8 0.1 multiply_add_fusion
  96.9 0.8 pad_maximum_fusion.1
  (21 shorter events, 0.3 us)
Async XLA Ops:
  0.0 1.0 %copy-start.3 = (f32[2,32,1024]{2,1,0:T(8,128)S(1)}, f32[2,32,1024]{2,1,0:T(8,128)}, u32[]{:S(2)}) copy-start(f32[2,32,1024]{2,1,0:T(8,128)} %frc_ref.1) | copy-start | bytes 786436
  0.0 1.2 %copy-start = (f32[2,2,32,1024]{3,2,1,0:T(8,128)S(1)}, f32[2,2,32,1024]{3,2,1,0:T(8,128)}, u32[]{:S(2)}) copy-start(f32[2,2,32,1024]{3,2,1,0:T(8,128)} %param.4) | copy-start | bytes 1572868
  1.3 6.8 %copy-start.2 = (f32[2,2,32,1024]{3,2,1,0:T(8,128)S(1)}, f32[2,2,32,1024]{3,2,1,0:T(8,128)}, u32[]{:S(2)}) copy-start(f32[2,2,32,1024]{3,2,1,0:T(8,128)} %param.5) | copy-start | bytes 1572868
  1.3 13.3 %collective-permute-start = (f32[7,16,1024]{2,1,0:T(8,128)S(1)}, f32[7,16,1024]{2,1,0:T(8,128)S(1)}, u32[]{:S(2)}, u32[]{:S(2)}) collective-permute-start(f32[7,16,1024]{2,1,0:T(8,128)S(1)} %pad_maximum_fusion.2), channel_id=1, source_target_pairs={{0,1},{1,2},{2,3},{4,5},{5,6},{6,7},{8,9},{9,10},{10,11},{12,13},{... | collective-permute-start | bytes 1376264 | tf_op jit(solution)/shard_map/ppermute | solution.py:111
  6.2 13.2 %collective-permute-start.1 = (f32[7,16,1024]{2,1,0:T(8,128)}, f32[7,16,1024]{2,1,0:T(8,128)S(1)}, u32[]{:S(2)}, u32[]{:S(2)}) collective-permute-start(f32[7,16,1024]{2,1,0:T(8,128)} %pad_maximum_fusion.3), channel_id=1, source_target_pairs={{1,0},{2,1},{3,2},{5,4},{6,5},{7,6},{9,8},{10,9},{11,10},{13,12},{... | collective-permute-start | bytes 1376264 | tf_op jit(solution)/shard_map/ppermute | solution.py:112
  8.2 28.4 %copy-start.1 = (f32[2,2,32,1024]{3,2,1,0:T(8,128)S(1)}, f32[2,2,32,1024]{3,2,1,0:T(8,128)}, u32[]{:S(2)}) copy-start(f32[2,2,32,1024]{3,2,1,0:T(8,128)} %param.4) | copy-start | bytes 1572868
  14.5 4.9 %copy-start.4 = (f32[7,16,1024]{2,1,0:T(8,128)}, f32[7,16,1024]{2,1,0:T(8,128)S(1)}, u32[]{:S(2)}) copy-start(f32[7,16,1024]{2,1,0:T(8,128)S(1)} %collective-permute-done.up_ref) | copy-start | bytes 1376260
  19.4 0.8 copy-start.5
  56.8 27.6 %copy-start.6 = (f32[8,8,8,128]{3,2,1,0:T(8,128)S(1)}, f32[8,8,8,128]{3,2,1,0:T(8,128)}, u32[]{:S(2)}) copy-start(f32[8,8,8,128]{3,2,1,0:T(8,128)} %get-tuple-element.9) | copy-start | bytes 786436
  56.8 27.6 %copy-start.7 = (f32[8,8,8,128]{3,2,1,0:T(8,128)S(1)}, f32[8,8,8,128]{3,2,1,0:T(8,128)}, u32[]{:S(2)}) copy-start(f32[8,8,8,128]{3,2,1,0:T(8,128)} %get-tuple-element.12) | copy-start | bytes 786436

commit v5 on v3

--- a/solution.py
+++ b/solution.py
@@ -58,11 +58,61 @@
     out_ref[...] = buf[:, HALO:HALO + own, :]
 
 
-def scan_kernel(a_ref, b_ref, x_ref):
-    x = jnp.zeros(a_ref.shape[1:], jnp.float32)
-    for s in range(a_ref.shape[0]):
-        x_ref[s] = x
-        x = a_ref[s] * x + b_ref[s]
+def exchange_kernel(send_ref, out_ref, recv, xbuf, back, s1, r1, s2, r2):
+    n = send_ref.shape[0]
+    me = lax.axis_index("tm")
+    sp = lax.axis_index("space")
+    mesh_id = pl.DeviceIdType.MESH
+
+    def outgoing(d, src, dst, ssem, rsem):
+        return pltpu.make_async_remote_copy(
+            src_ref=src.at[d], dst_ref=dst.at[me], send_sem=ssem.at[d], recv_sem=rsem.at[me],
+            device_id=(d, sp), device_id_type=mesh_id,
+        )
+
+    def incoming(e, src, dst, ssem, rsem):
+        return pltpu.make_async_remote_copy(
+            src_ref=src.at[e], dst_ref=dst.at[e], send_sem=ssem.at[e], recv_sem=rsem.at[e],
+            device_id=(e, sp), device_id_type=mesh_id,
+        )
+
+    def peer(k):
+        return lax.rem(me + k, n)
+
+    def start1(k, carry):
+        outgoing(peer(k), send_ref, recv, s1, r1).start()
+        return carry
+
+    lax.fori_loop(1, n, start1, 0)
+    recv[me] = send_ref[me]
+
+    def wait1(k, carry):
+        outgoing(peer(k), send_ref, recv, s1, r1).wait_send()
+        incoming(peer(k), send_ref, recv, s1, r1).wait_recv()
+        return carry
+
+    lax.fori_loop(1, n, wait1, 0)
+
+    def scan_step(s, x):
+        xbuf[s] = x
+        return recv[s, :, 0] * x + recv[s, :, 1]
+
+    lax.fori_loop(0, n, scan_step, jnp.zeros(xbuf.shape[1:], jnp.float32))
+
+    def start2(k, carry):
+        outgoing(peer(k), xbuf, back, s2, r2).start()
+        return carry
+
+    lax.fori_loop(1, n, start2, 0)
+    back[me] = xbuf[me]
+
+    def wait2(k, carry):
+        outgoing(peer(k), xbuf, back, s2, r2).wait_send()
+        incoming(peer(k), xbuf, back, s2, r2).wait_recv()
+        return carry
+
+    lax.fori_loop(1, n, wait2, 0)
+    out_ref[...] = back[...]
 
 
 def to_tiles(block):
@@ -121,18 +171,29 @@
     shift0 = jnp.where(at_anchor, coarse_decay[0] * coarse_points[0] + shift[0], shift[0])
     comp_shift = scale[1] * shift0 + shift[1]
 
-    both = jnp.stack([to_tiles(comp_scale), to_tiles(comp_shift)])
-    got = lax.all_to_all(both, "tm", split_axis=1, concat_axis=1, tiled=True)
-    got_scale, got_shift = got[0], got[1]
-    per_src = got_shift.shape[0] // tm_count
-    tile_shape = (tm_count, per_src, 8, 128)
-    prefix = pl.pallas_call(
-        scan_kernel,
-        out_shape=jax.ShapeDtypeStruct(tile_shape, jnp.float32),
-    )(got_scale.reshape(tile_shape), got_shift.reshape(tile_shape))
-    back = lax.all_to_all(
-        prefix.reshape(tm_count * per_src, 8, 128), "tm", split_axis=0, concat_axis=0, tiled=True
-    )
+    both = jnp.stack([to_tiles(comp_scale), to_tiles(comp_shift)], axis=1)
+    tiles = both.shape[0]
+    chunk = tiles // tm_count
+    both = both.reshape(tm_count, chunk, 2, 8, 128)
+    x_shape = (tm_count, chunk, 8, 128)
+    vmem = pl.BlockSpec(memory_space=pltpu.VMEM)
+    back = pl.pallas_call(
+        exchange_kernel,
+        out_shape=jax.ShapeDtypeStruct(x_shape, jnp.float32),
+        in_specs=[vmem],
+        out_specs=vmem,
+        scratch_shapes=[
+            pltpu.VMEM(both.shape, jnp.float32),
+            pltpu.VMEM(x_shape, jnp.float32),
+            pltpu.VMEM(x_shape, jnp.float32),
+            pltpu.SemaphoreType.DMA((tm_count,)),
+            pltpu.SemaphoreType.DMA((tm_count,)),
+            pltpu.SemaphoreType.DMA((tm_count,)),
+            pltpu.SemaphoreType.DMA((tm_count,)),
+        ],
+        compiler_params=pltpu.CompilerParams(has_side_effects=True),
+    )(both)
+    back = back.reshape(tiles, 8, 128)
     entering = from_tiles(back, (comps, row_count, col_count))
 
     first = scale0 * entering + shift0

time: 91.6 us -> 87.4 us (0.954)
  blocking collectives: 49.7 us -> 0 us
  Pallas kernels: 18.3 us -> 62.9 us
  other arithmetic: 3.72 us -> 5.48 us
    all_to_all x2 -> x0, blocking collectives: 49.7 us -> none  [the longest x1 31 us: per_device_body(): got = lax.all_to_all(both, 'tm', split_axis=1, concat_axis=1, tiled=True)]
    pallas_call x1, Pallas kernels: 1.86 us -> 46.4 us  [per_device_body(): pl.pallas_call(exchange_kernel, out_shape=jax.ShapeDtypeStruct(x_shape, j...]
    add x1, other arithmetic: 0.11 us -> 1.06 us  [per_device_body(): second = scale[1] * first + shift[1]]
where the time goes in v5:
time: 87.4 us; the launch traced here: 87.1 us
  Pallas kernels  62.9 us (72%)
  waiting for transfers between devices  11.2 us (13%)
  other arithmetic  5.48 us (6%)
  starting transfers between devices  5.37 us (6%)
  local copies, waits for them, and re-layouts  2.04 us (2%)
    pallas_call x1, Pallas kernels, per_device_body(): pl.pallas_call(exchange_kernel, out_shape=jax.ShapeDtypeStruct(x_shape, j...  46.4 us
    pallas_call x1, Pallas kernels, per_device_body(): pl.pallas_call(fine_kernel, out_shape=jax.ShapeDtypeStruct((slots * comps...  16.4 us
    ppermute x1, waiting for transfers between devices, per_device_body(): above = lax.ppermute(up_rim, 'space', forward)  6.34 us
    ppermute x1, waiting for transfers between devices, per_device_body(): below = lax.ppermute(dn_rim, 'space', backward)  4.86 us
    ppermute x1, starting transfers between devices, per_device_body(): above = lax.ppermute(up_rim, 'space', forward)  4.09 us
  transfers between devices with their start and end apart: 2, of which 2 were waited for; matrix products, arithmetic and copies ran while one was open for 2% of the time, Pallas kernels for 0%

profile of v5, /device:TPU:1, one launch (start us, length us, event | category | flops | bytes accessed | tf_op | source)
XLA Modules:
  0.0 87.1 jit_solution(5563060116254568823)
XLA Ops:
  0.0 0.0 copy-start.3
  0.0 1.0 %slice_bitcast_fusion = (f32[1,16,1024]{2,1,0:T(8,128)S(1)}, f32[1,16,1024]{2,1,0:T(8,128)S(1)}) fusion(f32[32,1024]{1,0:T(8,128)} %dif_ref.1), kind=kLoop, calls=%fused_computation.13 | loop fusion | bytes 262144 | tf_op jit(solution)/shard_map/broadcast_in_dim | solution.py:145
  1.0 0.1 copy-done.3
  1.0 0.2 copy-done
  1.3 0.0 copy-start.2
  1.3 4.1 %collective-permute-start = (f32[7,16,1024]{2,1,0:T(8,128)S(1)}, f32[7,16,1024]{2,1,0:T(8,128)S(1)}, u32[]{:S(2)}, u32[]{:S(2)}) collective-permute-start(f32[7,16,1024]{2,1,0:T(8,128)S(1)} %pad_maximum_fusion.1), channel_id=1, source_target_pairs={{0,1},{1,2},{2,3},{4,5},{5,6},{6,7},{8,9},{9,10},{10,11},{12,13},{... | collective-permute-start | bytes 1376264 | tf_op jit(solution)/shard_map/ppermute | solution.py:149
  5.4 0.8 pad_maximum_fusion.2
  6.2 1.3 %collective-permute-start.1 = (f32[7,16,1024]{2,1,0:T(8,128)}, f32[7,16,1024]{2,1,0:T(8,128)S(1)}, u32[]{:S(2)}, u32[]{:S(2)}) collective-permute-start(f32[7,16,1024]{2,1,0:T(8,128)} %pad_maximum_fusion.2), channel_id=1, source_target_pairs={{1,0},{2,1},{3,2},{5,4},{6,5},{7,6},{9,8},{10,9},{11,10},{13,12},{... | collective-permute-start | bytes 1376264 | tf_op jit(solution)/shard_map/ppermute | solution.py:150
  7.5 0.6 fusion.6.keep_ref
  8.1 0.0 copy-done.2
  8.1 0.1 slice_select_fusion
  8.2 0.0 copy-start.1
  8.2 6.3 %collective-permute-done.up_ref = f32[7,16,1024]{2,1,0:T(8,128)S(1)} collective-permute-done((f32[7,16,1024]{2,1,0:T(8,128)S(1)}, f32[7,16,1024]{2,1,0:T(8,128)S(1)}, u32[]{:S(2)}, u32[]{:S(2)}) %collective-permute-start) | collective-permute-done | bytes 458784 | tf_op jit(solution)/shard_map/ppermute | solution.py:149
  14.5 4.9 %collective-permute-done.1.dn_ref = f32[7,16,1024]{2,1,0:T(8,128)S(1)} collective-permute-done((f32[7,16,1024]{2,1,0:T(8,128)}, f32[7,16,1024]{2,1,0:T(8,128)S(1)}, u32[]{:S(2)}, u32[]{:S(2)}) %collective-permute-start.1) | collective-permute-done | bytes 458784 | tf_op jit(solution)/shard_map/ppermute | solution.py:150
  19.4 0.0 copy-done.4
  19.4 0.8 copy-done.5
  20.2 16.4 %shard_map.46 = f32[4,32,1024]{2,1,0:T(8,128)} custom-call(f32[4,32,1024]{2,1,0:T(8,128)} %bitcast.24, f32[32,1024]{1,0:T(8,128)} %dif_ref.1, f32[2,32,1024]{2,1,0:T(8,128)} %frc_ref.1, f32[7,16,1024]{2,1,0:T(8,128)} %copy-done.4, f32[7,16,1024]{2,1,0:T(8,128)} %copy-done.5, f32[64,1]{1,0:T(8,128)} %fusion.6.keep_ref), custom_call_target="tpu_custom_call" | custom-call | tf_op jit(solution)/shard_map/pallas_call | solution.py:156
  36.6 0.0 copy-done.1
  36.6 1.1 %multiply_subtract_fusion = f32[2,2,32,1024]{3,2,1,0:T(8,128)S(1)} fusion(f32[2,2,32,1024]{3,2,1,0:T(8,128)} %bitcast.27, f32[2,2,32,1024]{3,2,1,0:T(8,128)S(1)} %copy-done.2, f32[2,2,32,1024]{3,2,1,0:T(8,128)S(1)} %copy-done.1), kind=kLoop, calls=%fused_computation.2 | loop fusion | flops 262144 | bytes 2097152 | tf_op jit(solution)/shard_map/sub | solution.py:169
  37.8 0.1 fusion.10
  37.9 0.8 maximum_bitcast_fusion.send_ref
  38.7 46.4 %shard_map.47 = f32[64,1,8,128]{3,2,1,0:T(8,128)} custom-call(f32[64,1,2,8,128]{4,3,2,1,0:T(8,128)} %maximum_bitcast_fusion.send_ref), custom_call_target="tpu_custom_call" | custom-call | tf_op jit(solution)/shard_map/pallas_call | solution.py:180
  85.2 1.1 %multiply_add_fusion = (f32[1,2,32,1024]{3,2,1,0:T(8,128)S(1)}, f32[1,2,32,1024]{3,2,1,0:T(8,128)S(1)}) fusion(f32[2,2,32,1024]{3,2,1,0:T(8,128)S(1)} %multiply_subtract_fusion, f32[2,2,32,1024]{3,2,1,0:T(8,128)S(1)} %copy-done.2, f32[1,2,32,1024]{3,2,1,0:T(8,128)S(1)} %get-tuple-element.8, f32[1,2,32,1024]{3,2,1,0:T(8,128)} %bitcast.28, pred[]{:T(512)S(6)} %eq.3), kind=kLoop, calls=%fused_computation.10 | loop fusion | flops 458752 | bytes 2097153 | tf_op jit(solution)/shard_map/add | solution.py:200
  86.2 0.8 pad_maximum_fusion
  (7 shorter events, 0.1 us)
Async XLA Ops:
  0.0 1.0 %copy-start.3 = (f32[2,32,1024]{2,1,0:T(8,128)S(1)}, f32[2,32,1024]{2,1,0:T(8,128)}, u32[]{:S(2)}) copy-start(f32[2,32,1024]{2,1,0:T(8,128)} %frc_ref.1) | copy-start | bytes 786436
  0.0 1.2 %copy-start = (f32[2,2,32,1024]{3,2,1,0:T(8,128)S(1)}, f32[2,2,32,1024]{3,2,1,0:T(8,128)}, u32[]{:S(2)}) copy-start(f32[2,2,32,1024]{3,2,1,0:T(8,128)} %param.4) | copy-start | bytes 1572868
  1.3 6.8 %copy-start.2 = (f32[2,2,32,1024]{3,2,1,0:T(8,128)S(1)}, f32[2,2,32,1024]{3,2,1,0:T(8,128)}, u32[]{:S(2)}) copy-start(f32[2,2,32,1024]{3,2,1,0:T(8,128)} %param.5) | copy-start | bytes 1572868
  1.3 13.3 %collective-permute-start = (f32[7,16,1024]{2,1,0:T(8,128)S(1)}, f32[7,16,1024]{2,1,0:T(8,128)S(1)}, u32[]{:S(2)}, u32[]{:S(2)}) collective-permute-start(f32[7,16,1024]{2,1,0:T(8,128)S(1)} %pad_maximum_fusion.1), channel_id=1, source_target_pairs={{0,1},{1,2},{2,3},{4,5},{5,6},{6,7},{8,9},{9,10},{10,11},{12,13},{... | collective-permute-start | bytes 1376264 | tf_op jit(solution)/shard_map/ppermute | solution.py:149
  6.2 13.2 %collective-permute-start.1 = (f32[7,16,1024]{2,1,0:T(8,128)}, f32[7,16,1024]{2,1,0:T(8,128)S(1)}, u32[]{:S(2)}, u32[]{:S(2)}) collective-permute-start(f32[7,16,1024]{2,1,0:T(8,128)} %pad_maximum_fusion.2), channel_id=1, source_target_pairs={{1,0},{2,1},{3,2},{5,4},{6,5},{7,6},{9,8},{10,9},{11,10},{13,12},{... | collective-permute-start | bytes 1376264 | tf_op jit(solution)/shard_map/ppermute | solution.py:150
  8.2 28.4 %copy-start.1 = (f32[2,2,32,1024]{3,2,1,0:T(8,128)S(1)}, f32[2,2,32,1024]{3,2,1,0:T(8,128)}, u32[]{:S(2)}) copy-start(f32[2,2,32,1024]{3,2,1,0:T(8,128)} %param.4) | copy-start | bytes 1572868
  14.5 4.9 %copy-start.4 = (f32[7,16,1024]{2,1,0:T(8,128)}, f32[7,16,1024]{2,1,0:T(8,128)S(1)}, u32[]{:S(2)}) copy-start(f32[7,16,1024]{2,1,0:T(8,128)S(1)} %collective-permute-done.up_ref) | copy-start | bytes 1376260
  19.4 0.8 copy-start.5

commit v6 on v3

--- a/solution.py
+++ b/solution.py
@@ -58,11 +58,78 @@
     out_ref[...] = buf[:, HALO:HALO + own, :]
 
 
-def scan_kernel(a_ref, b_ref, x_ref):
-    x = jnp.zeros(a_ref.shape[1:], jnp.float32)
-    for s in range(a_ref.shape[0]):
-        x_ref[s] = x
-        x = a_ref[s] * x + b_ref[s]
+def exchange_kernel(send_ref, out_ref, recv1, pa, pb, gsend, recv2, xg, back2, xs, back1, sems):
+    nq = send_ref.shape[0]
+    nz = gsend.shape[0]
+    mz = lax.axis_index("tz")
+    mq = lax.axis_index("tq")
+    sp = lax.axis_index("space")
+    mesh_id = pl.DeviceIdType.MESH
+
+    def exchange(phase, src, dst, n, me, where):
+        ssem, rsem = sems.at[2 * phase], sems.at[2 * phase + 1]
+
+        def outgoing(d):
+            return pltpu.make_async_remote_copy(
+                src_ref=src.at[d], dst_ref=dst.at[me], send_sem=ssem.at[d], recv_sem=rsem.at[me],
+                device_id=where(d), device_id_type=mesh_id,
+            )
+
+        def incoming(e):
+            return pltpu.make_async_remote_copy(
+                src_ref=src.at[e], dst_ref=dst.at[e], send_sem=ssem.at[e], recv_sem=rsem.at[e],
+                device_id=where(e), device_id_type=mesh_id,
+            )
+
+        def start(k, carry):
+            outgoing(lax.rem(me + k, n)).start()
+            return carry
+
+        lax.fori_loop(1, n, start, 0)
+        dst[me] = src[me]
+
+        def wait(k, carry):
+            d = lax.rem(me + k, n)
+            outgoing(d).wait_send()
+            incoming(d).wait_recv()
+            return carry
+
+        lax.fori_loop(1, n, wait, 0)
+
+    in_plane = lambda d: (mz, d, sp)
+    across = lambda d: (d, mq, sp)
+    exchange(0, send_ref, recv1, nq, mq, in_plane)
+
+    def group_step(s, carry):
+        ga, gb = carry
+        pa[s] = ga
+        pb[s] = gb
+        a = recv1[s, :, 0]
+        return a * ga, a * gb + recv1[s, :, 1]
+
+    ones = jnp.ones(pa.shape[1:], jnp.float32)
+    ga, gb = lax.fori_loop(0, nq, group_step, (ones, jnp.zeros_like(ones)))
+    c2 = gsend.shape[1]
+    for z in range(nz):
+        gsend[z, :, 0] = ga[z * c2:(z + 1) * c2]
+        gsend[z, :, 1] = gb[z * c2:(z + 1) * c2]
+    exchange(1, gsend, recv2, nz, mz, across)
+
+    def entry_step(s, x):
+        xg[s] = x
+        return recv2[s, :, 0] * x + recv2[s, :, 1]
+
+    lax.fori_loop(0, nz, entry_step, jnp.zeros(xg.shape[1:], jnp.float32))
+    exchange(2, xg, back2, nz, mz, across)
+    group_in = back2[...].reshape(pa.shape[1:])
+
+    def spread_step(s, carry):
+        xs[s] = pa[s] * group_in + pb[s]
+        return carry
+
+    lax.fori_loop(0, nq, spread_step, 0)
+    exchange(3, xs, back1, nq, mq, in_plane)
+    out_ref[...] = back1[...]
 
 
 def to_tiles(block):
@@ -80,10 +147,9 @@
 def per_device_body(coarse_points, coarse_decay, diffusion, forcing):
     slots, comps, row_count, col_count = coarse_points.shape
     space_count = lax.axis_size("space")
-    tm_count = lax.axis_size("tm")
     me = lax.axis_index("space")
 
-    at_anchor = lax.axis_index("tm") == 0
+    at_anchor = (lax.axis_index("tz") == 0) & (lax.axis_index("tq") == 0)
     scale0 = jnp.where(at_anchor, 0.0, coarse_decay[0])
     comp_scale = coarse_decay[1] * scale0
 
@@ -121,18 +187,36 @@
     shift0 = jnp.where(at_anchor, coarse_decay[0] * coarse_points[0] + shift[0], shift[0])
     comp_shift = scale[1] * shift0 + shift[1]
 
-    both = jnp.stack([to_tiles(comp_scale), to_tiles(comp_shift)])
-    got = lax.all_to_all(both, "tm", split_axis=1, concat_axis=1, tiled=True)
-    got_scale, got_shift = got[0], got[1]
-    per_src = got_shift.shape[0] // tm_count
-    tile_shape = (tm_count, per_src, 8, 128)
-    prefix = pl.pallas_call(
-        scan_kernel,
-        out_shape=jax.ShapeDtypeStruct(tile_shape, jnp.float32),
-    )(got_scale.reshape(tile_shape), got_shift.reshape(tile_shape))
-    back = lax.all_to_all(
-        prefix.reshape(tm_count * per_src, 8, 128), "tm", split_axis=0, concat_axis=0, tiled=True
-    )
+    both = jnp.stack([to_tiles(comp_scale), to_tiles(comp_shift)], axis=1)
+    tiles = both.shape[0]
+    q_count = lax.axis_size("tq")
+    z_count = lax.axis_size("tz")
+    c1 = tiles // q_count
+    c2 = c1 // z_count
+    both = both.reshape(q_count, c1, 2, 8, 128)
+    x1 = (q_count, c1, 8, 128)
+    x2 = (z_count, c2, 8, 128)
+    vmem = pl.BlockSpec(memory_space=pltpu.VMEM)
+    back = pl.pallas_call(
+        exchange_kernel,
+        out_shape=jax.ShapeDtypeStruct(x1, jnp.float32),
+        in_specs=[vmem],
+        out_specs=vmem,
+        scratch_shapes=[
+            pltpu.VMEM(both.shape, jnp.float32),
+            pltpu.VMEM(x1, jnp.float32),
+            pltpu.VMEM(x1, jnp.float32),
+            pltpu.VMEM((z_count, c2, 2, 8, 128), jnp.float32),
+            pltpu.VMEM((z_count, c2, 2, 8, 128), jnp.float32),
+            pltpu.VMEM(x2, jnp.float32),
+            pltpu.VMEM(x2, jnp.float32),
+            pltpu.VMEM(x1, jnp.float32),
+            pltpu.VMEM(x1, jnp.float32),
+            pltpu.SemaphoreType.DMA((8, max(q_count, z_count))),
+        ],
+        compiler_params=pltpu.CompilerParams(has_side_effects=True),
+    )(both)
+    back = back.reshape(tiles, 8, 128)
     entering = from_tiles(back, (comps, row_count, col_count))
 
     first = scale0 * entering + shift0
@@ -141,9 +225,14 @@
 
 
 def solution(mesh):
+    tm_count = mesh.shape["tm"]
+    q_count = 8 if tm_count >= 16 and tm_count % 8 == 0 else 2
+    grid = mesh.devices.reshape(tm_count // q_count, q_count, mesh.shape["space"])
+    mesh = jax.sharding.Mesh(grid, ("tz", "tq", "space"))
+    time_axes = ("tz", "tq")
     placed = (
-        P("tm", None, "space", None),
-        P("tm", None, "space", None),
+        P(time_axes, None, "space", None),
+        P(time_axes, None, "space", None),
         P("space", None),
         P(None, "space", None),
     )
@@ -151,6 +240,6 @@
         per_device_body,
         mesh=mesh,
         in_specs=placed,
-        out_specs=P("tm", None, "space", None),
+        out_specs=P(time_axes, None, "space", None),
         check_vma=False,
     )

time: 91.6 us -> 81.9 us (0.89)
  blocking collectives: 49.7 us -> 0 us
  Pallas kernels: 18.3 us -> 57.4 us
  other arithmetic: 3.72 us -> 5.49 us
    all_to_all x2 -> x0, blocking collectives: 49.7 us -> none  [the longest x1 31 us: per_device_body(): got = lax.all_to_all(both, 'tm', split_axis=1, concat_axis=1, tiled=True)]
    pallas_call x1, Pallas kernels: 1.86 us -> 41 us  [per_device_body(): pl.pallas_call(exchange_kernel, out_shape=jax.ShapeDtypeStruct(x1, jnp.fl...]
    add x1, other arithmetic: 0.11 us -> 1.06 us  [per_device_body(): second = scale[1] * first + shift[1]]
where the time goes in v6:
time: 81.9 us; the launch traced here: 81.6 us
  Pallas kernels  57.4 us (70%)
  waiting for transfers between devices  11.2 us (14%)
  other arithmetic  5.49 us (7%)
  starting transfers between devices  5.37 us (7%)
  local copies, waits for them, and re-layouts  2.04 us (2%)
    pallas_call x1, Pallas kernels, per_device_body(): pl.pallas_call(exchange_kernel, out_shape=jax.ShapeDtypeStruct(x1, jnp.fl...  41 us
    pallas_call x1, Pallas kernels, per_device_body(): pl.pallas_call(fine_kernel, out_shape=jax.ShapeDtypeStruct((slots * comps...  16.4 us
    ppermute x1, waiting for transfers between devices, per_device_body(): above = lax.ppermute(up_rim, 'space', forward)  6.33 us
    ppermute x1, waiting for transfers between devices, per_device_body(): below = lax.ppermute(dn_rim, 'space', backward)  4.86 us
    ppermute x1, starting transfers between devices, per_device_body(): above = lax.ppermute(up_rim, 'space', forward)  4.09 us
  transfers between devices with their start and end apart: 2, of which 2 were waited for; matrix products, arithmetic and copies ran while one was open for 2% of the time, Pallas kernels for 0%

profile of v6, /device:TPU:1, one launch (start us, length us, event | category | flops | bytes accessed | tf_op | source)
XLA Modules:
  0.0 81.6 jit_solution(8299255684743942689)
XLA Ops:
  0.0 0.0 copy-start.3
  0.0 1.0 %slice_bitcast_fusion = (f32[1,16,1024]{2,1,0:T(8,128)S(1)}, f32[1,16,1024]{2,1,0:T(8,128)S(1)}) fusion(f32[32,1024]{1,0:T(8,128)} %dif_ref.1), kind=kLoop, calls=%fused_computation.15 | loop fusion | bytes 262144 | tf_op jit(solution)/shard_map/broadcast_in_dim | solution.py:161
  1.0 0.1 copy-done.3
  1.0 0.2 copy-done
  1.3 0.0 copy-start.2
  1.3 4.1 %collective-permute-start = (f32[7,16,1024]{2,1,0:T(8,128)S(1)}, f32[7,16,1024]{2,1,0:T(8,128)S(1)}, u32[]{:S(2)}, u32[]{:S(2)}) collective-permute-start(f32[7,16,1024]{2,1,0:T(8,128)S(1)} %pad_maximum_fusion.2), channel_id=1, source_target_pairs={{0,1},{1,2},{2,3},{4,5},{5,6},{6,7},{8,9},{9,10},{10,11},{12,13},{... | collective-permute-start | bytes 1376264 | tf_op jit(solution)/shard_map/ppermute | solution.py:165
  5.4 0.8 pad_maximum_fusion.3
  6.2 1.3 %collective-permute-start.1 = (f32[7,16,1024]{2,1,0:T(8,128)}, f32[7,16,1024]{2,1,0:T(8,128)S(1)}, u32[]{:S(2)}, u32[]{:S(2)}) collective-permute-start(f32[7,16,1024]{2,1,0:T(8,128)} %pad_maximum_fusion.3), channel_id=1, source_target_pairs={{1,0},{2,1},{3,2},{5,4},{6,5},{7,6},{9,8},{10,9},{11,10},{13,12},{... | collective-permute-start | bytes 1376264 | tf_op jit(solution)/shard_map/ppermute | solution.py:166
  7.5 0.6 fusion.7.keep_ref
  8.1 0.0 copy-done.2
  8.1 0.1 slice_select_fusion
  8.2 0.0 copy-start.1
  8.2 6.3 %collective-permute-done.up_ref = f32[7,16,1024]{2,1,0:T(8,128)S(1)} collective-permute-done((f32[7,16,1024]{2,1,0:T(8,128)S(1)}, f32[7,16,1024]{2,1,0:T(8,128)S(1)}, u32[]{:S(2)}, u32[]{:S(2)}) %collective-permute-start) | collective-permute-done | bytes 458784 | tf_op jit(solution)/shard_map/ppermute | solution.py:165
  14.5 4.9 %collective-permute-done.1.dn_ref = f32[7,16,1024]{2,1,0:T(8,128)S(1)} collective-permute-done((f32[7,16,1024]{2,1,0:T(8,128)}, f32[7,16,1024]{2,1,0:T(8,128)S(1)}, u32[]{:S(2)}, u32[]{:S(2)}) %collective-permute-start.1) | collective-permute-done | bytes 458784 | tf_op jit(solution)/shard_map/ppermute | solution.py:166
  19.4 0.0 copy-done.4
  19.4 0.8 copy-done.5
  20.2 16.4 %shard_map.46 = f32[4,32,1024]{2,1,0:T(8,128)} custom-call(f32[4,32,1024]{2,1,0:T(8,128)} %bitcast.24, f32[32,1024]{1,0:T(8,128)} %dif_ref.1, f32[2,32,1024]{2,1,0:T(8,128)} %frc_ref.1, f32[7,16,1024]{2,1,0:T(8,128)} %copy-done.4, f32[7,16,1024]{2,1,0:T(8,128)} %copy-done.5, f32[64,1]{1,0:T(8,128)} %fusion.7.keep_ref), custom_call_target="tpu_custom_call" | custom-call | tf_op jit(solution)/shard_map/pallas_call | solution.py:172
  36.6 0.0 copy-done.1
  36.6 1.1 %multiply_subtract_fusion = f32[2,2,32,1024]{3,2,1,0:T(8,128)S(1)} fusion(f32[2,2,32,1024]{3,2,1,0:T(8,128)} %bitcast.27, f32[2,2,32,1024]{3,2,1,0:T(8,128)S(1)} %copy-done.2, f32[2,2,32,1024]{3,2,1,0:T(8,128)S(1)} %copy-done.1), kind=kLoop, calls=%fused_computation.2 | loop fusion | flops 262144 | bytes 2097152 | tf_op jit(solution)/shard_map/sub | solution.py:185
  37.8 0.1 multiply_bitcast_fusion
  37.9 0.8 %pad_maximum_fusion.send_ref = f32[8,8,2,8,128]{4,3,2,1,0:T(8,128)} fusion(f32[8,8,1,8,128]{4,3,2,1,0:T(8,128)S(1)} %get-tuple-element.15, f32[8,8,1,8,128]{4,3,2,1,0:T(8,128)S(1)} %get-tuple-element.14), kind=kLoop, calls=%fused_computation | loop fusion | flops 131072 | bytes 1048576 | tf_op jit(solution)/shard_map/stack | solution.py:190
  38.7 41.0 %shard_map.47 = f32[8,8,8,128]{3,2,1,0:T(8,128)} custom-call(f32[8,8,2,8,128]{4,3,2,1,0:T(8,128)} %pad_maximum_fusion.send_ref), custom_call_target="tpu_custom_call" | custom-call | tf_op jit(solution)/shard_map/pallas_call | solution.py:200
  79.7 1.1 %multiply_add_fusion = (f32[1,2,32,1024]{3,2,1,0:T(8,128)S(1)}, f32[1,2,32,1024]{3,2,1,0:T(8,128)S(1)}) fusion(f32[2,2,32,1024]{3,2,1,0:T(8,128)S(1)} %multiply_subtract_fusion, f32[2,2,32,1024]{3,2,1,0:T(8,128)S(1)} %copy-done.2, f32[1,2,32,1024]{3,2,1,0:T(8,128)S(1)} %get-tuple-element.8, f32[1,2,32,1024]{3,2,1,0:T(8,128)} %bitcast.28, pred[]{:T(512)S(6)} %and.17), kind=kLoop, calls=%fused_computation.11 | loop fusion | flops 458752 | bytes 2097153 | tf_op jit(solution)/shard_map/add | solution.py:223
  80.8 0.8 %pad_maximum_fusion.1 = f32[2,2,32,1024]{3,2,1,0:T(8,128)} fusion(f32[1,2,32,1024]{3,2,1,0:T(8,128)S(1)} %get-tuple-element.5, f32[1,2,32,1024]{3,2,1,0:T(8,128)S(1)} %get-tuple-element.6), kind=kLoop, calls=%fused_computation.1 | loop fusion | flops 131072 | bytes 1048576 | tf_op jit(solution)/shard_map/stack | solution.py:224
  (7 shorter events, 0.1 us)
Async XLA Ops:
  0.0 1.0 %copy-start.3 = (f32[2,32,1024]{2,1,0:T(8,128)S(1)}, f32[2,32,1024]{2,1,0:T(8,128)}, u32[]{:S(2)}) copy-start(f32[2,32,1024]{2,1,0:T(8,128)} %frc_ref.1) | copy-start | bytes 786436
  0.0 1.2 %copy-start = (f32[2,2,32,1024]{3,2,1,0:T(8,128)S(1)}, f32[2,2,32,1024]{3,2,1,0:T(8,128)}, u32[]{:S(2)}) copy-start(f32[2,2,32,1024]{3,2,1,0:T(8,128)} %param.4) | copy-start | bytes 1572868
  1.3 6.8 %copy-start.2 = (f32[2,2,32,1024]{3,2,1,0:T(8,128)S(1)}, f32[2,2,32,1024]{3,2,1,0:T(8,128)}, u32[]{:S(2)}) copy-start(f32[2,2,32,1024]{3,2,1,0:T(8,128)} %param.5) | copy-start | bytes 1572868
  1.3 13.3 %collective-permute-start = (f32[7,16,1024]{2,1,0:T(8,128)S(1)}, f32[7,16,1024]{2,1,0:T(8,128)S(1)}, u32[]{:S(2)}, u32[]{:S(2)}) collective-permute-start(f32[7,16,1024]{2,1,0:T(8,128)S(1)} %pad_maximum_fusion.2), channel_id=1, source_target_pairs={{0,1},{1,2},{2,3},{4,5},{5,6},{6,7},{8,9},{9,10},{10,11},{12,13},{... | collective-permute-start | bytes 1376264 | tf_op jit(solution)/shard_map/ppermute | solution.py:165
  6.2 13.2 %collective-permute-start.1 = (f32[7,16,1024]{2,1,0:T(8,128)}, f32[7,16,1024]{2,1,0:T(8,128)S(1)}, u32[]{:S(2)}, u32[]{:S(2)}) collective-permute-start(f32[7,16,1024]{2,1,0:T(8,128)} %pad_maximum_fusion.3), channel_id=1, source_target_pairs={{1,0},{2,1},{3,2},{5,4},{6,5},{7,6},{9,8},{10,9},{11,10},{13,12},{... | collective-permute-start | bytes 1376264 | tf_op jit(solution)/shard_map/ppermute | solution.py:166
  8.2 28.4 %copy-start.1 = (f32[2,2,32,1024]{3,2,1,0:T(8,128)S(1)}, f32[2,2,32,1024]{3,2,1,0:T(8,128)}, u32[]{:S(2)}) copy-start(f32[2,2,32,1024]{3,2,1,0:T(8,128)} %param.4) | copy-start | bytes 1572868
  14.5 4.9 %copy-start.4 = (f32[7,16,1024]{2,1,0:T(8,128)}, f32[7,16,1024]{2,1,0:T(8,128)S(1)}, u32[]{:S(2)}) copy-start(f32[7,16,1024]{2,1,0:T(8,128)S(1)} %collective-permute-done.up_ref) | copy-start | bytes 1376260
  19.4 0.8 copy-start.5

commit v7 on v6

--- a/solution.py
+++ b/solution.py
@@ -9,20 +9,69 @@
 HALO = M
 
 
-def fine_kernel(st_ref, dif_ref, frc_ref, up_ref, dn_ref, keep_ref, out_ref, buf, dbuf, fbuf):
+def fine_kernel(st_ref, dif_ref, frc_ref, keep_ref, out_ref, buf, dbuf, fbuf, sems):
     n_state = st_ref.shape[0]
     own = st_ref.shape[1]
     cols = st_ref.shape[2]
     rows = own + 2 * HALO
-    buf[:, :HALO] = up_ref[:n_state]
+    n = lax.axis_size("space")
+    me = lax.axis_index("space")
+    place = (lax.axis_index("tz"), lax.axis_index("tq"))
+    mesh_id = pl.DeviceIdType.MESH
+    pairs = ((st_ref, buf), (dif_ref, dbuf), (frc_ref, fbuf))
+
+    def rim_copy(k, src, dst, down, target):
+        if down:
+            s_rows, d_rows = pl.ds(own - HALO, HALO), pl.ds(0, HALO)
+        else:
+            s_rows, d_rows = pl.ds(0, HALO), pl.ds(HALO + own, HALO)
+        if src.ndim == 3:
+            src_v, dst_v = src.at[:, s_rows], dst.at[:, d_rows]
+        else:
+            src_v, dst_v = src.at[s_rows], dst.at[d_rows]
+        slot = k + (0 if down else 3)
+        return pltpu.make_async_remote_copy(
+            src_ref=src_v, dst_ref=dst_v, send_sem=sems.at[slot], recv_sem=sems.at[6 + slot],
+            device_id=place + (target,), device_id_type=mesh_id,
+        )
+
+    @pl.when(me < n - 1)
+    def _():
+        for k, (src, dst) in enumerate(pairs):
+            rim_copy(k, src, dst, True, me + 1).start()
+
+    @pl.when(me > 0)
+    def _():
+        for k, (src, dst) in enumerate(pairs):
+            rim_copy(k, src, dst, False, me - 1).start()
+
     buf[:, HALO:HALO + own] = st_ref[...]
-    buf[:, HALO + own:] = dn_ref[:n_state]
-    dbuf[:HALO] = up_ref[n_state]
     dbuf[HALO:HALO + own] = dif_ref[...]
-    dbuf[HALO + own:] = dn_ref[n_state]
-    fbuf[:, :HALO] = up_ref[n_state + 1:]
     fbuf[:, HALO:HALO + own] = frc_ref[...]
-    fbuf[:, HALO + own:] = dn_ref[n_state + 1:]
+
+    @pl.when(me == 0)
+    def _():
+        buf[:, :HALO] = jnp.zeros((n_state, HALO, cols), jnp.float32)
+        dbuf[:HALO] = jnp.zeros((HALO, cols), jnp.float32)
+        fbuf[:, :HALO] = jnp.zeros((fbuf.shape[0], HALO, cols), jnp.float32)
+
+    @pl.when(me == n - 1)
+    def _():
+        buf[:, HALO + own:] = jnp.zeros((n_state, HALO, cols), jnp.float32)
+        dbuf[HALO + own:] = jnp.zeros((HALO, cols), jnp.float32)
+        fbuf[:, HALO + own:] = jnp.zeros((fbuf.shape[0], HALO, cols), jnp.float32)
+
+    @pl.when(me < n - 1)
+    def _():
+        for k, (src, dst) in enumerate(pairs):
+            rim_copy(k, src, dst, True, me + 1).wait_send()
+            rim_copy(k, src, dst, False, me + 1).wait_recv()
+
+    @pl.when(me > 0)
+    def _():
+        for k, (src, dst) in enumerate(pairs):
+            rim_copy(k, src, dst, False, me - 1).wait_send()
+            rim_copy(k, src, dst, True, me - 1).wait_recv()
 
     def make_step(lo, hi):
         span = hi - lo
@@ -154,16 +203,6 @@
     comp_scale = coarse_decay[1] * scale0
 
     state = coarse_points.reshape(slots * comps, row_count, col_count)
-    forward = [(i, i + 1) for i in range(space_count - 1)]
-    backward = [(i + 1, i) for i in range(space_count - 1)]
-
-    def rim(lo, hi):
-        return jnp.concatenate([state[:, lo:hi], diffusion[None, lo:hi], forcing[:, lo:hi]], axis=0)
-
-    up_rim = rim(row_count - HALO, row_count)
-    dn_rim = rim(0, HALO)
-    above = lax.ppermute(up_rim, "space", forward)
-    below = lax.ppermute(dn_rim, "space", backward)
     ext_rows = row_count + 2 * HALO
     global_row = me * row_count - HALO + lax.broadcasted_iota(jnp.int32, (ext_rows, 1), 0)
     keep = ((global_row >= 0) & (global_row < space_count * row_count)).astype(jnp.float32)
@@ -172,14 +211,16 @@
     fine_end = pl.pallas_call(
         fine_kernel,
         out_shape=jax.ShapeDtypeStruct((slots * comps, row_count, col_count), jnp.float32),
-        in_specs=[vmem] * 6,
+        in_specs=[vmem] * 4,
         out_specs=vmem,
         scratch_shapes=[
             pltpu.VMEM((slots * comps, ext_rows, col_count), jnp.float32),
             pltpu.VMEM((ext_rows, col_count), jnp.float32),
             pltpu.VMEM((comps, ext_rows, col_count), jnp.float32),
+            pltpu.SemaphoreType.DMA((12,)),
         ],
-    )(state, diffusion, forcing, above, below, keep)
+        compiler_params=pltpu.CompilerParams(has_side_effects=True),
+    )(state, diffusion, forcing, keep)
     fine_end = fine_end.reshape(coarse_points.shape)
 
     shift = fine_end - coarse_decay * coarse_points

time: 81.9 us -> 85.9 us (1.049)
  Pallas kernels: 57.4 us -> 80.9 us
  waiting for transfers between devices: 11.2 us -> 0 us
  starting transfers between devices: 5.37 us -> 0 us
  local copies, waits for them, and re-layouts: 2.04 us -> 0.04 us
  other arithmetic: 5.49 us -> 4.62 us
    pallas_call x1, Pallas kernels: 16.4 us -> 41.8 us  [per_device_body(): pl.pallas_call(fine_kernel, out_shape=jax.ShapeDtypeStruct((slots * comps...]
    ppermute x2 -> x0, waiting for transfers between devices: 11.2 us -> none  [the longest x1 6.33 us: per_device_body(): above = lax.ppermute(up_rim, 'space', forward)]
    ppermute x2 -> x0, starting transfers between devices: 5.37 us -> none  [the longest x1 4.09 us: per_device_body(): above = lax.ppermute(up_rim, 'space', forward)]
    pallas_call x1, Pallas kernels: 41 us -> 39.2 us  [per_device_body(): pl.pallas_call(exchange_kernel, out_shape=jax.ShapeDtypeStruct(x1, jnp.fl...]
    unnamed x12 -> x4, local copies, waits for them, and re-layouts: 0.99 us -> 0.01 us
    broadcast_in_dim x1 -> x0, local copies, waits for them, and re-layouts: 0.95 us -> none  [rim(): diffusion[None, lo:hi]]
  transfers between devices with their start and end apart: 2 -> 0, of which waited for: 2 -> 0; matrix products, arithmetic and copies ran while one was open for 2% -> 0% of each run, Pallas kernels for 0% -> 0%
where the time goes in v7:
time: 85.9 us; the launch traced here: 85.7 us
  Pallas kernels  80.9 us (94%)
  other arithmetic  4.62 us (5%)
    pallas_call x1, Pallas kernels, per_device_body(): pl.pallas_call(fine_kernel, out_shape=jax.ShapeDtypeStruct((slots * comps...  41.8 us
    pallas_call x1, Pallas kernels, per_device_body(): pl.pallas_call(exchange_kernel, out_shape=jax.ShapeDtypeStruct(x1, jnp.fl...  39.2 us

profile of v7, /device:TPU:1, one launch (start us, length us, event | category | flops | bytes accessed | tf_op | source)
XLA Modules:
  0.0 85.7 jit_solution(482039383860372010)
XLA Ops:
  0.0 0.6 fusion.7.keep_ref
  0.6 0.0 copy-start
  0.6 0.0 copy-start.1
  0.6 41.8 %shard_map.46 = f32[4,32,1024]{2,1,0:T(8,128)} custom-call(f32[4,32,1024]{2,1,0:T(8,128)} %bitcast.20, f32[32,1024]{1,0:T(8,128)} %dif_ref.1, f32[2,32,1024]{2,1,0:T(8,128)} %frc_ref.1, f32[64,1]{1,0:T(8,128)} %fusion.7.keep_ref), custom_call_target="tpu_custom_call" | custom-call | tf_op jit(solution)/shard_map/pallas_call | solution.py:211
  42.4 0.0 copy-done
  42.4 0.0 copy-done.1
  42.4 1.1 %multiply_subtract_fusion = f32[2,2,32,1024]{3,2,1,0:T(8,128)S(1)} fusion(f32[2,2,32,1024]{3,2,1,0:T(8,128)} %bitcast.22, f32[2,2,32,1024]{3,2,1,0:T(8,128)S(1)} %copy-done, f32[2,2,32,1024]{3,2,1,0:T(8,128)S(1)} %copy-done.1), kind=kLoop, calls=%fused_computation.2 | loop fusion | flops 262144 | bytes 2097152 | tf_op jit(solution)/shard_map/sub | solution.py:226
  43.6 0.1 slice_select_fusion
  43.7 0.1 multiply_bitcast_fusion
  43.7 0.8 pad_maximum_fusion.send_ref
  44.6 39.2 %shard_map.47 = f32[8,8,8,128]{3,2,1,0:T(8,128)} custom-call(f32[8,8,2,8,128]{4,3,2,1,0:T(8,128)} %pad_maximum_fusion.send_ref), custom_call_target="tpu_custom_call" | custom-call | tf_op jit(solution)/shard_map/pallas_call | solution.py:241
  83.8 1.1 %multiply_add_fusion = (f32[1,2,32,1024]{3,2,1,0:T(8,128)S(1)}, f32[1,2,32,1024]{3,2,1,0:T(8,128)S(1)}) fusion(f32[2,2,32,1024]{3,2,1,0:T(8,128)S(1)} %multiply_subtract_fusion, f32[2,2,32,1024]{3,2,1,0:T(8,128)S(1)} %copy-done, f32[1,2,32,1024]{3,2,1,0:T(8,128)S(1)} %get-tuple-element.8, f32[1,2,32,1024]{3,2,1,0:T(8,128)} %bitcast.23, pred[]{:T(512)S(6)} %and.17), kind=kLoop, calls=%fused_computation.9 | loop fusion | flops 458752 | bytes 2097153 | tf_op jit(solution)/shard_map/add | solution.py:264
  84.8 0.8 pad_maximum_fusion.1
  (1 shorter events, 0.0 us)
Async XLA Ops:
  0.6 41.8 %copy-start = (f32[2,2,32,1024]{3,2,1,0:T(8,128)S(1)}, f32[2,2,32,1024]{3,2,1,0:T(8,128)}, u32[]{:S(2)}) copy-start(f32[2,2,32,1024]{3,2,1,0:T(8,128)} %param.5) | copy-start | bytes 1572868
  0.6 41.8 %copy-start.1 = (f32[2,2,32,1024]{3,2,1,0:T(8,128)S(1)}, f32[2,2,32,1024]{3,2,1,0:T(8,128)}, u32[]{:S(2)}) copy-start(f32[2,2,32,1024]{3,2,1,0:T(8,128)} %param.4) | copy-start | bytes 1572868

commit v8 on v6

--- a/solution.py
+++ b/solution.py
@@ -98,6 +98,16 @@
 
     in_plane = lambda d: (mz, d, sp)
     across = lambda d: (d, mq, sp)
+    barrier = pltpu.get_barrier_semaphore()
+    for k in range(1, nq):
+        pl.semaphore_signal(
+            barrier, 1, device_id=in_plane(lax.rem(mq + k, nq)), device_id_type=mesh_id
+        )
+    for k in range(1, nz):
+        pl.semaphore_signal(
+            barrier, 1, device_id=across(lax.rem(mz + k, nz)), device_id_type=mesh_id
+        )
+    pl.semaphore_wait(barrier, nq + nz - 2)
     exchange(0, send_ref, recv1, nq, mq, in_plane)
 
     def group_step(s, carry):
@@ -214,7 +224,7 @@
             pltpu.VMEM(x1, jnp.float32),
             pltpu.SemaphoreType.DMA((8, max(q_count, z_count))),
         ],
-        compiler_params=pltpu.CompilerParams(has_side_effects=True),
+        compiler_params=pltpu.CompilerParams(collective_id=0, has_side_effects=True),
     )(both)
     back = back.reshape(tiles, 8, 128)
     entering = from_tiles(back, (comps, row_count, col_count))

time: 81.9 us -> 73.4 us (0.90)
  Pallas kernels: 57.4 us -> 48.9 us
    pallas_call x1, Pallas kernels: 41 us -> 32.5 us  [per_device_body(): pl.pallas_call(exchange_kernel, out_shape=jax.ShapeDtypeStruct(x1, jnp.fl...]
where the time goes in v8:
time: 73.4 us; the launch traced here: 73.1 us
  Pallas kernels  48.9 us (67%)
  waiting for transfers between devices  11.2 us (15%)
  other arithmetic  5.49 us (7%)
  starting transfers between devices  5.37 us (7%)
  local copies, waits for them, and re-layouts  2.04 us (3%)
    pallas_call x1, Pallas kernels, per_device_body(): pl.pallas_call(exchange_kernel, out_shape=jax.ShapeDtypeStruct(x1, jnp.fl...  32.5 us
    pallas_call x1, Pallas kernels, per_device_body(): pl.pallas_call(fine_kernel, out_shape=jax.ShapeDtypeStruct((slots * comps...  16.4 us
    ppermute x1, waiting for transfers between devices, per_device_body(): above = lax.ppermute(up_rim, 'space', forward)  6.33 us
    ppermute x1, waiting for transfers between devices, per_device_body(): below = lax.ppermute(dn_rim, 'space', backward)  4.86 us
    ppermute x1, starting transfers between devices, per_device_body(): above = lax.ppermute(up_rim, 'space', forward)  4.09 us
  transfers between devices with their start and end apart: 2, of which 2 were waited for; matrix products, arithmetic and copies ran while one was open for 2% of the time, Pallas kernels for 0%

profile of v8, /device:TPU:1, one launch (start us, length us, event | category | flops | bytes accessed | tf_op | source)
XLA Modules:
  0.0 73.1 jit_solution(15246610133769088716)
XLA Ops:
  0.0 0.0 copy-start.3
  0.0 1.0 %slice_bitcast_fusion = (f32[1,16,1024]{2,1,0:T(8,128)S(1)}, f32[1,16,1024]{2,1,0:T(8,128)S(1)}) fusion(f32[32,1024]{1,0:T(8,128)} %dif_ref.1), kind=kLoop, calls=%fused_computation.15 | loop fusion | bytes 262144 | tf_op jit(solution)/shard_map/broadcast_in_dim | solution.py:171
  1.0 0.1 copy-done.3
  1.0 0.2 copy-done
  1.3 0.0 copy-start.2
  1.3 4.1 %collective-permute-start = (f32[7,16,1024]{2,1,0:T(8,128)S(1)}, f32[7,16,1024]{2,1,0:T(8,128)S(1)}, u32[]{:S(2)}, u32[]{:S(2)}) collective-permute-start(f32[7,16,1024]{2,1,0:T(8,128)S(1)} %pad_maximum_fusion.2), channel_id=1, source_target_pairs={{0,1},{1,2},{2,3},{4,5},{5,6},{6,7},{8,9},{9,10},{10,11},{12,13},{... | collective-permute-start | bytes 1376264 | tf_op jit(solution)/shard_map/ppermute | solution.py:175
  5.4 0.8 %pad_maximum_fusion.3 = f32[7,16,1024]{2,1,0:T(8,128)} fusion(f32[2,16,1024]{2,1,0:T(8,128)S(1)} %get-tuple-element.16, f32[1,16,1024]{2,1,0:T(8,128)S(1)} %get-tuple-element.18, f32[4,16,1024]{2,1,0:T(8,128)S(1)} %get-tuple-element.12), kind=kLoop, calls=%fused_computation.4 | loop fusion | flops 229376 | bytes 917504 | tf_op jit(solution)/shard_map/concatenate | solution.py:171
  6.2 1.3 %collective-permute-start.1 = (f32[7,16,1024]{2,1,0:T(8,128)}, f32[7,16,1024]{2,1,0:T(8,128)S(1)}, u32[]{:S(2)}, u32[]{:S(2)}) collective-permute-start(f32[7,16,1024]{2,1,0:T(8,128)} %pad_maximum_fusion.3), channel_id=1, source_target_pairs={{1,0},{2,1},{3,2},{5,4},{6,5},{7,6},{9,8},{10,9},{11,10},{13,12},{... | collective-permute-start | bytes 1376264 | tf_op jit(solution)/shard_map/ppermute | solution.py:176
  7.5 0.6 fusion.7.keep_ref
  8.1 0.0 copy-done.2
  8.1 0.1 slice_select_fusion
  8.2 0.0 copy-start.1
  8.2 6.3 %collective-permute-done.up_ref = f32[7,16,1024]{2,1,0:T(8,128)S(1)} collective-permute-done((f32[7,16,1024]{2,1,0:T(8,128)S(1)}, f32[7,16,1024]{2,1,0:T(8,128)S(1)}, u32[]{:S(2)}, u32[]{:S(2)}) %collective-permute-start) | collective-permute-done | bytes 458784 | tf_op jit(solution)/shard_map/ppermute | solution.py:175
  14.5 4.9 %collective-permute-done.1.dn_ref = f32[7,16,1024]{2,1,0:T(8,128)S(1)} collective-permute-done((f32[7,16,1024]{2,1,0:T(8,128)}, f32[7,16,1024]{2,1,0:T(8,128)S(1)}, u32[]{:S(2)}, u32[]{:S(2)}) %collective-permute-start.1) | collective-permute-done | bytes 458784 | tf_op jit(solution)/shard_map/ppermute | solution.py:176
  19.4 0.0 copy-done.4
  19.4 0.8 %copy-done.5 = f32[7,16,1024]{2,1,0:T(8,128)} copy-done((f32[7,16,1024]{2,1,0:T(8,128)}, f32[7,16,1024]{2,1,0:T(8,128)S(1)}, u32[]{:S(2)}) %copy-start.5) | copy-done | bytes 458776
  20.2 16.4 %shard_map.46 = f32[4,32,1024]{2,1,0:T(8,128)} custom-call(f32[4,32,1024]{2,1,0:T(8,128)} %bitcast.24, f32[32,1024]{1,0:T(8,128)} %dif_ref.1, f32[2,32,1024]{2,1,0:T(8,128)} %frc_ref.1, f32[7,16,1024]{2,1,0:T(8,128)} %copy-done.4, f32[7,16,1024]{2,1,0:T(8,128)} %copy-done.5, f32[64,1]{1,0:T(8,128)} %fusion.7.keep_ref), custom_call_target="tpu_custom_call" | custom-call | tf_op jit(solution)/shard_map/pallas_call | solution.py:182
  36.6 0.0 copy-done.1
  36.6 1.1 %multiply_subtract_fusion = f32[2,2,32,1024]{3,2,1,0:T(8,128)S(1)} fusion(f32[2,2,32,1024]{3,2,1,0:T(8,128)} %bitcast.27, f32[2,2,32,1024]{3,2,1,0:T(8,128)S(1)} %copy-done.2, f32[2,2,32,1024]{3,2,1,0:T(8,128)S(1)} %copy-done.1), kind=kLoop, calls=%fused_computation.2 | loop fusion | flops 262144 | bytes 2097152 | tf_op jit(solution)/shard_map/sub | solution.py:195
  37.8 0.1 multiply_bitcast_fusion
  37.9 0.8 %pad_maximum_fusion.send_ref = f32[8,8,2,8,128]{4,3,2,1,0:T(8,128)} fusion(f32[8,8,1,8,128]{4,3,2,1,0:T(8,128)S(1)} %get-tuple-element.15, f32[8,8,1,8,128]{4,3,2,1,0:T(8,128)S(1)} %get-tuple-element.14), kind=kLoop, calls=%fused_computation | loop fusion | flops 131072 | bytes 1048576 | tf_op jit(solution)/shard_map/stack | solution.py:200
  38.7 32.5 %shard_map.47 = f32[8,8,8,128]{3,2,1,0:T(8,128)} custom-call(f32[8,8,2,8,128]{4,3,2,1,0:T(8,128)} %pad_maximum_fusion.send_ref), custom_call_target="tpu_custom_call" | custom-call | tf_op jit(solution)/shard_map/pallas_call | solution.py:210
  71.2 1.1 %multiply_add_fusion = (f32[1,2,32,1024]{3,2,1,0:T(8,128)S(1)}, f32[1,2,32,1024]{3,2,1,0:T(8,128)S(1)}) fusion(f32[2,2,32,1024]{3,2,1,0:T(8,128)S(1)} %multiply_subtract_fusion, f32[2,2,32,1024]{3,2,1,0:T(8,128)S(1)} %copy-done.2, f32[1,2,32,1024]{3,2,1,0:T(8,128)S(1)} %get-tuple-element.8, f32[1,2,32,1024]{3,2,1,0:T(8,128)} %bitcast.28, pred[]{:T(512)S(6)} %and.17), kind=kLoop, calls=%fused_computation.11 | loop fusion | flops 458752 | bytes 2097153 | tf_op jit(solution)/shard_map/add | solution.py:233
  72.3 0.8 %pad_maximum_fusion.1 = f32[2,2,32,1024]{3,2,1,0:T(8,128)} fusion(f32[1,2,32,1024]{3,2,1,0:T(8,128)S(1)} %get-tuple-element.5, f32[1,2,32,1024]{3,2,1,0:T(8,128)S(1)} %get-tuple-element.6), kind=kLoop, calls=%fused_computation.1 | loop fusion | flops 131072 | bytes 1048576 | tf_op jit(solution)/shard_map/stack | solution.py:234
  (7 shorter events, 0.1 us)
Async XLA Ops:
  0.0 1.0 %copy-start.3 = (f32[2,32,1024]{2,1,0:T(8,128)S(1)}, f32[2,32,1024]{2,1,0:T(8,128)}, u32[]{:S(2)}) copy-start(f32[2,32,1024]{2,1,0:T(8,128)} %frc_ref.1) | copy-start | bytes 786436
  0.0 1.2 %copy-start = (f32[2,2,32,1024]{3,2,1,0:T(8,128)S(1)}, f32[2,2,32,1024]{3,2,1,0:T(8,128)}, u32[]{:S(2)}) copy-start(f32[2,2,32,1024]{3,2,1,0:T(8,128)} %param.4) | copy-start | bytes 1572868
  1.3 6.8 %copy-start.2 = (f32[2,2,32,1024]{3,2,1,0:T(8,128)S(1)}, f32[2,2,32,1024]{3,2,1,0:T(8,128)}, u32[]{:S(2)}) copy-start(f32[2,2,32,1024]{3,2,1,0:T(8,128)} %param.5) | copy-start | bytes 1572868
  1.3 13.3 %collective-permute-start = (f32[7,16,1024]{2,1,0:T(8,128)S(1)}, f32[7,16,1024]{2,1,0:T(8,128)S(1)}, u32[]{:S(2)}, u32[]{:S(2)}) collective-permute-start(f32[7,16,1024]{2,1,0:T(8,128)S(1)} %pad_maximum_fusion.2), channel_id=1, source_target_pairs={{0,1},{1,2},{2,3},{4,5},{5,6},{6,7},{8,9},{9,10},{10,11},{12,13},{... | collective-permute-start | bytes 1376264 | tf_op jit(solution)/shard_map/ppermute | solution.py:175
  6.2 13.2 %collective-permute-start.1 = (f32[7,16,1024]{2,1,0:T(8,128)}, f32[7,16,1024]{2,1,0:T(8,128)S(1)}, u32[]{:S(2)}, u32[]{:S(2)}) collective-permute-start(f32[7,16,1024]{2,1,0:T(8,128)} %pad_maximum_fusion.3), channel_id=1, source_target_pairs={{1,0},{2,1},{3,2},{5,4},{6,5},{7,6},{9,8},{10,9},{11,10},{13,12},{... | collective-permute-start | bytes 1376264 | tf_op jit(solution)/shard_map/ppermute | solution.py:176
  8.2 28.4 %copy-start.1 = (f32[2,2,32,1024]{3,2,1,0:T(8,128)S(1)}, f32[2,2,32,1024]{3,2,1,0:T(8,128)}, u32[]{:S(2)}) copy-start(f32[2,2,32,1024]{3,2,1,0:T(8,128)} %param.4) | copy-start | bytes 1572868
  14.5 4.9 %copy-start.4 = (f32[7,16,1024]{2,1,0:T(8,128)}, f32[7,16,1024]{2,1,0:T(8,128)S(1)}, u32[]{:S(2)}) copy-start(f32[7,16,1024]{2,1,0:T(8,128)S(1)} %collective-permute-done.up_ref) | copy-start | bytes 1376260
  19.4 0.8 %copy-start.5 = (f32[7,16,1024]{2,1,0:T(8,128)}, f32[7,16,1024]{2,1,0:T(8,128)S(1)}, u32[]{:S(2)}) copy-start(f32[7,16,1024]{2,1,0:T(8,128)S(1)} %collective-permute-done.1.dn_ref) | copy-start | bytes 1376260

commit v9 on v7

--- a/solution.py
+++ b/solution.py
@@ -19,6 +19,23 @@
     place = (lax.axis_index("tz"), lax.axis_index("tq"))
     mesh_id = pl.DeviceIdType.MESH
     pairs = ((st_ref, buf), (dif_ref, dbuf), (frc_ref, fbuf))
+    barrier = pltpu.get_barrier_semaphore()
+
+    @pl.when(me > 0)
+    def _():
+        pl.semaphore_signal(barrier, 1, device_id=place + (me - 1,), device_id_type=mesh_id)
+
+    @pl.when(me < n - 1)
+    def _():
+        pl.semaphore_signal(barrier, 1, device_id=place + (me + 1,), device_id_type=mesh_id)
+
+    @pl.when((me > 0) & (me < n - 1))
+    def _():
+        pl.semaphore_wait(barrier, 2)
+
+    @pl.when((me == 0) | (me == n - 1))
+    def _():
+        pl.semaphore_wait(barrier, 1)
 
     def rim_copy(k, src, dst, down, target):
         if down:
@@ -147,6 +164,16 @@
 
     in_plane = lambda d: (mz, d, sp)
     across = lambda d: (d, mq, sp)
+    barrier = pltpu.get_barrier_semaphore()
+    for k in range(1, nq):
+        pl.semaphore_signal(
+            barrier, 1, device_id=in_plane(lax.rem(mq + k, nq)), device_id_type=mesh_id
+        )
+    for k in range(1, nz):
+        pl.semaphore_signal(
+            barrier, 1, device_id=across(lax.rem(mz + k, nz)), device_id_type=mesh_id
+        )
+    pl.semaphore_wait(barrier, nq + nz - 2)
     exchange(0, send_ref, recv1, nq, mq, in_plane)
 
     def group_step(s, carry):
@@ -219,7 +246,7 @@
             pltpu.VMEM((comps, ext_rows, col_count), jnp.float32),
             pltpu.SemaphoreType.DMA((12,)),
         ],
-        compiler_params=pltpu.CompilerParams(has_side_effects=True),
+        compiler_params=pltpu.CompilerParams(collective_id=1, has_side_effects=True),
     )(state, diffusion, forcing, keep)
     fine_end = fine_end.reshape(coarse_points.shape)
 
@@ -255,7 +282,7 @@
             pltpu.VMEM(x1, jnp.float32),
             pltpu.SemaphoreType.DMA((8, max(q_count, z_count))),
         ],
-        compiler_params=pltpu.CompilerParams(has_side_effects=True),
+        compiler_params=pltpu.CompilerParams(collective_id=0, has_side_effects=True),
     )(both)
     back = back.reshape(tiles, 8, 128)
     entering = from_tiles(back, (comps, row_count, col_count))

time: 85.9 us -> 66.6 us (0.78)
  Pallas kernels: 80.9 us -> 61.7 us
    pallas_call x1, Pallas kernels: 41.8 us -> 28.6 us  [per_device_body(): pl.pallas_call(fine_kernel, out_shape=jax.ShapeDtypeStruct((slots * comps...]
    pallas_call x1, Pallas kernels: 39.2 us -> 33 us  [per_device_body(): pl.pallas_call(exchange_kernel, out_shape=jax.ShapeDtypeStruct(x1, jnp.fl...]
where the time goes in v9:
time: 66.6 us; the launch traced here: 66.4 us
  Pallas kernels  61.7 us (93%)
  other arithmetic  4.62 us (7%)
    pallas_call x1, Pallas kernels, per_device_body(): pl.pallas_call(exchange_kernel, out_shape=jax.ShapeDtypeStruct(x1, jnp.fl...  33 us
    pallas_call x1, Pallas kernels, per_device_body(): pl.pallas_call(fine_kernel, out_shape=jax.ShapeDtypeStruct((slots * comps...  28.6 us

profile of v9, /device:TPU:1, one launch (start us, length us, event | category | flops | bytes accessed | tf_op | source)
XLA Modules:
  0.0 66.4 jit_solution(13129258330230702124)
XLA Ops:
  0.0 0.6 fusion.7.keep_ref
  0.6 0.0 copy-start
  0.6 0.0 copy-start.1
  0.6 28.6 %shard_map.46 = f32[4,32,1024]{2,1,0:T(8,128)} custom-call(f32[4,32,1024]{2,1,0:T(8,128)} %bitcast.20, f32[32,1024]{1,0:T(8,128)} %dif_ref.1, f32[2,32,1024]{2,1,0:T(8,128)} %frc_ref.1, f32[64,1]{1,0:T(8,128)} %fusion.7.keep_ref), custom_call_target="tpu_custom_call" | custom-call | tf_op jit(solution)/shard_map/pallas_call | solution.py:238
  29.3 0.0 copy-done
  29.3 0.0 copy-done.1
  29.3 1.1 %multiply_subtract_fusion = f32[2,2,32,1024]{3,2,1,0:T(8,128)S(1)} fusion(f32[2,2,32,1024]{3,2,1,0:T(8,128)} %bitcast.22, f32[2,2,32,1024]{3,2,1,0:T(8,128)S(1)} %copy-done, f32[2,2,32,1024]{3,2,1,0:T(8,128)S(1)} %copy-done.1), kind=kLoop, calls=%fused_computation.2 | loop fusion | flops 262144 | bytes 2097152 | tf_op jit(solution)/shard_map/sub | solution.py:253
  30.5 0.1 slice_select_fusion
  30.5 0.1 multiply_bitcast_fusion
  30.6 0.8 %pad_maximum_fusion.send_ref = f32[8,8,2,8,128]{4,3,2,1,0:T(8,128)} fusion(f32[8,8,1,8,128]{4,3,2,1,0:T(8,128)S(1)} %get-tuple-element.13, f32[8,8,1,8,128]{4,3,2,1,0:T(8,128)S(1)} %get-tuple-element.12), kind=kLoop, calls=%fused_computation | loop fusion | flops 131072 | bytes 1048576 | tf_op jit(solution)/shard_map/stack | solution.py:258
  31.5 33.0 %shard_map.47 = f32[8,8,8,128]{3,2,1,0:T(8,128)} custom-call(f32[8,8,2,8,128]{4,3,2,1,0:T(8,128)} %pad_maximum_fusion.send_ref), custom_call_target="tpu_custom_call" | custom-call | tf_op jit(solution)/shard_map/pallas_call | solution.py:268
  64.5 1.1 %multiply_add_fusion = (f32[1,2,32,1024]{3,2,1,0:T(8,128)S(1)}, f32[1,2,32,1024]{3,2,1,0:T(8,128)S(1)}) fusion(f32[2,2,32,1024]{3,2,1,0:T(8,128)S(1)} %multiply_subtract_fusion, f32[2,2,32,1024]{3,2,1,0:T(8,128)S(1)} %copy-done, f32[1,2,32,1024]{3,2,1,0:T(8,128)S(1)} %get-tuple-element.8, f32[1,2,32,1024]{3,2,1,0:T(8,128)} %bitcast.23, pred[]{:T(512)S(6)} %and.17), kind=kLoop, calls=%fused_computation.9 | loop fusion | flops 458752 | bytes 2097153 | tf_op jit(solution)/shard_map/add | solution.py:291
  65.6 0.8 %pad_maximum_fusion.1 = f32[2,2,32,1024]{3,2,1,0:T(8,128)} fusion(f32[1,2,32,1024]{3,2,1,0:T(8,128)S(1)} %get-tuple-element.5, f32[1,2,32,1024]{3,2,1,0:T(8,128)S(1)} %get-tuple-element.6), kind=kLoop, calls=%fused_computation.1 | loop fusion | flops 131072 | bytes 1048576 | tf_op jit(solution)/shard_map/stack | solution.py:292
  (1 shorter events, 0.0 us)
Async XLA Ops:
  0.6 28.7 %copy-start = (f32[2,2,32,1024]{3,2,1,0:T(8,128)S(1)}, f32[2,2,32,1024]{3,2,1,0:T(8,128)}, u32[]{:S(2)}) copy-start(f32[2,2,32,1024]{3,2,1,0:T(8,128)} %param.5) | copy-start | bytes 1572868
  0.6 28.7 %copy-start.1 = (f32[2,2,32,1024]{3,2,1,0:T(8,128)S(1)}, f32[2,2,32,1024]{3,2,1,0:T(8,128)}, u32[]{:S(2)}) copy-start(f32[2,2,32,1024]{3,2,1,0:T(8,128)} %param.4) | copy-start | bytes 1572868

commit v10 on v9

--- a/solution.py
+++ b/solution.py
@@ -9,7 +9,7 @@
 HALO = M
 
 
-def fine_kernel(st_ref, dif_ref, frc_ref, keep_ref, out_ref, buf, dbuf, fbuf, sems):
+def fine_kernel(st_ref, dif_ref, frc_ref, keep_ref, cd_ref, tiles_ref, shift_ref, buf, dbuf, fbuf, sems):
     n_state = st_ref.shape[0]
     own = st_ref.shape[1]
     cols = st_ref.shape[2]
@@ -121,7 +121,26 @@
     half = M // 2
     lax.fori_loop(0, half, make_step(0, rows), 0)
     lax.fori_loop(0, M - half, make_step(half, rows - half), 0)
-    out_ref[...] = buf[:, HALO:HALO + own, :]
+    anchor = (lax.axis_index("tz") == 0) & (lax.axis_index("tq") == 0)
+    comps = n_state // 2
+    blocks = own // 8
+    for comp in range(comps):
+        d0, d1 = cd_ref[comp], cd_ref[comps + comp]
+        c0, c1 = st_ref[comp], st_ref[comps + comp]
+        plain0 = buf[comp, HALO:HALO + own] - d0 * c0
+        sh1 = buf[comps + comp, HALO:HALO + own] - d1 * c1
+        sh0 = jnp.where(anchor, d0 * c0 + plain0, plain0)
+        s0 = jnp.where(anchor, 0.0, d0)
+        shift_ref[comp] = sh0
+        shift_ref[comps + comp] = sh1
+        comp_scale = d1 * s0
+        comp_shift = d1 * sh0 + sh1
+        for rb in range(blocks):
+            for cb in range(cols // 128):
+                p = (comp * blocks + rb) * (cols // 128) + cb
+                rs, cs = slice(rb * 8, rb * 8 + 8), slice(cb * 128, cb * 128 + 128)
+                tiles_ref[p, 0] = comp_scale[rs, cs]
+                tiles_ref[p, 1] = comp_shift[rs, cs]
 
 
 def exchange_kernel(send_ref, out_ref, recv1, pa, pb, gsend, recv2, xg, back2, xs, back1, sems):
@@ -208,12 +227,6 @@
     out_ref[...] = back1[...]
 
 
-def to_tiles(block):
-    rows, cols = block.shape[-2] * block.shape[-3], block.shape[-1]
-    flat = block.reshape(rows // 8, 8, cols // 128, 128)
-    return flat.transpose(0, 2, 1, 3).reshape(-1, 8, 128)
-
-
 def from_tiles(tiles, shape):
     rows, cols = shape[0] * shape[1], shape[2]
     grid = tiles.reshape(rows // 8, cols // 128, 8, 128)
@@ -225,9 +238,6 @@
     space_count = lax.axis_size("space")
     me = lax.axis_index("space")
 
-    at_anchor = (lax.axis_index("tz") == 0) & (lax.axis_index("tq") == 0)
-    scale0 = jnp.where(at_anchor, 0.0, coarse_decay[0])
-    comp_scale = coarse_decay[1] * scale0
 
     state = coarse_points.reshape(slots * comps, row_count, col_count)
     ext_rows = row_count + 2 * HALO
@@ -235,11 +245,15 @@
     keep = ((global_row >= 0) & (global_row < space_count * row_count)).astype(jnp.float32)
 
     vmem = pl.BlockSpec(memory_space=pltpu.VMEM)
-    fine_end = pl.pallas_call(
+    tile_count = slots * comps * row_count * col_count // (2 * 8 * 128)
+    both, shifts = pl.pallas_call(
         fine_kernel,
-        out_shape=jax.ShapeDtypeStruct((slots * comps, row_count, col_count), jnp.float32),
-        in_specs=[vmem] * 4,
-        out_specs=vmem,
+        out_shape=(
+            jax.ShapeDtypeStruct((tile_count, 2, 8, 128), jnp.float32),
+            jax.ShapeDtypeStruct((slots * comps, row_count, col_count), jnp.float32),
+        ),
+        in_specs=[vmem] * 5,
+        out_specs=(vmem, vmem),
         scratch_shapes=[
             pltpu.VMEM((slots * comps, ext_rows, col_count), jnp.float32),
             pltpu.VMEM((ext_rows, col_count), jnp.float32),
@@ -247,15 +261,13 @@
             pltpu.SemaphoreType.DMA((12,)),
         ],
         compiler_params=pltpu.CompilerParams(collective_id=1, has_side_effects=True),
-    )(state, diffusion, forcing, keep)
-    fine_end = fine_end.reshape(coarse_points.shape)
-
-    shift = fine_end - coarse_decay * coarse_points
+    )(state, diffusion, forcing, keep, coarse_decay.reshape(state.shape))
     scale = coarse_decay
-    shift0 = jnp.where(at_anchor, coarse_decay[0] * coarse_points[0] + shift[0], shift[0])
-    comp_shift = scale[1] * shift0 + shift[1]
-
-    both = jnp.stack([to_tiles(comp_scale), to_tiles(comp_shift)], axis=1)
+    at_anchor = (lax.axis_index("tz") == 0) & (lax.axis_index("tq") == 0)
+    scale0 = jnp.where(at_anchor, 0.0, coarse_decay[0])
+    shifts = shifts.reshape(coarse_points.shape)
+    shift0 = shifts[0]
+    shift = shifts
     tiles = both.shape[0]
     q_count = lax.axis_size("tq")
     z_count = lax.axis_size("tz")

time: 66.6 us -> 65.1 us (0.977)
  other arithmetic: 4.62 us -> 2.66 us
    sub x1 -> x0, other arithmetic: 1.13 us -> none  [per_device_body(): shift = fine_end - coarse_decay * coarse_points]
    another operation x2 -> x0, other arithmetic: 0.91 us -> none  [per_device_body(): both = jnp.stack([to_tiles(comp_scale), to_tiles(comp_shift)], axis=1)]
where the time goes in v10:
time: 65.1 us; the launch traced here: 65 us
  Pallas kernels  62.3 us (96%)
  other arithmetic  2.66 us (4%)
    pallas_call x1, Pallas kernels, per_device_body(): pl.pallas_call(exchange_kernel, out_shape=jax.ShapeDtypeStruct(x1, jnp.fl...  33.2 us
    pallas_call x1, Pallas kernels, per_device_body(): pl.pallas_call(fine_kernel, out_shape=(jax.ShapeDtypeStruct((tile_count,...  29.1 us

profile of v10, /device:TPU:1, one launch (start us, length us, event | category | flops | bytes accessed | tf_op | source)
XLA Modules:
  0.0 65.0 jit_solution(8359651024622143238)
XLA Ops:
  0.0 0.6 fusion.3.keep_ref
  0.6 29.1 %shard_map.46 = (f32[64,2,8,128]{3,2,1,0:T(8,128)}, f32[4,32,1024]{2,1,0:T(8,128)}) custom-call(f32[4,32,1024]{2,1,0:T(8,128)} %bitcast.13, f32[32,1024]{1,0:T(8,128)} %dif_ref.1, f32[2,32,1024]{2,1,0:T(8,128)} %frc_ref.1, f32[64,1]{1,0:T(8,128)} %fusion.3.keep_ref, f32[4,32,1024]{2,1,0:T(8,128)} %bitcast.11), custom_call_target="tpu_custom_call" | custom-call | tf_op jit(solution)/shard_map/pallas_call | solution.py:249
  29.7 0.0 copy-start
  29.7 33.2 %shard_map.47 = f32[8,8,8,128]{3,2,1,0:T(8,128)} custom-call(f32[8,8,2,8,128]{4,3,2,1,0:T(8,128)} %bitcast.14), custom_call_target="tpu_custom_call" | custom-call | tf_op jit(solution)/shard_map/pallas_call | solution.py:280
  62.9 0.0 copy-done
  62.9 1.2 %bitcast_add_fusion = (f32[1,2,32,1024]{3,2,1,0:T(8,128)S(1)}, f32[1,2,32,1024]{3,2,1,0:T(8,128)S(1)}) fusion(f32[4,32,1024]{2,1,0:T(8,128)} %get-tuple-element.8, f32[2,2,32,1024]{3,2,1,0:T(8,128)S(1)} %copy-done, f32[1,2,32,1024]{3,2,1,0:T(8,128)} %bitcast.12, pred[]{:T(512)S(6)} %and.17), kind=kLoop, calls=%fused_computation.1 | loop fusion | flops 327680 | bytes 1835009 | tf_op jit(solution)/shard_map/add | solution.py:303
  64.1 0.8 %pad_maximum_fusion = f32[2,2,32,1024]{3,2,1,0:T(8,128)} fusion(f32[1,2,32,1024]{3,2,1,0:T(8,128)S(1)} %get-tuple-element.9, f32[1,2,32,1024]{3,2,1,0:T(8,128)S(1)} %get-tuple-element.10), kind=kLoop, calls=%fused_computation | loop fusion | flops 131072 | bytes 1048576 | tf_op jit(solution)/shard_map/stack | solution.py:304
Async XLA Ops:
  29.7 33.2 %copy-start = (f32[2,2,32,1024]{3,2,1,0:T(8,128)S(1)}, f32[2,2,32,1024]{3,2,1,0:T(8,128)}, u32[]{:S(2)}) copy-start(f32[2,2,32,1024]{3,2,1,0:T(8,128)} %param.5) | copy-start | bytes 1572868

commit v11 on v10

--- a/solution.py
+++ b/solution.py
@@ -143,7 +143,7 @@
                 tiles_ref[p, 1] = comp_shift[rs, cs]
 
 
-def exchange_kernel(send_ref, out_ref, recv1, pa, pb, gsend, recv2, xg, back2, xs, back1, sems):
+def exchange_kernel(send_ref, cd_ref, sh_ref, out_ref, recv1, pa, pb, gsend, recv2, xg, back2, xs, back1, sems):
     nq = send_ref.shape[0]
     nz = gsend.shape[0]
     mz = lax.axis_index("tz")
@@ -224,13 +224,23 @@
 
     lax.fori_loop(0, nq, spread_step, 0)
     exchange(3, xs, back1, nq, mq, in_plane)
-    out_ref[...] = back1[...]
-
-
-def from_tiles(tiles, shape):
-    rows, cols = shape[0] * shape[1], shape[2]
-    grid = tiles.reshape(rows // 8, cols // 128, 8, 128)
-    return grid.transpose(0, 2, 1, 3).reshape(shape)
+    anchor = (mz == 0) & (mq == 0)
+    n_state, own, cols = cd_ref.shape
+    comps = n_state // 2
+    blocks = own // 8
+    c1 = back1.shape[1]
+    for comp in range(comps):
+        for rb in range(blocks):
+            for cb in range(cols // 128):
+                p = (comp * blocks + rb) * (cols // 128) + cb
+                rs, cs = pl.ds(rb * 8, 8), pl.ds(cb * 128, 128)
+                entering = back1[p // c1, p % c1]
+                s0 = jnp.where(anchor, 0.0, cd_ref[comp, rs, cs])
+                first = s0 * entering + sh_ref[comp, rs, cs]
+                out_ref[comp, rs, cs] = first
+                out_ref[comps + comp, rs, cs] = (
+                    cd_ref[comps + comp, rs, cs] * first + sh_ref[comps + comp, rs, cs]
+                )
 
 
 def per_device_body(coarse_points, coarse_decay, diffusion, forcing):
@@ -262,12 +272,9 @@
         ],
         compiler_params=pltpu.CompilerParams(collective_id=1, has_side_effects=True),
     )(state, diffusion, forcing, keep, coarse_decay.reshape(state.shape))
-    scale = coarse_decay
     at_anchor = (lax.axis_index("tz") == 0) & (lax.axis_index("tq") == 0)
     scale0 = jnp.where(at_anchor, 0.0, coarse_decay[0])
     shifts = shifts.reshape(coarse_points.shape)
-    shift0 = shifts[0]
-    shift = shifts
     tiles = both.shape[0]
     q_count = lax.axis_size("tq")
     z_count = lax.axis_size("tz")
@@ -277,10 +284,10 @@
     x1 = (q_count, c1, 8, 128)
     x2 = (z_count, c2, 8, 128)
     vmem = pl.BlockSpec(memory_space=pltpu.VMEM)
-    back = pl.pallas_call(
+    updated = pl.pallas_call(
         exchange_kernel,
-        out_shape=jax.ShapeDtypeStruct(x1, jnp.float32),
-        in_specs=[vmem],
+        out_shape=jax.ShapeDtypeStruct(state.shape, jnp.float32),
+        in_specs=[vmem] * 3,
         out_specs=vmem,
         scratch_shapes=[
             pltpu.VMEM(both.shape, jnp.float32),
@@ -295,13 +302,8 @@
             pltpu.SemaphoreType.DMA((8, max(q_count, z_count))),
         ],
         compiler_params=pltpu.CompilerParams(collective_id=0, has_side_effects=True),
-    )(both)
-    back = back.reshape(tiles, 8, 128)
-    entering = from_tiles(back, (comps, row_count, col_count))
-
-    first = scale0 * entering + shift0
-    second = scale[1] * first + shift[1]
-    return jnp.stack([first, second], axis=0)
+    )(both, coarse_decay.reshape(state.shape), shifts.reshape(state.shape))
+    return updated.reshape(coarse_points.shape)
 
 
 def solution(mesh):

time: 65.1 us -> 65.4 us (level)
  other arithmetic: 2.66 us -> 0.62 us
  local copies, waits for them, and re-layouts: 0.01 us -> 1.89 us
    unnamed x2 -> x1, local copies, waits for them, and re-layouts: 0.01 us -> 1.89 us
    add x1 -> x0, other arithmetic: 1.19 us -> none  [per_device_body(): second = scale[1] * first + shift[1]]
    another operation x1 -> x0, other arithmetic: 0.84 us -> none  [per_device_body(): return jnp.stack([first, second], axis=0)]
where the time goes in v11:
time: 65.4 us; the launch traced here: 65.3 us
  Pallas kernels  62.7 us (96%)
  local copies, waits for them, and re-layouts  1.89 us (3%)
    pallas_call x1, Pallas kernels, per_device_body(): pl.pallas_call(exchange_kernel, out_shape=jax.ShapeDtypeStruct(state.shap...  33.6 us
    pallas_call x1, Pallas kernels, per_device_body(): pl.pallas_call(fine_kernel, out_shape=(jax.ShapeDtypeStruct((tile_count,...  29.1 us
    unnamed x1, local copies, waits for them, and re-layouts  1.89 us

profile of v11, /device:TPU:1, one launch (start us, length us, event | category | flops | bytes accessed | tf_op | source)
XLA Modules:
  0.0 65.3 jit_solution(11728625551103249461)
XLA Ops:
  0.0 0.6 fusion.3.keep_ref
  0.6 29.1 %shard_map.46 = (f32[64,2,8,128]{3,2,1,0:T(8,128)}, f32[4,32,1024]{2,1,0:T(8,128)}) custom-call(f32[4,32,1024]{2,1,0:T(8,128)} %bitcast.7, f32[32,1024]{1,0:T(8,128)} %dif_ref.1, f32[2,32,1024]{2,1,0:T(8,128)} %frc_ref.1, f32[64,1]{1,0:T(8,128)} %fusion.3.keep_ref, f32[4,32,1024]{2,1,0:T(8,128)} %bitcast.4), custom_call_target="tpu_custom_call" | custom-call | tf_op jit(solution)/shard_map/pallas_call | solution.py:259
  29.7 33.6 %shard_map.47 = f32[4,32,1024]{2,1,0:T(8,128)} custom-call(f32[8,8,2,8,128]{4,3,2,1,0:T(8,128)} %bitcast.8, f32[4,32,1024]{2,1,0:T(8,128)} %bitcast.5, f32[4,32,1024]{2,1,0:T(8,128)} %get-tuple-element.8.sh_ref), custom_call_target="tpu_custom_call" | custom-call | tf_op jit(solution)/shard_map/pallas_call | solution.py:287
  63.4 1.9 %copy.7 = f32[2,2,32,1024]{3,2,1,0:T(8,128)} copy(f32[2,2,32,1024]{3,2,1,0:T(8,128)} %bitcast.6) | data formatting | bytes 1048576

commit v12 on v10

--- a/solution.py
+++ b/solution.py
@@ -204,19 +204,15 @@
 
     ones = jnp.ones(pa.shape[1:], jnp.float32)
     ga, gb = lax.fori_loop(0, nq, group_step, (ones, jnp.zeros_like(ones)))
-    c2 = gsend.shape[1]
     for z in range(nz):
-        gsend[z, :, 0] = ga[z * c2:(z + 1) * c2]
-        gsend[z, :, 1] = gb[z * c2:(z + 1) * c2]
+        gsend[z, :, 0] = ga
+        gsend[z, :, 1] = gb
     exchange(1, gsend, recv2, nz, mz, across)
 
     def entry_step(s, x):
-        xg[s] = x
-        return recv2[s, :, 0] * x + recv2[s, :, 1]
-
-    lax.fori_loop(0, nz, entry_step, jnp.zeros(xg.shape[1:], jnp.float32))
-    exchange(2, xg, back2, nz, mz, across)
-    group_in = back2[...].reshape(pa.shape[1:])
+        return jnp.where(s < mz, recv2[s, :, 0] * x + recv2[s, :, 1], x)
+
+    group_in = lax.fori_loop(0, nz, entry_step, jnp.zeros(pa.shape[1:], jnp.float32))
 
     def spread_step(s, carry):
         xs[s] = pa[s] * group_in + pb[s]
@@ -286,8 +282,8 @@
             pltpu.VMEM(both.shape, jnp.float32),
             pltpu.VMEM(x1, jnp.float32),
             pltpu.VMEM(x1, jnp.float32),
-            pltpu.VMEM((z_count, c2, 2, 8, 128), jnp.float32),
-            pltpu.VMEM((z_count, c2, 2, 8, 128), jnp.float32),
+            pltpu.VMEM((z_count, c1, 2, 8, 128), jnp.float32),
+            pltpu.VMEM((z_count, c1, 2, 8, 128), jnp.float32),
             pltpu.VMEM(x2, jnp.float32),
             pltpu.VMEM(x2, jnp.float32),
             pltpu.VMEM(x1, jnp.float32),

time: 65.1 us -> 71.1 us (1.092)
  Pallas kernels: 62.3 us -> 68.3 us
    pallas_call x1, Pallas kernels: 33.2 us -> 39.2 us  [per_device_body(): pl.pallas_call(exchange_kernel, out_shape=jax.ShapeDtypeStruct(x1, jnp.fl...]
where the time goes in v12:
time: 71.1 us; the launch traced here: 71 us
  Pallas kernels  68.3 us (96%)
  other arithmetic  2.66 us (4%)
    pallas_call x1, Pallas kernels, per_device_body(): pl.pallas_call(exchange_kernel, out_shape=jax.ShapeDtypeStruct(x1, jnp.fl...  39.2 us
    pallas_call x1, Pallas kernels, per_device_body(): pl.pallas_call(fine_kernel, out_shape=(jax.ShapeDtypeStruct((tile_count,...  29.1 us

profile of v12, /device:TPU:1, one launch (start us, length us, event | category | flops | bytes accessed | tf_op | source)
XLA Modules:
  0.0 71.0 jit_solution(6977722013381342001)
XLA Ops:
  0.0 0.6 fusion.3.keep_ref
  0.6 29.1 %shard_map.46 = (f32[64,2,8,128]{3,2,1,0:T(8,128)}, f32[4,32,1024]{2,1,0:T(8,128)}) custom-call(f32[4,32,1024]{2,1,0:T(8,128)} %bitcast.13, f32[32,1024]{1,0:T(8,128)} %dif_ref.1, f32[2,32,1024]{2,1,0:T(8,128)} %frc_ref.1, f32[64,1]{1,0:T(8,128)} %fusion.3.keep_ref, f32[4,32,1024]{2,1,0:T(8,128)} %bitcast.11), custom_call_target="tpu_custom_call" | custom-call | tf_op jit(solution)/shard_map/pallas_call | solution.py:245
  29.7 0.0 copy-start
  29.7 39.2 %shard_map.47 = f32[8,8,8,128]{3,2,1,0:T(8,128)} custom-call(f32[8,8,2,8,128]{4,3,2,1,0:T(8,128)} %bitcast.14), custom_call_target="tpu_custom_call" | custom-call | tf_op jit(solution)/shard_map/pallas_call | solution.py:276
  68.9 0.0 copy-done
  68.9 1.2 %bitcast_add_fusion = (f32[1,2,32,1024]{3,2,1,0:T(8,128)S(1)}, f32[1,2,32,1024]{3,2,1,0:T(8,128)S(1)}) fusion(f32[4,32,1024]{2,1,0:T(8,128)} %get-tuple-element.8, f32[2,2,32,1024]{3,2,1,0:T(8,128)S(1)} %copy-done, f32[1,2,32,1024]{3,2,1,0:T(8,128)} %bitcast.12, pred[]{:T(512)S(6)} %and.17), kind=kLoop, calls=%fused_computation.1 | loop fusion | flops 327680 | bytes 1835009 | tf_op jit(solution)/shard_map/add | solution.py:299
  70.1 0.8 %pad_maximum_fusion = f32[2,2,32,1024]{3,2,1,0:T(8,128)} fusion(f32[1,2,32,1024]{3,2,1,0:T(8,128)S(1)} %get-tuple-element.9, f32[1,2,32,1024]{3,2,1,0:T(8,128)S(1)} %get-tuple-element.10), kind=kLoop, calls=%fused_computation | loop fusion | flops 131072 | bytes 1048576 | tf_op jit(solution)/shard_map/stack | solution.py:300
Async XLA Ops:
  29.7 39.2 %copy-start = (f32[2,2,32,1024]{3,2,1,0:T(8,128)S(1)}, f32[2,2,32,1024]{3,2,1,0:T(8,128)}, u32[]{:S(2)}) copy-start(f32[2,2,32,1024]{3,2,1,0:T(8,128)} %param.5) | copy-start | bytes 1572868

commit v13 on v10

--- a/solution.py
+++ b/solution.py
@@ -9,7 +9,7 @@
 HALO = M
 
 
-def fine_kernel(st_ref, dif_ref, frc_ref, keep_ref, cd_ref, tiles_ref, shift_ref, buf, dbuf, fbuf, sems):
+def fine_body(st_ref, dif_ref, frc_ref, keep_ref, cd_ref, tiles_ref, shift_ref, buf, dbuf, fbuf, sems):
     n_state = st_ref.shape[0]
     own = st_ref.shape[1]
     cols = st_ref.shape[2]
@@ -19,23 +19,6 @@
     place = (lax.axis_index("tz"), lax.axis_index("tq"))
     mesh_id = pl.DeviceIdType.MESH
     pairs = ((st_ref, buf), (dif_ref, dbuf), (frc_ref, fbuf))
-    barrier = pltpu.get_barrier_semaphore()
-
-    @pl.when(me > 0)
-    def _():
-        pl.semaphore_signal(barrier, 1, device_id=place + (me - 1,), device_id_type=mesh_id)
-
-    @pl.when(me < n - 1)
-    def _():
-        pl.semaphore_signal(barrier, 1, device_id=place + (me + 1,), device_id_type=mesh_id)
-
-    @pl.when((me > 0) & (me < n - 1))
-    def _():
-        pl.semaphore_wait(barrier, 2)
-
-    @pl.when((me == 0) | (me == n - 1))
-    def _():
-        pl.semaphore_wait(barrier, 1)
 
     def rim_copy(k, src, dst, down, target):
         if down:
@@ -139,11 +122,12 @@
             for cb in range(cols // 128):
                 p = (comp * blocks + rb) * (cols // 128) + cb
                 rs, cs = slice(rb * 8, rb * 8 + 8), slice(cb * 128, cb * 128 + 128)
-                tiles_ref[p, 0] = comp_scale[rs, cs]
-                tiles_ref[p, 1] = comp_shift[rs, cs]
-
-
-def exchange_kernel(send_ref, out_ref, recv1, pa, pb, gsend, recv2, xg, back2, xs, back1, sems):
+                c1 = tiles_ref.shape[1]
+                tiles_ref[p // c1, p % c1, 0] = comp_scale[rs, cs]
+                tiles_ref[p // c1, p % c1, 1] = comp_shift[rs, cs]
+
+
+def exchange_body(send_ref, out_ref, recv1, pa, pb, gsend, recv2, xg, back2, xs, back1, sems):
     nq = send_ref.shape[0]
     nz = gsend.shape[0]
     mz = lax.axis_index("tz")
@@ -183,16 +167,6 @@
 
     in_plane = lambda d: (mz, d, sp)
     across = lambda d: (d, mq, sp)
-    barrier = pltpu.get_barrier_semaphore()
-    for k in range(1, nq):
-        pl.semaphore_signal(
-            barrier, 1, device_id=in_plane(lax.rem(mq + k, nq)), device_id_type=mesh_id
-        )
-    for k in range(1, nz):
-        pl.semaphore_signal(
-            barrier, 1, device_id=across(lax.rem(mz + k, nz)), device_id_type=mesh_id
-        )
-    pl.semaphore_wait(barrier, nq + nz - 2)
     exchange(0, send_ref, recv1, nq, mq, in_plane)
 
     def group_step(s, carry):
@@ -227,6 +201,47 @@
     out_ref[...] = back1[...]
 
 
+def whole_kernel(st_ref, dif_ref, frc_ref, keep_ref, cd_ref, shift_ref, x_ref,
+                 buf, dbuf, fbuf, fsems, send, recv1, pa, pb, gsend, recv2, xg, back2, xs, back1, xsems):
+    n = lax.axis_size("space")
+    me = lax.axis_index("space")
+    mz = lax.axis_index("tz")
+    mq = lax.axis_index("tq")
+    nq = lax.axis_size("tq")
+    nz = lax.axis_size("tz")
+    mesh_id = pl.DeviceIdType.MESH
+    barrier = pltpu.get_barrier_semaphore()
+
+    @pl.when(me > 0)
+    def _():
+        pl.semaphore_signal(barrier, 1, device_id=(mz, mq, me - 1), device_id_type=mesh_id)
+
+    @pl.when(me < n - 1)
+    def _():
+        pl.semaphore_signal(barrier, 1, device_id=(mz, mq, me + 1), device_id_type=mesh_id)
+
+    for k in range(1, nq):
+        pl.semaphore_signal(
+            barrier, 1, device_id=(mz, lax.rem(mq + k, nq), me), device_id_type=mesh_id
+        )
+    for k in range(1, nz):
+        pl.semaphore_signal(
+            barrier, 1, device_id=(lax.rem(mz + k, nz), mq, me), device_id_type=mesh_id
+        )
+    peers = nq + nz - 2
+
+    @pl.when((me > 0) & (me < n - 1))
+    def _():
+        pl.semaphore_wait(barrier, peers + 2)
+
+    @pl.when((me == 0) | (me == n - 1))
+    def _():
+        pl.semaphore_wait(barrier, peers + 1)
+
+    fine_body(st_ref, dif_ref, frc_ref, keep_ref, cd_ref, send, shift_ref, buf, dbuf, fbuf, fsems)
+    exchange_body(send, x_ref, recv1, pa, pb, gsend, recv2, xg, back2, xs, back1, xsems)
+
+
 def from_tiles(tiles, shape):
     rows, cols = shape[0] * shape[1], shape[2]
     grid = tiles.reshape(rows // 8, cols // 128, 8, 128)
@@ -245,12 +260,19 @@
     keep = ((global_row >= 0) & (global_row < space_count * row_count)).astype(jnp.float32)
 
     vmem = pl.BlockSpec(memory_space=pltpu.VMEM)
-    tile_count = slots * comps * row_count * col_count // (2 * 8 * 128)
-    both, shifts = pl.pallas_call(
-        fine_kernel,
+    tiles = slots * comps * row_count * col_count // (2 * 8 * 128)
+    q_count = lax.axis_size("tq")
+    z_count = lax.axis_size("tz")
+    c1 = tiles // q_count
+    c2 = c1 // z_count
+    x1 = (q_count, c1, 8, 128)
+    x2 = (z_count, c2, 8, 128)
+    send_shape = (q_count, c1, 2, 8, 128)
+    shifts, back = pl.pallas_call(
+        whole_kernel,
         out_shape=(
-            jax.ShapeDtypeStruct((tile_count, 2, 8, 128), jnp.float32),
             jax.ShapeDtypeStruct((slots * comps, row_count, col_count), jnp.float32),
+            jax.ShapeDtypeStruct(x1, jnp.float32),
         ),
         in_specs=[vmem] * 5,
         out_specs=(vmem, vmem),
@@ -259,31 +281,8 @@
             pltpu.VMEM((ext_rows, col_count), jnp.float32),
             pltpu.VMEM((comps, ext_rows, col_count), jnp.float32),
             pltpu.SemaphoreType.DMA((12,)),
-        ],
-        compiler_params=pltpu.CompilerParams(collective_id=1, has_side_effects=True),
-    )(state, diffusion, forcing, keep, coarse_decay.reshape(state.shape))
-    scale = coarse_decay
-    at_anchor = (lax.axis_index("tz") == 0) & (lax.axis_index("tq") == 0)
-    scale0 = jnp.where(at_anchor, 0.0, coarse_decay[0])
-    shifts = shifts.reshape(coarse_points.shape)
-    shift0 = shifts[0]
-    shift = shifts
-    tiles = both.shape[0]
-    q_count = lax.axis_size("tq")
-    z_count = lax.axis_size("tz")
-    c1 = tiles // q_count
-    c2 = c1 // z_count
-    both = both.reshape(q_count, c1, 2, 8, 128)
-    x1 = (q_count, c1, 8, 128)
-    x2 = (z_count, c2, 8, 128)
-    vmem = pl.BlockSpec(memory_space=pltpu.VMEM)
-    back = pl.pallas_call(
-        exchange_kernel,
-        out_shape=jax.ShapeDtypeStruct(x1, jnp.float32),
-        in_specs=[vmem],
-        out_specs=vmem,
-        scratch_shapes=[
-            pltpu.VMEM(both.shape, jnp.float32),
+            pltpu.VMEM(send_shape, jnp.float32),
+            pltpu.VMEM(send_shape, jnp.float32),
             pltpu.VMEM(x1, jnp.float32),
             pltpu.VMEM(x1, jnp.float32),
             pltpu.VMEM((z_count, c2, 2, 8, 128), jnp.float32),
@@ -295,7 +294,13 @@
             pltpu.SemaphoreType.DMA((8, max(q_count, z_count))),
         ],
         compiler_params=pltpu.CompilerParams(collective_id=0, has_side_effects=True),
-    )(both)
+    )(state, diffusion, forcing, keep, coarse_decay.reshape(state.shape))
+    scale = coarse_decay
+    at_anchor = (lax.axis_index("tz") == 0) & (lax.axis_index("tq") == 0)
+    scale0 = jnp.where(at_anchor, 0.0, coarse_decay[0])
+    shifts = shifts.reshape(coarse_points.shape)
+    shift0 = shifts[0]
+    shift = shifts
     back = back.reshape(tiles, 8, 128)
     entering = from_tiles(back, (comps, row_count, col_count))
 

time: 65.1 us -> 62.1 us (0.954)
  Pallas kernels: 62.3 us -> 59.3 us
    pallas_call x2 -> x1, Pallas kernels: 62.3 us -> 59.3 us  [per_device_body(): pl.pallas_call(whole_kernel, out_shape=(jax.ShapeDtypeStruct((slots * com...]
where the time goes in v13:
time: 62.1 us; the launch traced here: 61.9 us
  Pallas kernels  59.3 us (95%)
  other arithmetic  2.66 us (4%)
    pallas_call x1, Pallas kernels, per_device_body(): pl.pallas_call(whole_kernel, out_shape=(jax.ShapeDtypeStruct((slots * com...  59.3 us

profile of v13, /device:TPU:1, one launch (start us, length us, event | category | flops | bytes accessed | tf_op | source)
XLA Modules:
  0.0 61.9 jit_solution(10964327309100063912)
XLA Ops:
  0.0 0.6 %fusion.3.keep_ref = f32[64,1]{1,0:T(8,128)} fusion(s32[]{:T(128)S(6)} %sub.3), kind=kLoop, calls=%fused_computation.7 | loop fusion | flops 320 | bytes 260 | tf_op jit(solution)/shard_map/convert_element_type | solution.py:260
  0.6 0.0 copy-start
  0.6 59.3 %shard_map.46 = (f32[4,32,1024]{2,1,0:T(8,128)}, f32[8,8,8,128]{3,2,1,0:T(8,128)}) custom-call(f32[4,32,1024]{2,1,0:T(8,128)} %bitcast.11, f32[32,1024]{1,0:T(8,128)} %dif_ref.1, f32[2,32,1024]{2,1,0:T(8,128)} %frc_ref.1, f32[64,1]{1,0:T(8,128)} %fusion.3.keep_ref, f32[4,32,1024]{2,1,0:T(8,128)} %bitcast.10), custom_call_target="tpu_custom_call" | custom-call | tf_op jit(solution)/shard_map/pallas_call | solution.py:271
  59.9 0.0 copy-done
  59.9 1.2 %bitcast_add_fusion = (f32[1,2,32,1024]{3,2,1,0:T(8,128)S(1)}, f32[1,2,32,1024]{3,2,1,0:T(8,128)S(1)}) fusion(f32[4,32,1024]{2,1,0:T(8,128)} %get-tuple-element.8, f32[2,2,32,1024]{3,2,1,0:T(8,128)S(1)} %copy-done, f32[1,2,32,1024]{3,2,1,0:T(8,128)} %bitcast.12, pred[]{:T(512)S(6)} %and.17), kind=kLoop, calls=%fused_computation.1 | loop fusion | flops 327680 | bytes 1835009 | tf_op jit(solution)/shard_map/add | solution.py:308
  61.1 0.8 %pad_maximum_fusion = f32[2,2,32,1024]{3,2,1,0:T(8,128)} fusion(f32[1,2,32,1024]{3,2,1,0:T(8,128)S(1)} %get-tuple-element.9, f32[1,2,32,1024]{3,2,1,0:T(8,128)S(1)} %get-tuple-element.10), kind=kLoop, calls=%fused_computation | loop fusion | flops 131072 | bytes 1048576 | tf_op jit(solution)/shard_map/stack | solution.py:309
Async XLA Ops:
  0.6 59.3 %copy-start = (f32[2,2,32,1024]{3,2,1,0:T(8,128)S(1)}, f32[2,2,32,1024]{3,2,1,0:T(8,128)}, u32[]{:S(2)}) copy-start(f32[2,2,32,1024]{3,2,1,0:T(8,128)} %param.5) | copy-start | bytes 1572868

commit v14 on v13

--- a/solution.py
+++ b/solution.py
@@ -113,21 +113,18 @@
         plain0 = buf[comp, HALO:HALO + own] - d0 * c0
         sh1 = buf[comps + comp, HALO:HALO + own] - d1 * c1
         sh0 = jnp.where(anchor, d0 * c0 + plain0, plain0)
-        s0 = jnp.where(anchor, 0.0, d0)
         shift_ref[comp] = sh0
         shift_ref[comps + comp] = sh1
-        comp_scale = d1 * s0
         comp_shift = d1 * sh0 + sh1
         for rb in range(blocks):
             for cb in range(cols // 128):
                 p = (comp * blocks + rb) * (cols // 128) + cb
                 rs, cs = slice(rb * 8, rb * 8 + 8), slice(cb * 128, cb * 128 + 128)
                 c1 = tiles_ref.shape[1]
-                tiles_ref[p // c1, p % c1, 0] = comp_scale[rs, cs]
                 tiles_ref[p // c1, p % c1, 1] = comp_shift[rs, cs]
 
 
-def exchange_body(send_ref, out_ref, recv1, pa, pb, gsend, recv2, xg, back2, xs, back1, sems):
+def exchange_body(send_ref, out_ref, recv1, pa, pb, gsend, recv2, xg, back2, xs, back1, sems, first=True):
     nq = send_ref.shape[0]
     nz = gsend.shape[0]
     mz = lax.axis_index("tz")
@@ -167,7 +164,8 @@
 
     in_plane = lambda d: (mz, d, sp)
     across = lambda d: (d, mq, sp)
-    exchange(0, send_ref, recv1, nq, mq, in_plane)
+    if first:
+        exchange(0, send_ref, recv1, nq, mq, in_plane)
 
     def group_step(s, carry):
         ga, gb = carry
@@ -238,8 +236,50 @@
     def _():
         pl.semaphore_wait(barrier, peers + 1)
 
+    def half_copy(h, d_src, d_dst, peer):
+        return pltpu.make_async_remote_copy(
+            src_ref=send.at[d_src, :, h], dst_ref=recv1.at[d_dst, :, h],
+            send_sem=xsems.at[8 + 2 * h, d_src], recv_sem=xsems.at[9 + 2 * h, d_dst],
+            device_id=(mz, peer, me), device_id_type=mesh_id,
+        )
+
+    def start_half(h):
+        def start(k, carry):
+            d = lax.rem(mq + k, nq)
+            half_copy(h, d, mq, d).start()
+            return carry
+
+        lax.fori_loop(1, nq, start, 0)
+        recv1[mq, :, h] = send[mq, :, h]
+
+    def wait_half(h):
+        def wait(k, carry):
+            d = lax.rem(mq + k, nq)
+            half_copy(h, d, mq, d).wait_send()
+            half_copy(h, d, d, d).wait_recv()
+            return carry
+
+        lax.fori_loop(1, nq, wait, 0)
+
+    anchor = (mz == 0) & (mq == 0)
+    n_state, own, cols = cd_ref.shape
+    comps = n_state // 2
+    blocks = own // 8
+    c1 = send.shape[1]
+    for comp in range(comps):
+        s0 = jnp.where(anchor, 0.0, cd_ref[comp])
+        comp_scale = cd_ref[comps + comp] * s0
+        for rb in range(blocks):
+            for cb in range(cols // 128):
+                p = (comp * blocks + rb) * (cols // 128) + cb
+                rs, cs = slice(rb * 8, rb * 8 + 8), slice(cb * 128, cb * 128 + 128)
+                send[p // c1, p % c1, 0] = comp_scale[rs, cs]
+    start_half(0)
     fine_body(st_ref, dif_ref, frc_ref, keep_ref, cd_ref, send, shift_ref, buf, dbuf, fbuf, fsems)
-    exchange_body(send, x_ref, recv1, pa, pb, gsend, recv2, xg, back2, xs, back1, xsems)
+    start_half(1)
+    wait_half(0)
+    wait_half(1)
+    exchange_body(send, x_ref, recv1, pa, pb, gsend, recv2, xg, back2, xs, back1, xsems, first=False)
 
 
 def from_tiles(tiles, shape):
@@ -291,7 +331,7 @@
             pltpu.VMEM(x2, jnp.float32),
             pltpu.VMEM(x1, jnp.float32),
             pltpu.VMEM(x1, jnp.float32),
-            pltpu.SemaphoreType.DMA((8, max(q_count, z_count))),
+            pltpu.SemaphoreType.DMA((12, max(q_count, z_count))),
         ],
         compiler_params=pltpu.CompilerParams(collective_id=0, has_side_effects=True),
     )(state, diffusion, forcing, keep, coarse_decay.reshape(state.shape))

time: 62.1 us -> 60 us (0.966)
  Pallas kernels: 59.3 us -> 57.2 us
    pallas_call x1, Pallas kernels: 59.3 us -> 57.2 us  [per_device_body(): pl.pallas_call(whole_kernel, out_shape=(jax.ShapeDtypeStruct((slots * com...]
where the time goes in v14:
time: 60 us; the launch traced here: 59.9 us
  Pallas kernels  57.2 us (95%)
  other arithmetic  2.66 us (4%)
    pallas_call x1, Pallas kernels, per_device_body(): pl.pallas_call(whole_kernel, out_shape=(jax.ShapeDtypeStruct((slots * com...  57.2 us

profile of v14, /device:TPU:1, one launch (start us, length us, event | category | flops | bytes accessed | tf_op | source)
XLA Modules:
  0.0 59.9 jit_solution(3213876028881868695)
XLA Ops:
  0.0 0.6 %fusion.3.keep_ref = f32[64,1]{1,0:T(8,128)} fusion(s32[]{:T(128)S(6)} %sub.3), kind=kLoop, calls=%fused_computation.7 | loop fusion | flops 320 | bytes 260 | tf_op jit(solution)/shard_map/convert_element_type | solution.py:300
  0.6 0.0 copy-start
  0.6 57.2 %shard_map.46 = (f32[4,32,1024]{2,1,0:T(8,128)}, f32[8,8,8,128]{3,2,1,0:T(8,128)}) custom-call(f32[4,32,1024]{2,1,0:T(8,128)} %bitcast.11, f32[32,1024]{1,0:T(8,128)} %dif_ref.1, f32[2,32,1024]{2,1,0:T(8,128)} %frc_ref.1, f32[64,1]{1,0:T(8,128)} %fusion.3.keep_ref, f32[4,32,1024]{2,1,0:T(8,128)} %bitcast.10), custom_call_target="tpu_custom_call" | custom-call | tf_op jit(solution)/shard_map/pallas_call | solution.py:311
  57.8 0.0 copy-done
  57.8 1.2 %bitcast_add_fusion = (f32[1,2,32,1024]{3,2,1,0:T(8,128)S(1)}, f32[1,2,32,1024]{3,2,1,0:T(8,128)S(1)}) fusion(f32[4,32,1024]{2,1,0:T(8,128)} %get-tuple-element.8, f32[2,2,32,1024]{3,2,1,0:T(8,128)S(1)} %copy-done, f32[1,2,32,1024]{3,2,1,0:T(8,128)} %bitcast.12, pred[]{:T(512)S(6)} %and.17), kind=kLoop, calls=%fused_computation.1 | loop fusion | flops 327680 | bytes 1835009 | tf_op jit(solution)/shard_map/add | solution.py:348
  59.0 0.8 %pad_maximum_fusion = f32[2,2,32,1024]{3,2,1,0:T(8,128)} fusion(f32[1,2,32,1024]{3,2,1,0:T(8,128)S(1)} %get-tuple-element.9, f32[1,2,32,1024]{3,2,1,0:T(8,128)S(1)} %get-tuple-element.10), kind=kLoop, calls=%fused_computation | loop fusion | flops 131072 | bytes 1048576 | tf_op jit(solution)/shard_map/stack | solution.py:349
Async XLA Ops:
  0.6 57.2 %copy-start = (f32[2,2,32,1024]{3,2,1,0:T(8,128)S(1)}, f32[2,2,32,1024]{3,2,1,0:T(8,128)}, u32[]{:S(2)}) copy-start(f32[2,2,32,1024]{3,2,1,0:T(8,128)} %param.5) | copy-start | bytes 1572868

commit v15 on v14

--- a/solution.py
+++ b/solution.py
@@ -9,7 +9,7 @@
 HALO = M
 
 
-def fine_body(st_ref, dif_ref, frc_ref, keep_ref, cd_ref, tiles_ref, shift_ref, buf, dbuf, fbuf, sems):
+def fine_body(st_ref, dif_ref, frc_ref, keep_ref, cd_ref, tiles_ref, shift_ref, buf, dbuf, fbuf, sems, early=None):
     n_state = st_ref.shape[0]
     own = st_ref.shape[1]
     cols = st_ref.shape[2]
@@ -45,6 +45,8 @@
         for k, (src, dst) in enumerate(pairs):
             rim_copy(k, src, dst, False, me - 1).start()
 
+    if early is not None:
+        early()
     buf[:, HALO:HALO + own] = st_ref[...]
     dbuf[HALO:HALO + own] = dif_ref[...]
     fbuf[:, HALO:HALO + own] = frc_ref[...]
@@ -72,6 +74,8 @@
         for k, (src, dst) in enumerate(pairs):
             rim_copy(k, src, dst, False, me - 1).wait_send()
             rim_copy(k, src, dst, True, me - 1).wait_recv()
+
+    fbuf[...] = 0.05 * fbuf[...]
 
     def make_step(lo, hi):
         span = hi - lo
@@ -92,7 +96,7 @@
                         c
                         + dif * (next_row + prev_row + next_col + prev_col - 4.0 * c)
                         - 0.05 * (u * (next_row - prev_row) + v * (next_col - prev_col))
-                        + 0.05 * fbuf[comp, lo:hi]
+                        + fbuf[comp, lo:hi]
                     )
                     new.append(jnp.where(keep, value, 0.0))
                 buf[2 * slot, lo:hi] = new[0]
@@ -266,16 +270,20 @@
     comps = n_state // 2
     blocks = own // 8
     c1 = send.shape[1]
-    for comp in range(comps):
-        s0 = jnp.where(anchor, 0.0, cd_ref[comp])
-        comp_scale = cd_ref[comps + comp] * s0
-        for rb in range(blocks):
-            for cb in range(cols // 128):
-                p = (comp * blocks + rb) * (cols // 128) + cb
-                rs, cs = slice(rb * 8, rb * 8 + 8), slice(cb * 128, cb * 128 + 128)
-                send[p // c1, p % c1, 0] = comp_scale[rs, cs]
-    start_half(0)
-    fine_body(st_ref, dif_ref, frc_ref, keep_ref, cd_ref, send, shift_ref, buf, dbuf, fbuf, fsems)
+
+    def early():
+        for comp in range(comps):
+            s0 = jnp.where(anchor, 0.0, cd_ref[comp])
+            comp_scale = cd_ref[comps + comp] * s0
+            for rb in range(blocks):
+                for cb in range(cols // 128):
+                    p = (comp * blocks + rb) * (cols // 128) + cb
+                    rs, cs = slice(rb * 8, rb * 8 + 8), slice(cb * 128, cb * 128 + 128)
+                    send[p // c1, p % c1, 0] = comp_scale[rs, cs]
+        start_half(0)
+
+    fine_body(st_ref, dif_ref, frc_ref, keep_ref, cd_ref, send, shift_ref, buf, dbuf, fbuf, fsems,
+              early=early)
     start_half(1)
     wait_half(0)
     wait_half(1)

time: 60 us -> 59.7 us (level)
  no operation moved by 1% of the time
where the time goes in v15:
time: 59.7 us; the launch traced here: 59.5 us
  Pallas kernels  56.9 us (95%)
  other arithmetic  2.66 us (4%)
    pallas_call x1, Pallas kernels, per_device_body(): pl.pallas_call(whole_kernel, out_shape=(jax.ShapeDtypeStruct((slots * com...  56.9 us

profile of v15, /device:TPU:1, one launch (start us, length us, event | category | flops | bytes accessed | tf_op | source)
XLA Modules:
  0.0 59.5 jit_solution(17276239240837963887)
XLA Ops:
  0.0 0.6 %fusion.3.keep_ref = f32[64,1]{1,0:T(8,128)} fusion(s32[]{:T(128)S(6)} %sub.3), kind=kLoop, calls=%fused_computation.7 | loop fusion | flops 320 | bytes 260 | tf_op jit(solution)/shard_map/convert_element_type | solution.py:308
  0.6 0.0 copy-start
  0.6 56.9 %shard_map.46 = (f32[4,32,1024]{2,1,0:T(8,128)}, f32[8,8,8,128]{3,2,1,0:T(8,128)}) custom-call(f32[4,32,1024]{2,1,0:T(8,128)} %bitcast.11, f32[32,1024]{1,0:T(8,128)} %dif_ref.1, f32[2,32,1024]{2,1,0:T(8,128)} %frc_ref.1, f32[64,1]{1,0:T(8,128)} %fusion.3.keep_ref, f32[4,32,1024]{2,1,0:T(8,128)} %bitcast.10), custom_call_target="tpu_custom_call" | custom-call | tf_op jit(solution)/shard_map/pallas_call | solution.py:319
  57.5 0.0 copy-done
  57.5 1.2 %bitcast_add_fusion = (f32[1,2,32,1024]{3,2,1,0:T(8,128)S(1)}, f32[1,2,32,1024]{3,2,1,0:T(8,128)S(1)}) fusion(f32[4,32,1024]{2,1,0:T(8,128)} %get-tuple-element.8, f32[2,2,32,1024]{3,2,1,0:T(8,128)S(1)} %copy-done, f32[1,2,32,1024]{3,2,1,0:T(8,128)} %bitcast.12, pred[]{:T(512)S(6)} %and.17), kind=kLoop, calls=%fused_computation.1 | loop fusion | flops 327680 | bytes 1835009 | tf_op jit(solution)/shard_map/add | solution.py:356
  58.7 0.8 %pad_maximum_fusion = f32[2,2,32,1024]{3,2,1,0:T(8,128)} fusion(f32[1,2,32,1024]{3,2,1,0:T(8,128)S(1)} %get-tuple-element.9, f32[1,2,32,1024]{3,2,1,0:T(8,128)S(1)} %get-tuple-element.10), kind=kLoop, calls=%fused_computation | loop fusion | flops 131072 | bytes 1048576 | tf_op jit(solution)/shard_map/stack | solution.py:357
Async XLA Ops:
  0.6 56.9 %copy-start = (f32[2,2,32,1024]{3,2,1,0:T(8,128)S(1)}, f32[2,2,32,1024]{3,2,1,0:T(8,128)}, u32[]{:S(2)}) copy-start(f32[2,2,32,1024]{3,2,1,0:T(8,128)} %param.5) | copy-start | bytes 1572868

commit v16 on v14

--- a/solution.py
+++ b/solution.py
@@ -190,12 +190,32 @@
     exchange(2, xg, back2, nz, mz, across)
     group_in = back2[...].reshape(pa.shape[1:])
 
-    def spread_step(s, carry):
-        xs[s] = pa[s] * group_in + pb[s]
+    ssem, rsem = sems.at[6], sems.at[7]
+
+    def back_copy(d, at):
+        return pltpu.make_async_remote_copy(
+            src_ref=xs.at[d], dst_ref=back1.at[at], send_sem=ssem.at[d], recv_sem=rsem.at[at],
+            device_id=in_plane(d), device_id_type=mesh_id,
+        )
+
+    xs[mq] = pa[mq] * group_in + pb[mq]
+    back1[mq] = xs[mq]
+
+    def spread_step(k, carry):
+        d = lax.rem(mq + k, nq)
+        xs[d] = pa[d] * group_in + pb[d]
+        back_copy(d, mq).start()
         return carry
 
-    lax.fori_loop(0, nq, spread_step, 0)
-    exchange(3, xs, back1, nq, mq, in_plane)
+    lax.fori_loop(1, nq, spread_step, 0)
+
+    def spread_wait(k, carry):
+        d = lax.rem(mq + k, nq)
+        back_copy(d, mq).wait_send()
+        back_copy(d, d).wait_recv()
+        return carry
+
+    lax.fori_loop(1, nq, spread_wait, 0)
     out_ref[...] = back1[...]
 
 

time: 60 us -> 59.9 us (level)
  no operation moved by 1% of the time
where the time goes in v16:
time: 59.9 us; the launch traced here: 59.8 us
  Pallas kernels  57.1 us (95%)
  other arithmetic  2.66 us (4%)
    pallas_call x1, Pallas kernels, per_device_body(): pl.pallas_call(whole_kernel, out_shape=(jax.ShapeDtypeStruct((slots * com...  57.1 us

profile of v16, /device:TPU:1, one launch (start us, length us, event | category | flops | bytes accessed | tf_op | source)
XLA Modules:
  0.0 59.8 jit_solution(1004794971486158512)
XLA Ops:
  0.0 0.6 %fusion.3.keep_ref = f32[64,1]{1,0:T(8,128)} fusion(s32[]{:T(128)S(6)} %sub.3), kind=kLoop, calls=%fused_computation.7 | loop fusion | flops 320 | bytes 260 | tf_op jit(solution)/shard_map/convert_element_type | solution.py:320
  0.6 0.0 copy-start
  0.6 57.1 %shard_map.46 = (f32[4,32,1024]{2,1,0:T(8,128)}, f32[8,8,8,128]{3,2,1,0:T(8,128)}) custom-call(f32[4,32,1024]{2,1,0:T(8,128)} %bitcast.11, f32[32,1024]{1,0:T(8,128)} %dif_ref.1, f32[2,32,1024]{2,1,0:T(8,128)} %frc_ref.1, f32[64,1]{1,0:T(8,128)} %fusion.3.keep_ref, f32[4,32,1024]{2,1,0:T(8,128)} %bitcast.10), custom_call_target="tpu_custom_call" | custom-call | tf_op jit(solution)/shard_map/pallas_call | solution.py:331
  57.8 0.0 copy-done
  57.8 1.2 %bitcast_add_fusion = (f32[1,2,32,1024]{3,2,1,0:T(8,128)S(1)}, f32[1,2,32,1024]{3,2,1,0:T(8,128)S(1)}) fusion(f32[4,32,1024]{2,1,0:T(8,128)} %get-tuple-element.8, f32[2,2,32,1024]{3,2,1,0:T(8,128)S(1)} %copy-done, f32[1,2,32,1024]{3,2,1,0:T(8,128)} %bitcast.12, pred[]{:T(512)S(6)} %and.17), kind=kLoop, calls=%fused_computation.1 | loop fusion | flops 327680 | bytes 1835009 | tf_op jit(solution)/shard_map/add | solution.py:368
  59.0 0.8 %pad_maximum_fusion = f32[2,2,32,1024]{3,2,1,0:T(8,128)} fusion(f32[1,2,32,1024]{3,2,1,0:T(8,128)S(1)} %get-tuple-element.9, f32[1,2,32,1024]{3,2,1,0:T(8,128)S(1)} %get-tuple-element.10), kind=kLoop, calls=%fused_computation | loop fusion | flops 131072 | bytes 1048576 | tf_op jit(solution)/shard_map/stack | solution.py:369
Async XLA Ops:
  0.6 57.1 %copy-start = (f32[2,2,32,1024]{3,2,1,0:T(8,128)S(1)}, f32[2,2,32,1024]{3,2,1,0:T(8,128)}, u32[]{:S(2)}) copy-start(f32[2,2,32,1024]{3,2,1,0:T(8,128)} %param.5) | copy-start | bytes 1572868

commit v17 on v14

--- a/solution.py
+++ b/solution.py
@@ -45,6 +45,8 @@
         for k, (src, dst) in enumerate(pairs):
             rim_copy(k, src, dst, False, me - 1).start()
 
+    global_row = me * own - HALO + lax.broadcasted_iota(jnp.int32, keep_ref.shape, 0)
+    keep_ref[...] = jnp.where((global_row >= 0) & (global_row < n * own), 1.0, 0.0)
     buf[:, HALO:HALO + own] = st_ref[...]
     dbuf[HALO:HALO + own] = dif_ref[...]
     fbuf[:, HALO:HALO + own] = frc_ref[...]
@@ -78,7 +80,7 @@
 
         def one_step(counter, carry):
             dif = dbuf[lo:hi]
-            keep = keep_ref[lo:hi] > 0.5
+            keep = keep_ref[lo:hi, 0:1] > 0.5
             for slot in range(2):
                 u = buf[2 * slot, lo:hi]
                 v = buf[2 * slot + 1, lo:hi]
@@ -199,8 +201,8 @@
     out_ref[...] = back1[...]
 
 
-def whole_kernel(st_ref, dif_ref, frc_ref, keep_ref, cd_ref, shift_ref, x_ref,
-                 buf, dbuf, fbuf, fsems, send, recv1, pa, pb, gsend, recv2, xg, back2, xs, back1, xsems):
+def whole_kernel(st_ref, dif_ref, frc_ref, cd_ref, shift_ref, x_ref,
+                 buf, dbuf, fbuf, fsems, keep_ref, send, recv1, pa, pb, gsend, recv2, xg, back2, xs, back1, xsems):
     n = lax.axis_size("space")
     me = lax.axis_index("space")
     mz = lax.axis_index("tz")
@@ -290,14 +292,10 @@
 
 def per_device_body(coarse_points, coarse_decay, diffusion, forcing):
     slots, comps, row_count, col_count = coarse_points.shape
-    space_count = lax.axis_size("space")
-    me = lax.axis_index("space")
 
 
     state = coarse_points.reshape(slots * comps, row_count, col_count)
     ext_rows = row_count + 2 * HALO
-    global_row = me * row_count - HALO + lax.broadcasted_iota(jnp.int32, (ext_rows, 1), 0)
-    keep = ((global_row >= 0) & (global_row < space_count * row_count)).astype(jnp.float32)
 
     vmem = pl.BlockSpec(memory_space=pltpu.VMEM)
     tiles = slots * comps * row_count * col_count // (2 * 8 * 128)
@@ -314,13 +312,14 @@
             jax.ShapeDtypeStruct((slots * comps, row_count, col_count), jnp.float32),
             jax.ShapeDtypeStruct(x1, jnp.float32),
         ),
-        in_specs=[vmem] * 5,
+        in_specs=[vmem] * 4,
         out_specs=(vmem, vmem),
         scratch_shapes=[
             pltpu.VMEM((slots * comps, ext_rows, col_count), jnp.float32),
             pltpu.VMEM((ext_rows, col_count), jnp.float32),
             pltpu.VMEM((comps, ext_rows, col_count), jnp.float32),
             pltpu.SemaphoreType.DMA((12,)),
+            pltpu.VMEM((ext_rows, 128), jnp.float32),
             pltpu.VMEM(send_shape, jnp.float32),
             pltpu.VMEM(send_shape, jnp.float32),
             pltpu.VMEM(x1, jnp.float32),
@@ -334,7 +333,7 @@
             pltpu.SemaphoreType.DMA((12, max(q_count, z_count))),
         ],
         compiler_params=pltpu.CompilerParams(collective_id=0, has_side_effects=True),
-    )(state, diffusion, forcing, keep, coarse_decay.reshape(state.shape))
+    )(state, diffusion, forcing, coarse_decay.reshape(state.shape))
     scale = coarse_decay
     at_anchor = (lax.axis_index("tz") == 0) & (lax.axis_index("tq") == 0)
     scale0 = jnp.where(at_anchor, 0.0, coarse_decay[0])

time: 60 us -> 59.3 us (0.988)
  other arithmetic: 2.66 us -> 2.03 us
    convert_element_type x1 -> x0, other arithmetic: 0.62 us -> none  [per_device_body(): ((global_row >= 0) & (global_row < space_count * row_count)).astype(jnp.f...]
where the time goes in v17:
time: 59.3 us; the launch traced here: 59.2 us
  Pallas kernels  57.2 us (96%)
  other arithmetic  2.03 us (3%)
    pallas_call x1, Pallas kernels, per_device_body(): pl.pallas_call(whole_kernel, out_shape=(jax.ShapeDtypeStruct((slots * com...  57.2 us
    add x1, other arithmetic, per_device_body(): second = scale[1] * first + shift[1]  1.19 us

profile of v17, /device:TPU:1, one launch (start us, length us, event | category | flops | bytes accessed | tf_op | source)
XLA Modules:
  0.0 59.2 jit_solution(4659422130417462317)
XLA Ops:
  0.0 0.0 copy-start
  0.0 57.2 %shard_map.46 = (f32[4,32,1024]{2,1,0:T(8,128)}, f32[8,8,8,128]{3,2,1,0:T(8,128)}) custom-call(f32[4,32,1024]{2,1,0:T(8,128)} %bitcast.11, f32[32,1024]{1,0:T(8,128)} %dif_ref.1, f32[2,32,1024]{2,1,0:T(8,128)} %frc_ref.1, f32[4,32,1024]{2,1,0:T(8,128)} %bitcast.10), custom_call_target="tpu_custom_call" | custom-call | tf_op jit(solution)/shard_map/pallas_call | solution.py:309
  57.2 0.0 copy-done
  57.2 1.2 %bitcast_add_fusion = (f32[1,2,32,1024]{3,2,1,0:T(8,128)S(1)}, f32[1,2,32,1024]{3,2,1,0:T(8,128)S(1)}) fusion(f32[4,32,1024]{2,1,0:T(8,128)} %get-tuple-element.8, f32[2,2,32,1024]{3,2,1,0:T(8,128)S(1)} %copy-done, f32[1,2,32,1024]{3,2,1,0:T(8,128)} %bitcast.12, pred[]{:T(512)S(6)} %and.5), kind=kLoop, calls=%fused_computation.1 | loop fusion | flops 327680 | bytes 1835009 | tf_op jit(solution)/shard_map/add | solution.py:347
  58.4 0.8 %pad_maximum_fusion = f32[2,2,32,1024]{3,2,1,0:T(8,128)} fusion(f32[1,2,32,1024]{3,2,1,0:T(8,128)S(1)} %get-tuple-element.9, f32[1,2,32,1024]{3,2,1,0:T(8,128)S(1)} %get-tuple-element.10), kind=kLoop, calls=%fused_computation | loop fusion | flops 131072 | bytes 1048576 | tf_op jit(solution)/shard_map/stack | solution.py:348
Async XLA Ops:
  0.0 57.2 %copy-start = (f32[2,2,32,1024]{3,2,1,0:T(8,128)S(1)}, f32[2,2,32,1024]{3,2,1,0:T(8,128)}, u32[]{:S(2)}) copy-start(f32[2,2,32,1024]{3,2,1,0:T(8,128)} %param.5) | copy-start | bytes 1572868

commit v18 on v17

--- a/solution.py
+++ b/solution.py
@@ -198,7 +198,14 @@
 
     lax.fori_loop(0, nq, spread_step, 0)
     exchange(3, xs, back1, nq, mq, in_plane)
-    out_ref[...] = back1[...]
+    n_comp, own, cols = out_ref.shape
+    blocks = own // 8
+    c1 = back1.shape[1]
+    for comp in range(n_comp):
+        for rb in range(blocks):
+            for cb in range(cols // 128):
+                p = (comp * blocks + rb) * (cols // 128) + cb
+                out_ref[comp, rb * 8:rb * 8 + 8, cb * 128:cb * 128 + 128] = back1[p // c1, p % c1]
 
 
 def whole_kernel(st_ref, dif_ref, frc_ref, cd_ref, shift_ref, x_ref,
@@ -284,12 +291,6 @@
     exchange_body(send, x_ref, recv1, pa, pb, gsend, recv2, xg, back2, xs, back1, xsems, first=False)
 
 
-def from_tiles(tiles, shape):
-    rows, cols = shape[0] * shape[1], shape[2]
-    grid = tiles.reshape(rows // 8, cols // 128, 8, 128)
-    return grid.transpose(0, 2, 1, 3).reshape(shape)
-
-
 def per_device_body(coarse_points, coarse_decay, diffusion, forcing):
     slots, comps, row_count, col_count = coarse_points.shape
 
@@ -310,7 +311,7 @@
         whole_kernel,
         out_shape=(
             jax.ShapeDtypeStruct((slots * comps, row_count, col_count), jnp.float32),
-            jax.ShapeDtypeStruct(x1, jnp.float32),
+            jax.ShapeDtypeStruct((comps, row_count, col_count), jnp.float32),
         ),
         in_specs=[vmem] * 4,
         out_specs=(vmem, vmem),
@@ -340,8 +341,7 @@
     shifts = shifts.reshape(coarse_points.shape)
     shift0 = shifts[0]
     shift = shifts
-    back = back.reshape(tiles, 8, 128)
-    entering = from_tiles(back, (comps, row_count, col_count))
+    entering = back
 
     first = scale0 * entering + shift0
     second = scale[1] * first + shift[1]

time: 59.3 us -> 59.3 us (level)
    add x1 -> x0, other arithmetic: 1.19 us -> none  [per_device_body(): second = scale[1] * first + shift[1]]
    another operation x1 -> x2, other arithmetic: 0.84 us -> 2.03 us  [per_device_body(): return jnp.stack([first, second], axis=0)]
where the time goes in v18:
time: 59.3 us; the launch traced here: 59.2 us
  Pallas kernels  57.2 us (96%)
  other arithmetic  2.03 us (3%)
    pallas_call x1, Pallas kernels, per_device_body(): pl.pallas_call(whole_kernel, out_shape=(jax.ShapeDtypeStruct((slots * com...  57.2 us
    another operation x2, other arithmetic, per_device_body(): return jnp.stack([first, second], axis=0)  2.03 us

profile of v18, /device:TPU:1, one launch (start us, length us, event | category | flops | bytes accessed | tf_op | source)
XLA Modules:
  0.0 59.2 jit_solution(1117329638493018308)
XLA Ops:
  0.0 0.0 copy-start
  0.0 57.2 %shard_map.46 = (f32[4,32,1024]{2,1,0:T(8,128)}, f32[2,32,1024]{2,1,0:T(8,128)}) custom-call(f32[4,32,1024]{2,1,0:T(8,128)} %bitcast.18, f32[32,1024]{1,0:T(8,128)} %dif_ref.1, f32[2,32,1024]{2,1,0:T(8,128)} %frc_ref.1, f32[4,32,1024]{2,1,0:T(8,128)} %bitcast.16), custom_call_target="tpu_custom_call" | custom-call | tf_op jit(solution)/shard_map/pallas_call | solution.py:310
  57.2 0.0 copy-done
  57.2 1.2 %fusion.1 = (f32[1,2,32,1024]{3,2,1,0:T(8,128)S(1)}, f32[2,32,1024]{2,1,0:T(8,128)S(1)}) fusion(f32[4,32,1024]{2,1,0:T(8,128)} %get-tuple-element.8, f32[2,2,32,1024]{3,2,1,0:T(8,128)S(1)} %copy-done, f32[2,32,1024]{2,1,0:T(8,128)} %get-tuple-element.7, pred[]{:T(512)S(6)} %and.5), kind=kLoop, calls=%fused_computation.3 | loop fusion | flops 327680 | bytes 1835009 | tf_op jit(solution)/shard_map/stack | solution.py:348
  58.4 0.8 %pad_maximum_fusion = f32[2,2,32,1024]{3,2,1,0:T(8,128)} fusion(f32[1,2,32,1024]{3,2,1,0:T(8,128)S(1)} %get-tuple-element.9, f32[1,2,32,1024]{3,2,1,0:T(8,128)S(1)} %bitcast.17), kind=kLoop, calls=%fused_computation | loop fusion | flops 131072 | bytes 1048576 | tf_op jit(solution)/shard_map/stack | solution.py:348
Async XLA Ops:
  0.0 57.2 %copy-start = (f32[2,2,32,1024]{3,2,1,0:T(8,128)S(1)}, f32[2,2,32,1024]{3,2,1,0:T(8,128)}, u32[]{:S(2)}) copy-start(f32[2,2,32,1024]{3,2,1,0:T(8,128)} %param.5) | copy-start | bytes 1572868
